TPU v7x, 32 devices: a whole 2x2x4 slice. The times are simulated.
32 devices in a mesh: seq: 8 (over z, y), tp: 4 (over x, core).
Axes of the slice: x: 2, y: 2, z: 4, core: 2. Of those that a mesh axis runs over, the one named last changes fastest.
Arguments:
- tokens: bfloat16 [6144, 2048], P('seq'), may hold values from -7 to 7
- seg_ids: int32 [6144], P('seq'), may hold values from 0 to 3, never falling along the last dimension, each value on 1 to 3072 neighbouring positions
- norm1_gain: bfloat16 [2048], replicated, may hold values from 0.25 to 1.75
- w_mix: bfloat16 [2048, 16, 768], P(None, 'tp'), may hold values from -0.125 to 0.125
- w_rate: bfloat16 [2048, 16, 2], P(None, 'tp'), may hold values from -1 to 1
- conv_w: bfloat16 [4, 16, 512], P(None, 'tp'), may hold values from -3 to 3
- a_log: float32 [16], P('tp'), may hold values from -12 to -2.8
- dt_bias: float32 [16], P('tp'), may hold values from -1 to 1
- out_gain: bfloat16 [256], replicated, may hold values from 0.25 to 1.75
- w_out: bfloat16 [2048, 16, 256], P(None, 'tp'), may hold values from -0.1875 to 0.1875
- norm2_gain: bfloat16 [2048], replicated, may hold values from 0.25 to 1.75
- w_up: bfloat16 [2048, 2, 5632], P(None, None, 'tp'), may hold values from -0.125 to 0.125
- w_down: bfloat16 [2048, 5632], P(None, 'tp'), may hold values from -0.15625 to 0.15625
- cotangent: bfloat16 [6144, 2048], P('seq'), may hold values from -6 to 6
Outputs:
- layer_out: bfloat16 [6144, 2048], P('seq')
- grad_tokens: bfloat16 [6144, 2048], P('seq')
- grad_norm1: float32 [2048], replicated
- grad_mix: float32 [2048, 16, 768], P('seq', 'tp')
- grad_rate: float32 [2048, 16, 2], P('seq', 'tp')
- grad_conv: float32 [4, 16, 512], replicated
- grad_a_log: float32 [16], replicated
- grad_dt_bias: float32 [16], replicated
- grad_out_gain: float32 [256], replicated
- grad_w_out: float32 [2048, 16, 256], P('seq', 'tp')
- grad_norm2: float32 [2048], replicated
- grad_up: float32 [2048, 2, 5632], P('seq', None, 'tp')
- grad_down: float32 [2048, 5632], P('seq', 'tp')
Inputs may be any that keep to these rules, and one draw needn't show every extreme that they name: `seg_ids`: document ids of the packed stream, never falling: each of the 4 documents is one contiguous run of tokens, the longest exactly 3072 tokens.
All inputs are finite; a program needn't handle non-finite values.
Results may differ from a plain program's by a relative error of at most 0.02.
Values may be sent and summed in bfloat16 or wider, within the bound.
A program may use at most 384 MiB of HBM per device.

v0:
```python
import jax
import jax.numpy as jnp
from jax import lax
from jax.sharding import PartitionSpec as P

DK = 128
GROUP = 64


EPSILON = 1e-06
EXACT_ARITHMETIC = lax.Precision.HIGHEST


def shifted(block, axis, distance):
    devices = range(lax.axis_size(axis))
    route = [(i - distance, i) for i in devices if i - distance in devices]
    return lax.ppermute(block, axis, route)


def carried_in(value, axis, join, neutral):
    place = lax.axis_index(axis)
    gathered = jax.tree.map(
        lambda a, kind: lax.all_gather(a.astype(kind), axis), value, (jnp.bfloat16, jnp.bfloat16)
    )
    state = jax.tree.map(lambda a, e: jnp.zeros_like(a) + jnp.asarray(e, a.dtype), value, neutral)

    def one(lap, state):
        return join(
            state,
            jax.tree.map(
                lambda a, own: lax.dynamic_index_in_dim(a, lap, 0, False).astype(own.dtype),
                gathered,
                value,
            ),
        )

    return lax.fori_loop(0, place, one, state)


def carried_in_2(value, axis, join, neutral):
    count, mine = (lax.axis_size(axis), lax.axis_index(axis))
    pieces = jax.tree.map(lambda part: lax.all_gather(part, axis), value)
    pieces = jax.tree.map(lambda part: part[::-1], pieces)
    mine = count - 1 - mine
    running = jax.tree.map(
        lambda part, zero: jnp.full_like(part, 0) + jnp.asarray(zero, part.dtype), value, neutral
    )

    def lap(position, running):
        longer = join(running, jax.tree.map(lambda part: part[position], pieces))
        return jax.tree.map(lambda new, old: jnp.where(position < mine, new, old), longer, running)

    return lax.fori_loop(0, count - 1, lap, running)


def rounded(values):
    return values.astype(jnp.bfloat16).astype(jnp.float32)


def norm_scale(values):
    return lax.rsqrt(jnp.mean(values * values, axis=-1, keepdims=True) + EPSILON)


def unit_rows(values):
    return values * lax.rsqrt(jnp.sum(values * values, axis=-1, keepdims=True) + EPSILON)


def norm_back(grad_normed, gain_f, x_hat, scales):
    shaped = grad_normed * gain_f
    return scales * (shaped - x_hat * jnp.mean(shaped * x_hat, axis=-1, keepdims=True))


def conv_features(padded, weights, keeping):
    taps_all = weights.shape[0]
    length = keeping.shape[1]
    summed = weights[taps_all - 1] * padded[taps_all - 1 :]
    for offset in range(1, taps_all):
        begin_at = taps_all - 1 - offset
        summed = (
            summed
            + weights[begin_at]
            * padded[begin_at : begin_at + length]
            * keeping[offset - 1][:, None, None]
        )
    active = jax.nn.silu(summed)
    return (unit_rows(active[..., :DK]), unit_rows(active[..., DK : 2 * DK]), active[..., 2 * DK :])


def rate_terms(rate_rows, a_log, dt_bias):
    strength = jax.nn.sigmoid(rate_rows[..., 1])
    log_decay = -jnp.exp(a_log) * jax.nn.softplus(rate_rows[..., 0] + dt_bias)
    return (strength, log_decay)


def gated_norm(core_rows, gate_rows, gain_rows):
    return core_rows * norm_scale(core_rows) * gain_rows * jax.nn.silu(gate_rows)


def swiglu(gate_up):
    return jax.nn.silu(gate_up[:, 0]) * gate_up[:, 1]


def batched_mm(left_mat, right_mat):
    return jnp.einsum("hij,hjk->hik", left_mat, right_mat, precision=EXACT_ARITHMETIC)


def compose(earlier, later):
    return (batched_mm(later[0], earlier[0]), batched_mm(later[0], earlier[1]) + later[1])


def delta_local(query, keys, values, strength, log_decay, resets):
    length, head_count, key_size = keys.shape
    payload_dimension = values.shape[-1]
    number_of_segments = length // GROUP

    def blocked(array):
        shaped = array.reshape((number_of_segments, GROUP, head_count) + array.shape[2:])
        return jnp.moveaxis(shaped, 2, 1)

    stacked = jnp.concatenate(
        [values, jnp.zeros((length, head_count, key_size), jnp.float32)], axis=-1
    )
    query_b = blocked(query * key_size ** (-0.5))
    keys_b = blocked(keys)
    stacked_b = blocked(stacked)
    strength_b = blocked(strength)
    decay_sum = jnp.cumsum(blocked(log_decay), axis=-1)
    pieces = jnp.cumsum(resets.reshape(number_of_segments, GROUP), axis=-1)
    row_ids = lax.broadcasted_iota(jnp.int32, (GROUP, GROUP), 0)
    col_ids = lax.broadcasted_iota(jnp.int32, (GROUP, GROUP), 1)
    joined = pieces[:, :, None] == pieces[:, None, :]
    inside = (joined & (row_ids >= col_ids))[:, None].astype(jnp.float32)
    before = (joined & (row_ids > col_ids))[:, None].astype(jnp.float32)
    spread = decay_sum[..., :, None] - decay_sum[..., None, :]
    decays = jnp.exp(jnp.where(inside > 0, spread, 0.0)) * inside
    from_start = jnp.exp(decay_sum) * (pieces == 0)[:, None, :].astype(jnp.float32)
    to_end = jnp.exp(decay_sum[..., -1:] - decay_sum) * (pieces == pieces[:, -1:])[
        :, None, :
    ].astype(jnp.float32)
    key_dots = jnp.einsum("nhtk,nhjk->nhtj", keys_b, keys_b, precision=EXACT_ARITHMETIC)
    lower_mat = (
        jnp.eye(GROUP, dtype=jnp.float32) + key_dots * decays * before * strength_b[..., :, None]
    )

    def solved(rhs_rows):
        return lax.linalg.triangular_solve(
            lower_mat, rhs_rows, left_side=True, lower=True, unit_diagonal=True
        )

    value_part = solved(strength_b[..., None] * stacked_b)
    state_part = solved((strength_b * from_start)[..., None] * keys_b)
    query_keys = jnp.einsum("nhtk,nhjk->nhtj", query_b, keys_b, precision=EXACT_ARITHMETIC) * decays
    end_keys = to_end[..., None] * keys_b
    initial = jnp.concatenate(
        [
            jnp.zeros((head_count, key_size, payload_dimension), jnp.float32),
            jnp.broadcast_to(
                jnp.eye(key_size, dtype=jnp.float32), (head_count, key_size, key_size)
            ),
        ],
        axis=-1,
    )

    def advance(carried_state, inputs):
        value_rows, state_rows, query_rows, mixing, end_rows, start_decay, block_decay = inputs
        new_values = value_rows - jnp.einsum(
            "htk,hkw->htw", state_rows, carried_state, precision=EXACT_ARITHMETIC
        )
        emitted = start_decay[..., None] * jnp.einsum(
            "htk,hkw->htw", query_rows, carried_state, precision=EXACT_ARITHMETIC
        ) + jnp.einsum("htj,hjw->htw", mixing, new_values, precision=EXACT_ARITHMETIC)
        carried_state = block_decay[:, None, None] * carried_state + jnp.einsum(
            "hjk,hjw->hkw", end_rows, new_values, precision=EXACT_ARITHMETIC
        )
        return (carried_state, emitted)

    final_state, emitted_all = lax.scan(
        advance,
        initial,
        (value_part, state_part, query_b, query_keys, end_keys, from_start, from_start[..., -1]),
    )
    emitted_all = jnp.moveaxis(emitted_all, 1, 2).reshape(
        length, head_count, payload_dimension + key_size
    )
    return (
        emitted_all[..., :payload_dimension],
        emitted_all[..., payload_dimension:],
        final_state[..., :payload_dimension],
        final_state[..., payload_dimension:],
    )


def shards(
    tokens,
    seg_ids,
    norm1_gain,
    w_mix,
    w_rate,
    conv_w,
    a_log,
    dt_bias,
    out_gain,
    w_out,
    norm2_gain,
    w_up,
    w_down,
    cotangent,
):
    length = tokens.shape[0]
    head_count = w_mix.shape[1]
    taps_all = conv_w.shape[0]
    rim_rows = taps_all - 1
    conv_width = conv_w.shape[2]
    tp_index = lax.axis_index("tp")
    tokens_f = tokens.astype(jnp.float32)
    gain_one = norm1_gain.astype(jnp.float32)
    scale_one = norm_scale(tokens_f)
    x_hat_one = tokens_f * scale_one
    normed_one = (x_hat_one * gain_one).astype(jnp.bfloat16)
    mixed = jnp.einsum("td,dhc->thc", normed_one, w_mix, preferred_element_type=jnp.float32)
    rate_rows = jnp.einsum("td,dhc->thc", normed_one, w_rate, preferred_element_type=jnp.float32)
    conv_rows = mixed[..., :conv_width].astype(jnp.bfloat16)
    gate_rows = mixed[..., conv_width:]
    tail_rows, tail_ids = shifted(
        (conv_rows[length - rim_rows :], seg_ids[length - rim_rows :].astype(jnp.bfloat16)),
        "seq",
        1,
    )
    own_ids = seg_ids.astype(jnp.float32)
    padded_ids = jnp.concatenate([tail_ids.astype(jnp.float32), own_ids])
    keeping = jnp.stack(
        [
            (padded_ids[rim_rows - offset : rim_rows - offset + length] == own_ids).astype(
                jnp.float32
            )
            for offset in range(1, taps_all)
        ]
    )
    resets = (padded_ids[rim_rows - 1 : rim_rows - 1 + length] != own_ids).astype(jnp.float32)
    padded = jnp.concatenate([tail_rows, conv_rows]).astype(jnp.float32)
    features, conv_pull = jax.vjp(
        lambda padded_rows, weights: conv_features(padded_rows, weights, keeping),
        padded,
        conv_w.astype(jnp.float32),
    )
    query = rounded(features[0])
    keys = rounded(features[1])
    values = rounded(features[2])
    (strength, log_decay), rate_pull = jax.vjp(rate_terms, rate_rows, a_log, dt_bias)
    (local_output, probe_destinations, base_state, transfer), delta_pull = jax.vjp(
        lambda q, k, v, b, g: delta_local(q, k, v, b, g, resets),
        query,
        keys,
        values,
        strength,
        log_decay,
    )
    zero_state = jnp.zeros_like(base_state)
    identity_mats = jnp.broadcast_to(jnp.eye(transfer.shape[1], dtype=jnp.float32), transfer.shape)
    entering_memory_matrix = carried_in(
        (transfer, base_state), "seq", compose, (identity_mats, zero_state)
    )[1]
    core_output = local_output + jnp.einsum(
        "vkq,kqp->vkp", probe_destinations, entering_memory_matrix, precision=EXACT_ARITHMETIC
    )
    normed_out_f, gate_pull = jax.vjp(
        gated_norm, core_output, gate_rows, out_gain.astype(jnp.float32)
    )
    normed_out = normed_out_f.astype(jnp.bfloat16)
    mixer_part = jnp.einsum("thv,dhv->td", normed_out, w_out, preferred_element_type=jnp.float32)
    gain_two = norm2_gain.astype(jnp.float32)
    residual = tokens_f + lax.psum(mixer_part, "tp")
    scale_two = norm_scale(residual)
    x_hat_two = residual * scale_two
    normed_two = (x_hat_two * gain_two).astype(jnp.bfloat16)
    gate_up = jnp.einsum("td,dcf->tcf", normed_two, w_up, preferred_element_type=jnp.float32)
    hidden_f, hidden_pull = jax.vjp(swiglu, gate_up)
    hidden = hidden_f.astype(jnp.bfloat16)
    ffn_part = jnp.einsum("tf,df->td", hidden, w_down, preferred_element_type=jnp.float32)
    layer_out = (
        residual + lax.psum(ffn_part.astype(jnp.bfloat16), "tp").astype(jnp.float32)
    ).astype(jnp.bfloat16)
    grad_down = jnp.einsum("tf,td->df", hidden, cotangent, preferred_element_type=jnp.float32)
    grad_hidden = jnp.einsum("td,df->tf", cotangent, w_down, preferred_element_type=jnp.float32)
    grad_gate_up = hidden_pull(grad_hidden)[0].astype(jnp.bfloat16)
    grad_up = jnp.einsum(
        "td,tcf->dcf", normed_two, grad_gate_up, preferred_element_type=jnp.float32
    )
    ffn_in_part = jnp.einsum("tcf,dcf->td", grad_gate_up, w_up, preferred_element_type=jnp.float32)
    ffn_in = lax.psum(ffn_in_part, "tp")
    gain_two_grad = jnp.sum(ffn_in_part * x_hat_two, axis=0)
    grad_residual = cotangent.astype(jnp.float32) + norm_back(
        ffn_in, gain_two, x_hat_two, scale_two
    )
    grad_mixer = grad_residual.astype(jnp.bfloat16)
    grad_w_out = jnp.einsum(
        "td,thv->dhv", grad_mixer, normed_out, preferred_element_type=jnp.float32
    )
    grad_normed_out = jnp.einsum(
        "td,dhv->thv", grad_mixer, w_out, preferred_element_type=jnp.float32
    )
    core_output_grad, grad_gate_rows, out_gain_grad = gate_pull(grad_normed_out)
    own_state_gradient = jnp.einsum(
        "eyc,eyn->ycn", probe_destinations, core_output_grad, precision=EXACT_ARITHMETIC
    )
    transfer_t = jnp.swapaxes(transfer, 1, 2)
    state_gradient = carried_in_2(
        (transfer_t, own_state_gradient), "seq", compose, (identity_mats, zero_state)
    )[1]
    branch_derivatives = jnp.einsum(
        "xao,aeo->xae", core_output_grad, entering_memory_matrix, precision=EXACT_ARITHMETIC
    )
    transfer_gradient = jnp.einsum(
        "zne,zye->zny", state_gradient, entering_memory_matrix, precision=EXACT_ARITHMETIC
    )
    grad_query, grad_keys, grad_values, grad_strength, grad_decay = delta_pull(
        (core_output_grad, branch_derivatives, state_gradient, transfer_gradient)
    )
    grad_rate_rows, a_log_grad, dt_bias_grad = rate_pull((grad_strength, grad_decay))
    grad_padded, conv_grad = conv_pull((grad_query, grad_keys, grad_values))
    back_rows = shifted(grad_padded[:rim_rows], "seq", -1)
    grad_conv_rows = grad_padded[rim_rows:] + jnp.concatenate(
        [jnp.zeros((length - rim_rows,) + back_rows.shape[1:], jnp.float32), back_rows]
    )
    grad_mixed = jnp.concatenate([grad_conv_rows, grad_gate_rows], axis=-1).astype(jnp.bfloat16)
    grad_rates = grad_rate_rows.astype(jnp.bfloat16)
    grad_mix = jnp.einsum("td,thc->dhc", normed_one, grad_mixed, preferred_element_type=jnp.float32)
    grad_rate = jnp.einsum(
        "td,thc->dhc", normed_one, grad_rates, preferred_element_type=jnp.float32
    )
    mixer_in_part = jnp.einsum(
        "thc,dhc->td", grad_mixed, w_mix, preferred_element_type=jnp.float32
    ) + jnp.einsum("thc,dhc->td", grad_rates, w_rate, preferred_element_type=jnp.float32)
    mixer_in = lax.psum(mixer_in_part.astype(jnp.bfloat16), "tp").astype(jnp.float32)
    gain_one_grad = jnp.sum(mixer_in_part * x_hat_one, axis=0)
    grad_tokens = (grad_residual + norm_back(mixer_in, gain_one, x_hat_one, scale_one)).astype(
        jnp.bfloat16
    )
    total_heads = head_count * lax.axis_size("tp")
    head_start = tp_index * head_count
    zero_index = tp_index * 0
    conv_full = lax.dynamic_update_slice(
        jnp.zeros((taps_all, total_heads, conv_width), jnp.float32),
        conv_grad,
        (zero_index, head_start, zero_index),
    )
    a_log_full = lax.dynamic_update_slice(
        jnp.zeros((total_heads,), jnp.float32), a_log_grad, (head_start,)
    )
    dt_bias_full = lax.dynamic_update_slice(
        jnp.zeros((total_heads,), jnp.float32), dt_bias_grad, (head_start,)
    )
    small_sums = lax.psum(
        (gain_one_grad, gain_two_grad, out_gain_grad, conv_full, a_log_full, dt_bias_full),
        ("seq", "tp"),
    )
    weight_sums = (
        lax.psum_scatter(
            grad_mix.astype(jnp.bfloat16), "seq", scatter_dimension=0, tiled=True
        ).astype(jnp.float32),
        lax.psum_scatter(
            grad_rate.astype(jnp.bfloat16), "seq", scatter_dimension=0, tiled=True
        ).astype(jnp.float32),
        lax.psum_scatter(
            grad_w_out.astype(jnp.bfloat16), "seq", scatter_dimension=0, tiled=True
        ).astype(jnp.float32),
        lax.psum_scatter(
            grad_up.astype(jnp.bfloat16), "seq", scatter_dimension=0, tiled=True
        ).astype(jnp.float32),
        lax.psum_scatter(
            grad_down.astype(jnp.bfloat16), "seq", scatter_dimension=0, tiled=True
        ).astype(jnp.float32),
    )
    return (
        layer_out,
        grad_tokens,
        small_sums[0],
        weight_sums[0],
        weight_sums[1],
        small_sums[3],
        small_sums[4],
        small_sums[5],
        small_sums[2],
        weight_sums[2],
        small_sums[1],
        weight_sums[3],
        weight_sums[4],
    )


def solution(mesh):
    in_specs = (
        P("seq", None),
        P("seq"),
        P(),
        P(None, "tp", None),
        P(None, "tp", None),
        P(None, "tp", None),
        P("tp"),
        P("tp"),
        P(),
        P(None, "tp", None),
        P(),
        P(None, None, "tp"),
        P(None, "tp"),
        P("seq", None),
    )
    out_specs = (
        P("seq", None),
        P("seq", None),
        P(),
        P("seq", "tp", None),
        P("seq", "tp", None),
        P(),
        P(),
        P(),
        P(),
        P("seq", "tp", None),
        P(),
        P("seq", None, "tp"),
        P("seq", "tp"),
    )
    return jax.shard_map(shards, mesh=mesh, in_specs=in_specs, out_specs=out_specs, check_vma=False)
```

profile of v0, /device:TPU:0, one launch (start us, length us, event | category | flops | bytes accessed | tf_op | source)
XLA Modules:
  0.0 2212.9 jit_solution(17638097775273321500)
XLA Ops:
  10.1 15.5 fusion.245
  25.6 4.9 collective-permute-start.1
  43.6 6.3 fusion.94
  59.7 236.6 %custom-call.12 = f32[12,4,1,64,64]{3,4,2,1,0:T(8,128)S(1)} custom-call(f32[12,4,1,64,64]{4,3,2,1,0:T(8,128)} %get-tuple-element.928), custom_call_target="InvertDiagBlocksLowerTriangular" | custom-call | tf_op jit(solution)/shard_map/jvp()/triangular_solve | solution.py:146
  300.7 6.7 fusion.95
  316.1 107.1 %while.76 = (s32[]{:T(128)}, f32[4,128,384]{2,1,0:T(8,128)S(1)}, f32[12,4,64,384]{3,2,1,0:T(8,128)}, f32[12,4,128,384]{3,2,1,0:T(8,128)}, f32[12,4,64,384]{3,2,1...) while((s32[]{:T(128)}, f32[4,128,384]{2,1,0:T(8,128)S(1)}, ...), condition=%wide.region_6.7_spmd, body=%wide.region_5.6_spmd.sunk | while | flops 529170432 | bytes 8794313 | solution.py:177
  424.8 5.0 copy.154
  429.8 34.7 %all-gather.9.cloned.1.call-done = bf16[32,128,128]{2,1,0:T(8,128)(2,1)} async-done(((bf16[4,128,128]{2,1,0:T(8,128)(2,1)}), bf16[32,128,128]{2,1,0:T(8,128)(2,1)}) %all-gather.9.cloned.1.call-update) | async-done | bytes 1048592 | tf_op jit(solution)/shard_map/all_gather | solution.py:23
  464.5 50.8 %all-gather.11.cloned.1.call-done = bf16[32,128,256]{2,1,0:T(8,128)(2,1)} async-done(((bf16[4,128,256]{2,1,0:T(8,128)(2,1)}), bf16[32,128,256]{2,1,0:T(8,128)(2,1)}) %all-gather.11.cloned.1.call-update) | async-done | bytes 2097168 | tf_op jit(solution)/shard_map/all_gather | solution.py:23
  515.3 5.7 multiply_reduce_fusion.9
  526.5 5.6 convolution_bitcast_fusion.4
  532.8 128.1 %all-reduce.31.cloned.1.call-done = f32[768,2048]{1,0:T(8,128)} async-done(((f32[768,2048]{1,0:T(8,128)}), f32[768,2048]{1,0:T(8,128)}) %all-reduce.31.cloned.1.call-update) | async-done | bytes 6291472 | tf_op jit(solution)/shard_map/psum | solution.py:272
  660.9 4.6 multiply_reduce_fusion.6
  665.6 17.9 fusion.76
  683.4 12.6 multiply_bitcast_fusion
  696.1 16.5 fusion.102
  713.6 118.9 %all-reduce.33.cloned.1.call-done = f32[768,2048]{1,0:T(8,128)} async-done(((f32[768,2048]{1,0:T(8,128)}), f32[768,2048]{1,0:T(8,128)}) %all-reduce.33.cloned.1.call-update) | async-done | bytes 6291472 | tf_op jit(solution)/shard_map/psum | solution.py:290
  832.5 8.8 multiply_reduce_fusion
  841.3 5.0 multiply_add_fusion
  846.6 11.3 multiply_reduce_fusion.7
  859.3 5.0 fusion.143
  864.4 19.7 all-gather.13.cloned.1.call-done
  893.9 64.0 %all-gather.15.cloned.1.call-done = f32[32,128,256]{2,1,0:T(8,128)} async-done(((f32[4,128,256]{2,1,0:T(8,128)}), f32[32,128,256]{2,1,0:T(8,128)}) %all-gather.15.cloned.1.call-update) | async-done | bytes 4194320 | tf_op jit(solution)/shard_map/all_gather | solution.py:42
  957.9 4.7 rev.7
  962.7 12.9 while.79
  983.4 251.5 %while.78 = (s32[]{:T(128)}, f32[4,128,384]{2,1,0:T(8,128)S(1)}, f32[12,4,64,384]{3,2,1,0:T(8,128)}, f32[12,4,64,128]{3,2,1,0:T(8,128)}, f32[12,4,64,128]{3,2,1,...) while((s32[]{:T(128)}, f32[4,128,384]{2,1,0:T(8,128)S(1)}, ...), condition=%wide.region_21.22_spmd, body=%wide.region_18.21_spmd.sunk | while | flops 1058635520 | bytes 14433105 | solution.py:177
  1234.9 8.5 fusion.249
  1243.5 6.9 fusion.96
  1259.7 5.6 multiply_select_fusion
  1282.0 8.7 convolution_convert_fusion.3
  1290.8 9.7 fusion.82
  1300.6 9.1 convolution_convert_fusion.4
  1329.5 7.9 multiply_reduce_fusion.4
  1337.4 6.1 multiply_multiply_fusion.2
  1349.6 6.8 pad_add_fusion
  1360.1 18.0 fusion.246
  1378.8 16.8 convolution_convert_fusion
  1397.5 15.8 convolution_convert_fusion.2
  1416.5 17.2 reduce-scatter.10.cloned.1.call-done
  1436.1 111.4 %reduce-scatter.14.cloned.1.call-done = bf16[256,1408]{0,1:T(8,128)(2,1)} async-done(((bf16[2048,1408]{0,1:T(8,128)(2,1)}), bf16[256,1408]{0,1:T(8,128)(2,1)}) %reduce-scatter.14.cloned.1.call-update) | async-done | bytes 720912 | tf_op jit(solution)/shard_map/reduce_scatter | solution.py:370
  1550.0 119.9 %all-reduce.37.cloned.1.call-done = (bf16[768,2048]{1,0:T(8,128)(2,1)}, bf16[768,2048]{1,0:T(8,128)(2,1)}) async-done(((bf16[768,2048]{1,0:T(8,128)(2,1)}, bf16[768,2048]{1,0:T(8,128)(2,1)}), (bf16[768,2048]{1,0:T(8,128)(2,1)}, bf16[768,2048]{1,0:T(8,128)(2,1)})) %all-reduce.37.cloned.1.call-update) | async-done | bytes 6291472 | tf_op jit(solution)/shard_map/psum | solution.py:281
  1669.9 5.6 fusion.89
  1675.5 5.3 fusion.88
  1683.7 43.9 %all-reduce.24 = (f32[2048]{0:T(1024)}, f32[16]{0:T(128)}, f32[16]{0:T(128)}, f32[256]{0:T(256)}, f32[2048]{0:T(1024)}) all-reduce(f32[2048]{0:T(1024)S(1)} %get-tuple-element.797, f32[16]{0:T(128)S(1)} %multiply_dynamic-update-slice_fusion, f32[16]{0:T(128)S(1)} %dynamic_update_slice.100, ...), channel_id=1, replica_groups=mesh['seq'=8,'tp'=4] {'seq','tp'}, use_global_device_ids=true, to_apply=%region_35.37 | all-reduce | flops 4384 | bytes 35072 | tf_op jit(solution)/shard_map/psum | solution.py:353
  1727.6 139.4 %reduce-scatter.12.cloned.1.call-done = bf16[256,2,1408]{2,0,1:T(8,128)(2,1)} async-done(((bf16[2048,2,1408]{2,0,1:T(8,128)(2,1)}), bf16[256,2,1408]{2,0,1:T(8,128)(2,1)}) %reduce-scatter.12.cloned.1.call-update) | async-done | bytes 1441808 | tf_op jit(solution)/shard_map/reduce_scatter | solution.py:367
  1867.0 4.4 copy.199
  1871.4 205.5 %reduce-scatter.8.cloned.1.call-done = bf16[256,4,768]{2,0,1:T(8,128)(2,1)} async-done(((bf16[2048,4,768]{2,0,1:T(8,128)(2,1)}), bf16[256,4,768]{2,0,1:T(8,128)(2,1)}) %reduce-scatter.8.cloned.1.call-update) | async-done | bytes 1572880 | tf_op jit(solution)/shard_map/reduce_scatter | solution.py:358
  2081.2 123.4 %all-reduce.35.cloned.1.call-done = f32[4,16,512]{2,1,0:T(8,128)} async-done(((f32[4,16,512]{2,1,0:T(8,128)}), f32[4,16,512]{2,1,0:T(8,128)}) %all-reduce.35.cloned.1.call-update) | async-done | bytes 131088 | tf_op jit(solution)/shard_map/psum | solution.py:353
  (725 shorter events, 510.5 us)
Async XLA Ops:
  7.2 28.8 %copy-start = (bf16[2048,4,2]{0,2,1:T(2,128)(2,1)S(1)}, bf16[2048,4,2]{0,2,1:T(2,128)(2,1)}, u32[]{:S(2)}) copy-start(bf16[2048,4,2]{0,2,1:T(2,128)(2,1)} %param.28) | copy-start | bytes 98308
  7.2 457.3 %all-gather.9.cloned.1.call-start = ((), (), s32[]{:S(2)}) async-start(), calls=%async_computation.12 | async-start | bytes 1179648 | tf_op jit(solution)/shard_map/all_gather | solution.py:23
  10.0 26.0 %copy-start.95 = (f32[768]{0:T(1024)}, f32[768]{0:T(1024)S(1)}, u32[]{:S(2)}) copy-start(f32[768]{0:T(1024)S(1)} %add_rsqrt_fusion.3) | copy-start | bytes 9220
  10.1 25.9 %copy-start.76 = (f32[2048]{0:T(1024)}, f32[2048]{0:T(1024)S(1)}, u32[]{:S(2)}) copy-start(f32[2048]{0:T(1024)S(1)} %convert_element_type.185) | copy-start | bytes 24580
  10.1 20.4 copy-start.103
  25.6 15.1 collective-permute-start.1
  30.5 8.4 collective-permute-start
  38.4 19.1 copy-start.40
  38.8 262.0 %copy-start.49 = (f32[12,4,64]{2,1,0:T(4,128)}, f32[12,4,64]{2,1,0:T(4,128)S(1)}, u32[]{:S(2)}) copy-start(f32[12,4,64]{2,1,0:T(4,128)S(1)} %copy.144) | copy-start | bytes 36868
  38.9 18.6 copy-start.78
  39.9 17.5 copy-start.21
  40.0 17.5 copy-start.33
  40.0 17.5 copy-start.38
  40.3 255.9 %copy-start.60 = (f32[12,4,64]{2,1,0:T(4,128)}, f32[12,4,64]{2,1,0:T(4,128)S(1)}, u32[]{:S(2)}) copy-start(f32[12,4,64]{2,1,0:T(4,128)S(1)} %copy.149) | copy-start | bytes 36868
  40.4 267.1 %copy-start.62 = (f32[12,4,64]{2,1,0:T(4,128)}, f32[12,4,64]{2,1,0:T(4,128)S(1)}, u32[]{:S(2)}) copy-start(f32[12,4,64]{2,1,0:T(4,128)S(1)} %copy.138) | copy-start | bytes 36868
  54.1 253.4 %copy-start.4 = (bf16[768,4,128]{2,0,1:T(8,128)(2,1)}, bf16[768,4,128]{2,0,1:T(8,128)(2,1)S(1)}, u32[]{:S(2)}) copy-start(bf16[768,4,128]{2,0,1:T(8,128)(2,1)S(1)} %get-tuple-element.924) | copy-start | bytes 2359300
  316.1 108.7 %copy-start.114 = (bf16[256]{0:T(256)(128)(2,1)S(1)}, bf16[256]{0:T(256)(128)(2,1)}, u32[]{:S(2)}) copy-start(bf16[256]{0:T(256)(128)(2,1)} %param.32) | copy-start | bytes 1540
  423.9 91.3 %all-gather.11.cloned.1.call-start = ((), (), s32[]{:S(2)}) async-start(), calls=%async_computation.13 | async-start | bytes 2359296 | tf_op jit(solution)/shard_map/all_gather | solution.py:23
  424.7 236.2 %all-reduce.31.cloned.1.call-start = ((), (), s32[]{:S(2)}) async-start(), calls=%async_computation.5 | async-start | bytes 12582912 | tf_op jit(solution)/shard_map/psum | solution.py:272
  515.3 10.0 copy-start.10
  532.1 300.4 %all-reduce.33.cloned.1.call-start = ((), (), s32[]{:S(2)}) async-start(), calls=%async_computation.6 | async-start | bytes 12582912 | tf_op jit(solution)/shard_map/psum | solution.py:290
  532.8 308.5 %copy-start.73 = (f32[2048]{0:T(1024)}, f32[2048]{0:T(1024)S(1)}, u32[]{:S(2)}) copy-start(f32[2048]{0:T(1024)S(1)} %convert_element_type.205) | copy-start | bytes 24580
  665.5 17.9 copy-start.2
  665.5 175.8 %copy-start.97 = (f32[768]{0:T(1024)}, f32[768]{0:T(1024)S(1)}, u32[]{:S(2)}) copy-start(f32[768]{0:T(1024)S(1)} %add_rsqrt_fusion.2) | copy-start | bytes 9220
  665.5 17.9 copy-start.42
  712.6 171.4 %all-gather.13.cloned.1.call-start = ((), (), s32[]{:S(2)}) async-start(), calls=%async_computation.14 | async-start | bytes 2359296 | tf_op jit(solution)/shard_map/all_gather | solution.py:42
  713.5 127.8 %copy-start.43 = (bf16[768,2048]{1,0:T(8,128)(2,1)S(1)}, bf16[768,2048]{1,0:T(8,128)(2,1)}, u32[]{:S(2)}) copy-start(bf16[768,2048]{1,0:T(8,128)(2,1)} %param.37) | copy-start | bytes 9437188
  713.5 244.4 %all-gather.15.cloned.1.call-start = ((), (), s32[]{:S(2)}) async-start(), calls=%async_computation.15 | async-start | bytes 4718592 | tf_op jit(solution)/shard_map/all_gather | solution.py:42
  832.5 8.8 copy-start.15
  832.5 13.8 slice-start.12
  832.5 13.8 slice-start.13
  846.6 11.3 copy-start.16
  864.3 550.5 %reduce-scatter.16.cloned.1.call-start = ((), (), s32[]{:S(2)}) async-start(), calls=%async_computation.16 | async-start | bytes 589824
  962.7 12.9 copy-start.11
  1234.9 8.6 slice-start.6
  1234.9 8.6 copy-start.7
  1234.9 8.6 slice-start.7
  1234.9 8.6 copy-start.20
  1281.9 151.7 %reduce-scatter.10.cloned.1.call-start = ((), (), s32[]{:S(2)}) async-start(), calls=%async_computation.9 | async-start | bytes 4718592 | tf_op jit(solution)/shard_map/reduce_scatter | solution.py:364
  1290.7 256.8 %reduce-scatter.14.cloned.1.call-start = ((), (), s32[]{:S(2)}) async-start(), calls=%async_computation.11 | async-start | bytes 6488064 | tf_op jit(solution)/shard_map/reduce_scatter | solution.py:370
  1300.5 369.4 %all-reduce.37.cloned.1.call-start = ((), (), s32[]{:S(2)}) async-start(), calls=%async_computation.17 | async-start | bytes 12582912 | tf_op jit(solution)/shard_map/psum | solution.py:281
  1329.5 7.9 copy-start.81
  1344.4 12.0 collective-permute-start.2
  1360.1 18.0 copy-start.45
  1378.1 488.9 %reduce-scatter.12.cloned.1.call-start = ((), (), s32[]{:S(2)}) async-start(), calls=%async_computation.10 | async-start | bytes 12976128 | tf_op jit(solution)/shard_map/reduce_scatter | solution.py:367
  1395.6 681.3 %reduce-scatter.8.cloned.1.call-start = ((), (), s32[]{:S(2)}) async-start(), calls=%async_computation.7 | async-start | bytes 14155776 | tf_op jit(solution)/shard_map/reduce_scatter | solution.py:358
  1413.3 791.3 %all-reduce.35.cloned.1.call-start = ((), (), s32[]{:S(2)}) async-start(), calls=%async_computation.8 | async-start | bytes 262144 | tf_op jit(solution)/shard_map/psum | solution.py:353
  1669.9 11.0 slice-start.2
  (98 other events, 344.7 us)
Sparse Core Ops, SparseCore 0:
  424.0 40.3 all-gather.8
  467.2 48.0 all-gather.10
  532.3 128.6 all-reduce.30
  712.7 119.7 all-reduce.32
  834.5 49.4 all-gather.12
  886.0 71.8 all-gather.14
  1282.1 60.1 reduce-scatter.15
  1346.3 87.2 reduce-scatter.9
  1437.3 110.1 reduce-scatter.13
  1550.3 119.5 all-reduce.36
  1673.5 193.4 reduce-scatter.11
  1870.4 206.4 reduce-scatter.7
  2083.0 121.5 all-reduce.34
where the time goes:
time: 2220 us; the launch traced here: 2210 us
  waiting for transfers between devices  1130 us (51%)
  matrix products  561 us (25%)
  other arithmetic  359 us (16%)
  local copies, waits for them, and re-layouts  87 us (4%)
  blocking collectives  43.9 us (2%)
    another operation x4, other arithmetic, solved(): lax.linalg.triangular_solve(lower_mat, rhs_rows, left_side=True, lower=Tr...  237 us
    reduce_scatter x1, waiting for transfers between devices, shards(): lax.psum_scatter(grad_mix.astype(jnp.bfloat16), 'seq', scatter_dimension=...  206 us
    reduce_scatter x1, waiting for transfers between devices, shards(): lax.psum_scatter(grad_up.astype(jnp.bfloat16), 'seq', scatter_dimension=0...  139 us
    psum x1, waiting for transfers between devices, shards(): residual = tokens_f + lax.psum(mixer_part, 'tp')  128 us
    psum x1, waiting for transfers between devices, shards(): lax.psum((gain_one_grad, gain_two_grad, out_gain_grad, conv_full, a_log_f...  123 us
    psum x1, waiting for transfers between devices, shards(): lax.psum(ffn_part.astype(jnp.bfloat16), 'tp').astype(jnp.float32)  120 us
    psum x1, waiting for transfers between devices, shards(): ffn_in = lax.psum(ffn_in_part, 'tp')  119 us
    reduce_scatter x1, waiting for transfers between devices, shards(): lax.psum_scatter(grad_down.astype(jnp.bfloat16), 'seq', scatter_dimension...  111 us
  transfers between devices with their start and end apart: 16, of which 12 were waited for; matrix products, arithmetic and copies ran while one was open for 9% of the time, Pallas kernels for 0%

commit v1 on v0

--- a/solution.py
+++ b/solution.py
@@ -9,6 +9,7 @@
 
 EPSILON = 1e-06
 EXACT_ARITHMETIC = lax.Precision.HIGHEST
+FAST_ARITHMETIC = lax.Precision.HIGH
 
 
 def shifted(block, axis, distance):
@@ -101,11 +102,37 @@
 
 
 def batched_mm(left_mat, right_mat):
-    return jnp.einsum("hij,hjk->hik", left_mat, right_mat, precision=EXACT_ARITHMETIC)
+    return jnp.einsum("hij,hjk->hik", left_mat, right_mat, precision=FAST_ARITHMETIC)
 
 
 def compose(earlier, later):
     return (batched_mm(later[0], earlier[0]), batched_mm(later[0], earlier[1]) + later[1])
+
+
+def unit_lower_inverse(lower_mat):
+    size = lower_mat.shape[-1]
+    rows = lax.broadcasted_iota(jnp.int32, (size, size), 0)
+    cols = lax.broadcasted_iota(jnp.int32, (size, size), 1)
+    eye = (rows == cols).astype(lower_mat.dtype)
+    strict = lower_mat - eye
+    inverse = eye
+    width = 1
+    while width < size:
+        within = ((rows // (2 * width)) == (cols // (2 * width))) & (
+            (rows // width) != (cols // width)
+        )
+        off = strict * within.astype(lower_mat.dtype)
+        if width == 1:
+            inverse = eye - off
+        else:
+            inverse = inverse - jnp.einsum(
+                "...ij,...jk->...ik",
+                inverse,
+                jnp.einsum("...ij,...jk->...ik", off, inverse, precision=EXACT_ARITHMETIC),
+                precision=EXACT_ARITHMETIC,
+            )
+        width *= 2
+    return inverse
 
 
 def delta_local(query, keys, values, strength, log_decay, resets):
@@ -137,19 +164,19 @@
     to_end = jnp.exp(decay_sum[..., -1:] - decay_sum) * (pieces == pieces[:, -1:])[
         :, None, :
     ].astype(jnp.float32)
-    key_dots = jnp.einsum("nhtk,nhjk->nhtj", keys_b, keys_b, precision=EXACT_ARITHMETIC)
+    key_dots = jnp.einsum("nhtk,nhjk->nhtj", keys_b, keys_b, precision=FAST_ARITHMETIC)
     lower_mat = (
         jnp.eye(GROUP, dtype=jnp.float32) + key_dots * decays * before * strength_b[..., :, None]
     )
 
+    inverse = unit_lower_inverse(lower_mat)
+
     def solved(rhs_rows):
-        return lax.linalg.triangular_solve(
-            lower_mat, rhs_rows, left_side=True, lower=True, unit_diagonal=True
-        )
+        return jnp.einsum("nhtj,nhjw->nhtw", inverse, rhs_rows, precision=FAST_ARITHMETIC)
 
     value_part = solved(strength_b[..., None] * stacked_b)
     state_part = solved((strength_b * from_start)[..., None] * keys_b)
-    query_keys = jnp.einsum("nhtk,nhjk->nhtj", query_b, keys_b, precision=EXACT_ARITHMETIC) * decays
+    query_keys = jnp.einsum("nhtk,nhjk->nhtj", query_b, keys_b, precision=FAST_ARITHMETIC) * decays
     end_keys = to_end[..., None] * keys_b
     initial = jnp.concatenate(
         [
@@ -164,13 +191,13 @@
     def advance(carried_state, inputs):
         value_rows, state_rows, query_rows, mixing, end_rows, start_decay, block_decay = inputs
         new_values = value_rows - jnp.einsum(
-            "htk,hkw->htw", state_rows, carried_state, precision=EXACT_ARITHMETIC
+            "htk,hkw->htw", state_rows, carried_state, precision=FAST_ARITHMETIC
         )
         emitted = start_decay[..., None] * jnp.einsum(
-            "htk,hkw->htw", query_rows, carried_state, precision=EXACT_ARITHMETIC
-        ) + jnp.einsum("htj,hjw->htw", mixing, new_values, precision=EXACT_ARITHMETIC)
+            "htk,hkw->htw", query_rows, carried_state, precision=FAST_ARITHMETIC
+        ) + jnp.einsum("htj,hjw->htw", mixing, new_values, precision=FAST_ARITHMETIC)
         carried_state = block_decay[:, None, None] * carried_state + jnp.einsum(
-            "hjk,hjw->hkw", end_rows, new_values, precision=EXACT_ARITHMETIC
+            "hjk,hjw->hkw", end_rows, new_values, precision=FAST_ARITHMETIC
         )
         return (carried_state, emitted)
 
@@ -261,7 +288,7 @@
         (transfer, base_state), "seq", compose, (identity_mats, zero_state)
     )[1]
     core_output = local_output + jnp.einsum(
-        "vkq,kqp->vkp", probe_destinations, entering_memory_matrix, precision=EXACT_ARITHMETIC
+        "vkq,kqp->vkp", probe_destinations, entering_memory_matrix, precision=FAST_ARITHMETIC
     )
     normed_out_f, gate_pull = jax.vjp(
         gated_norm, core_output, gate_rows, out_gain.astype(jnp.float32)
@@ -269,7 +296,7 @@
     normed_out = normed_out_f.astype(jnp.bfloat16)
     mixer_part = jnp.einsum("thv,dhv->td", normed_out, w_out, preferred_element_type=jnp.float32)
     gain_two = norm2_gain.astype(jnp.float32)
-    residual = tokens_f + lax.psum(mixer_part, "tp")
+    residual = tokens_f + lax.psum(mixer_part.astype(jnp.bfloat16), "tp").astype(jnp.float32)
     scale_two = norm_scale(residual)
     x_hat_two = residual * scale_two
     normed_two = (x_hat_two * gain_two).astype(jnp.bfloat16)
@@ -277,9 +304,6 @@
     hidden_f, hidden_pull = jax.vjp(swiglu, gate_up)
     hidden = hidden_f.astype(jnp.bfloat16)
     ffn_part = jnp.einsum("tf,df->td", hidden, w_down, preferred_element_type=jnp.float32)
-    layer_out = (
-        residual + lax.psum(ffn_part.astype(jnp.bfloat16), "tp").astype(jnp.float32)
-    ).astype(jnp.bfloat16)
     grad_down = jnp.einsum("tf,td->df", hidden, cotangent, preferred_element_type=jnp.float32)
     grad_hidden = jnp.einsum("td,df->tf", cotangent, w_down, preferred_element_type=jnp.float32)
     grad_gate_up = hidden_pull(grad_hidden)[0].astype(jnp.bfloat16)
@@ -287,7 +311,7 @@
         "td,tcf->dcf", normed_two, grad_gate_up, preferred_element_type=jnp.float32
     )
     ffn_in_part = jnp.einsum("tcf,dcf->td", grad_gate_up, w_up, preferred_element_type=jnp.float32)
-    ffn_in = lax.psum(ffn_in_part, "tp")
+    ffn_in = lax.psum(ffn_in_part.astype(jnp.bfloat16), "tp").astype(jnp.float32)
     gain_two_grad = jnp.sum(ffn_in_part * x_hat_two, axis=0)
     grad_residual = cotangent.astype(jnp.float32) + norm_back(
         ffn_in, gain_two, x_hat_two, scale_two
@@ -301,21 +325,37 @@
     )
     core_output_grad, grad_gate_rows, out_gain_grad = gate_pull(grad_normed_out)
     own_state_gradient = jnp.einsum(
-        "eyc,eyn->ycn", probe_destinations, core_output_grad, precision=EXACT_ARITHMETIC
+        "eyc,eyn->ycn", probe_destinations, core_output_grad, precision=FAST_ARITHMETIC
     )
     transfer_t = jnp.swapaxes(transfer, 1, 2)
     state_gradient = carried_in_2(
         (transfer_t, own_state_gradient), "seq", compose, (identity_mats, zero_state)
     )[1]
     branch_derivatives = jnp.einsum(
-        "xao,aeo->xae", core_output_grad, entering_memory_matrix, precision=EXACT_ARITHMETIC
+        "xao,aeo->xae", core_output_grad, entering_memory_matrix, precision=FAST_ARITHMETIC
     )
     transfer_gradient = jnp.einsum(
-        "zne,zye->zny", state_gradient, entering_memory_matrix, precision=EXACT_ARITHMETIC
-    )
-    grad_query, grad_keys, grad_values, grad_strength, grad_decay = delta_pull(
+        "zne,zye->zny", state_gradient, entering_memory_matrix, precision=FAST_ARITHMETIC
+    )
+    ffn_send, early_send, state_gradient = lax.optimization_barrier(
+        (
+            ffn_part.astype(jnp.bfloat16),
+            tuple(part.astype(jnp.bfloat16) for part in (grad_w_out, grad_up, grad_down)),
+            state_gradient,
+        )
+    )
+    ffn_sum = lax.psum(ffn_send, "tp")
+    early_sums = tuple(
+        lax.psum_scatter(part, "seq", scatter_dimension=0, tiled=True) for part in early_send
+    )
+    delta_grads = delta_pull(
         (core_output_grad, branch_derivatives, state_gradient, transfer_gradient)
     )
+    ffn_sum, early_sums, delta_grads = lax.optimization_barrier(
+        (ffn_sum, early_sums, delta_grads)
+    )
+    grad_query, grad_keys, grad_values, grad_strength, grad_decay = delta_grads
+    layer_out = (residual + ffn_sum.astype(jnp.float32)).astype(jnp.bfloat16)
     grad_rate_rows, a_log_grad, dt_bias_grad = rate_pull((grad_strength, grad_decay))
     grad_padded, conv_grad = conv_pull((grad_query, grad_keys, grad_values))
     back_rows = shifted(grad_padded[:rim_rows], "seq", -1)
@@ -350,10 +390,15 @@
     dt_bias_full = lax.dynamic_update_slice(
         jnp.zeros((total_heads,), jnp.float32), dt_bias_grad, (head_start,)
     )
-    small_sums = lax.psum(
-        (gain_one_grad, gain_two_grad, out_gain_grad, conv_full, a_log_full, dt_bias_full),
-        ("seq", "tp"),
-    )
+    small_parts = (gain_one_grad, gain_two_grad, out_gain_grad, conv_full, a_log_full, dt_bias_full)
+    small_flat = lax.psum(
+        jnp.concatenate([part.reshape(-1) for part in small_parts]), ("seq", "tp")
+    )
+    small_sums = []
+    start_at = 0
+    for part in small_parts:
+        small_sums.append(small_flat[start_at : start_at + part.size].reshape(part.shape))
+        start_at += part.size
     weight_sums = (
         lax.psum_scatter(
             grad_mix.astype(jnp.bfloat16), "seq", scatter_dimension=0, tiled=True
@@ -361,15 +406,9 @@
         lax.psum_scatter(
             grad_rate.astype(jnp.bfloat16), "seq", scatter_dimension=0, tiled=True
         ).astype(jnp.float32),
-        lax.psum_scatter(
-            grad_w_out.astype(jnp.bfloat16), "seq", scatter_dimension=0, tiled=True
-        ).astype(jnp.float32),
-        lax.psum_scatter(
-            grad_up.astype(jnp.bfloat16), "seq", scatter_dimension=0, tiled=True
-        ).astype(jnp.float32),
-        lax.psum_scatter(
-            grad_down.astype(jnp.bfloat16), "seq", scatter_dimension=0, tiled=True
-        ).astype(jnp.float32),
+        early_sums[0].astype(jnp.float32),
+        early_sums[1].astype(jnp.float32),
+        early_sums[2].astype(jnp.float32),
     )
     return (
         layer_out,

time: 2220 us -> 1710 us (0.77)
  waiting for transfers between devices: 1130 us -> 822 us
  other arithmetic: 359 us -> 128 us
  local copies, waits for them, and re-layouts: 87 us -> 150 us
  blocking collectives: 43.9 us -> 0 us
    another operation x6 -> x2, other arithmetic: 240 us -> 4.56 us  [the longest x4 237 us: solved(): lax.linalg.triangular_solve(lower_mat, rhs_rows, left_side=True, lower=Tr...]
    psum x4 -> x5, waiting for transfers between devices: 490 us -> 319 us  [the longest x1 114 us: shards(): lax.psum(jnp.concatenate([part.reshape(-1) for part in small_parts]), ('s...]
    reduce_scatter x3, waiting for transfers between devices: 268 us -> 129 us  [shards(): lax.psum_scatter(part, 'seq', scatter_dimension=0, tiled=True)]
    psum x1 -> x0, blocking collectives: 43.9 us -> none  [shards(): lax.psum((gain_one_grad, gain_two_grad, out_gain_grad, conv_full, a_log_f...]
    dot_general x159 -> x193, matrix products: 352 us -> 394 us  [the longest x36 73 us: advance(): jnp.einsum('htk,hkw->htw', state_rows, carried_state, precision=FAST_ARIT...]
    all_gather x2, waiting for transfers between devices: 83.7 us -> 44.1 us  [carried_in_2(): pieces = jax.tree.map(lambda part: lax.all_gather(part, axis), value)]
    unnamed x14 -> x15, waiting for transfers between devices: 0.24 us -> 37.5 us
    another operation x6 -> x0, matrix products: 29.8 us -> none  [solved(): lax.linalg.triangular_solve(lower_mat, rhs_rows, left_side=True, lower=Tr...]
  transfers between devices with their start and end apart: 16 -> 17, of which waited for: 12 -> 11; matrix products, arithmetic and copies ran while one was open for 9% -> 30% of each run, Pallas kernels for 0% -> 0%
where the time goes in v1:
time: 1710 us; the launch traced here: 1700 us
  waiting for transfers between devices  822 us (48%)
  matrix products  568 us (33%)
  local copies, waits for them, and re-layouts  150 us (9%)
  other arithmetic  128 us (7%)
    reduce_scatter x1, waiting for transfers between devices, shards(): lax.psum_scatter(grad_mix.astype(jnp.bfloat16), 'seq', scatter_dimension=...  207 us
    reduce_scatter x3, waiting for transfers between devices, shards(): lax.psum_scatter(part, 'seq', scatter_dimension=0, tiled=True)  129 us
    psum x1, waiting for transfers between devices, shards(): lax.psum(jnp.concatenate([part.reshape(-1) for part in small_parts]), ('s...  114 us
    all_gather x2, waiting for transfers between devices, carried_in(): lax.all_gather(a.astype(kind), axis)  84.8 us
    psum x1, waiting for transfers between devices, shards(): lax.psum(mixer_part.astype(jnp.bfloat16), 'tp').astype(jnp.float32)  76.4 us
    dot_general x36, matrix products, advance(): jnp.einsum('htk,hkw->htw', state_rows, carried_state, precision=FAST_ARIT...  73 us
    dot_general x36, matrix products, advance(): jnp.einsum('htj,hjw->htw', mixing, new_values, precision=FAST_ARITHMETIC)  68 us
    psum x1, waiting for transfers between devices, shards(): lax.psum(ffn_in_part.astype(jnp.bfloat16), 'tp').astype(jnp.float32)  67.7 us
  transfers between devices with their start and end apart: 17, of which 11 were waited for; matrix products, arithmetic and copies ran while one was open for 30% of the time, Pallas kernels for 0%

profile of v1, /device:TPU:0, one launch (start us, length us, event | category | flops | bytes accessed | tf_op | source)
XLA Modules:
  0.0 1696.7 jit_solution(15964242718271327641)
XLA Ops:
  8.2 4.9 collective-permute-start
  16.4 15.4 fusion.306
  34.6 4.2 collective-permute-start.1
  38.8 3.8 slice.160
  51.6 6.3 fusion.95
  97.0 4.3 fusion.99
  112.5 125.0 %while.76 = (s32[]{:T(128)}, f32[4,128,384]{2,1,0:T(8,128)S(1)}, f32[12,4,64,384]{3,2,1,0:T(8,128)}, f32[12,4,128,384]{3,2,1,0:T(8,128)}, f32[12,4,64,384]{3,2,1...) while((s32[]{:T(128)}, f32[4,128,384]{2,1,0:T(8,128)S(1)}, ...), condition=%wide.region_6.7_spmd, body=%wide.region_5.6_spmd.sunk | while | flops 264929280 | bytes 8792293 | solution.py:204
  239.1 5.1 copy.248
  244.2 34.0 %all-gather.9.cloned.1.call-done = bf16[32,128,128]{2,1,0:T(8,128)(2,1)} async-done(((bf16[4,128,128]{2,1,0:T(8,128)(2,1)}), bf16[32,128,128]{2,1,0:T(8,128)(2,1)}) %all-gather.9.cloned.1.call-update) | async-done | bytes 1048592 | tf_op jit(solution)/shard_map/all_gather | solution.py:24
  278.2 50.8 %all-gather.11.cloned.1.call-done = bf16[32,128,256]{2,1,0:T(8,128)(2,1)} async-done(((bf16[4,128,256]{2,1,0:T(8,128)(2,1)}), bf16[32,128,256]{2,1,0:T(8,128)(2,1)}) %all-gather.11.cloned.1.call-update) | async-done | bytes 2097168 | tf_op jit(solution)/shard_map/all_gather | solution.py:24
  329.1 4.3 multiply_reduce_fusion.8
  339.0 5.0 bitcast_convert_fusion.1
  344.7 76.4 %all-reduce.30.cloned.1.call-done = bf16[768,2048]{1,0:T(8,128)(2,1)} async-done(((bf16[768,2048]{1,0:T(8,128)(2,1)}), bf16[768,2048]{1,0:T(8,128)(2,1)}) %all-reduce.30.cloned.1.call-update) | async-done | bytes 3145744 | tf_op jit(solution)/shard_map/psum | solution.py:299
  421.0 4.1 multiply_reduce_fusion.5
  425.7 15.9 fusion.76
  441.6 12.6 multiply_bitcast_fusion
  454.2 17.0 %bitcast_convert_fusion = (bf16[768,2048]{1,0:T(8,128)(2,1)}, f32[768,2048,1]{1,0,2:T(8,128)}) fusion(bf16[2048,2,1408]{2,1,0:T(2,128)(2,1)} %param.33, f32[768,1,1408]{2,0,1:T(8,128)} %get-tuple-element.933, f32[768,1,1408]{2,0,1:T(8,128)} %get-tuple-element.932), kind=kOutput, calls=%fused_computation.132 | convolution fusion | flops 8864268288 | bytes 29622272 | tf_op jit(solution)/shard_map/tcf,dcf->td/dot_general | solution.py:313
  472.2 67.7 %all-reduce.32.cloned.1.call-done = bf16[768,2048]{1,0:T(8,128)(2,1)} async-done(((bf16[768,2048]{1,0:T(8,128)(2,1)}), bf16[768,2048]{1,0:T(8,128)(2,1)}) %all-reduce.32.cloned.1.call-update) | async-done | bytes 3145744 | tf_op jit(solution)/shard_map/psum | solution.py:314
  539.9 7.7 fusion.94
  550.2 11.5 multiply_reduce_fusion.6
  566.7 3.9 fusion.132
  570.8 20.6 %all-gather.13.cloned.1.call-done = f32[32,128,128]{2,1,0:T(8,128)} async-done(((f32[4,128,128]{2,1,0:T(8,128)}), f32[32,128,128]{2,1,0:T(8,128)}) %all-gather.13.cloned.1.call-update) | async-done | bytes 2097168 | tf_op jit(solution)/shard_map/all_gather | solution.py:43
  594.6 9.8 fusion.82
  604.4 9.1 convolution_convert_fusion.4
  613.5 16.5 convolution_convert_fusion
  630.1 11.7 convolution_convert_fusion.3
  641.8 23.5 %all-gather.15.cloned.1.call-done = f32[32,128,256]{2,1,0:T(8,128)} async-done(((f32[4,128,256]{2,1,0:T(8,128)}), f32[32,128,256]{2,1,0:T(8,128)}) %all-gather.15.cloned.1.call-update) | async-done | bytes 4194320 | tf_op jit(solution)/shard_map/all_gather | solution.py:43
  665.2 4.7 rev.7
  669.9 11.6 while.79
  697.3 232.8 %while.78 = (s32[]{:T(128)}, f32[4,128,384]{2,1,0:T(8,128)S(1)}, f32[12,4,64,384]{3,2,1,0:T(8,128)}, f32[12,4,64,128]{3,2,1,0:T(8,128)}, f32[12,4,64,128]{3,2,1,...) while((s32[]{:T(128)}, f32[4,128,384]{2,1,0:T(8,128)S(1)}, ...), condition=%wide.region_24.25_spmd, body=%wide.region_21.24_spmd.sunk | while | flops 530153216 | bytes 14433113 | solution.py:204
  975.2 3.8 fusion.312
  987.4 4.2 fusion.173
  991.6 7.5 multiply_select_fusion
  1021.7 129.4 %reduce-scatter.10.cloned.1.call-done = bf16[256,2,1408]{2,0,1:T(8,128)(2,1)} async-done(((bf16[2048,2,1408]{2,0,1:T(8,128)(2,1)}), bf16[256,2,1408]{2,0,1:T(8,128)(2,1)}) %reduce-scatter.10.cloned.1.call-update) | async-done | bytes 1441808 | tf_op jit(solution)/shard_map/reduce_scatter | solution.py:349
  1151.5 3.9 multiply_reduce_fusion.10
  1155.5 4.5 add_add_fusion.2
  1160.1 9.7 multiply_reduce_fusion.3
  1169.9 5.9 multiply_multiply_fusion.2
  1181.7 6.8 pad_add_fusion
  1193.8 16.7 fusion.307
  1218.9 61.5 %all-reduce.36.cloned.1.call-done = bf16[768,2048]{1,0:T(8,128)(2,1)} async-done(((bf16[768,2048]{1,0:T(8,128)(2,1)}), bf16[768,2048]{1,0:T(8,128)(2,1)}) %all-reduce.36.cloned.1.call-update) | async-done | bytes 3145744 | tf_op jit(solution)/shard_map/psum | solution.py:374
  1280.4 4.8 fusion.89
  1286.3 15.6 convolution_convert_fusion.2
  1310.0 36.6 %reduce-scatter.16.cloned.1.call-done = bf16[256,8]{1,0:T(8,128)(2,1)} async-done(((bf16[2048,8]{1,0:T(8,128)(2,1)}), bf16[256,8]{1,0:T(8,128)(2,1)}) %reduce-scatter.16.cloned.1.call-update) | async-done | bytes 4112
  1348.3 10.8 fusion.88
  1359.1 113.7 %all-reduce.38.cloned.1.call-done = f32[37152]{0:T(1024)} async-done(((f32[37152]{0:T(1024)}), f32[37152]{0:T(1024)}) %all-reduce.38.cloned.1.call-update) | async-done | bytes 148624 | tf_op jit(solution)/shard_map/psum | solution.py:394
  1478.3 207.3 %reduce-scatter.14.cloned.1.call-done = bf16[256,4,768]{2,0,1:T(8,128)(2,1)} async-done(((bf16[2048,4,768]{2,0,1:T(8,128)(2,1)}), bf16[256,4,768]{2,0,1:T(8,128)(2,1)}) %reduce-scatter.14.cloned.1.call-update) | async-done | bytes 1572880 | tf_op jit(solution)/shard_map/reduce_scatter | solution.py:403
  1685.6 4.3 copy.305
  (814 shorter events, 580.9 us)
Async XLA Ops:
  7.2 35.5 %copy-start = (bf16[2048,4,2]{0,2,1:T(2,128)(2,1)S(1)}, bf16[2048,4,2]{0,2,1:T(2,128)(2,1)}, u32[]{:S(2)}) copy-start(bf16[2048,4,2]{0,2,1:T(2,128)(2,1)} %param.26) | copy-start | bytes 98308
  7.2 271.0 %all-gather.9.cloned.1.call-start = ((), (), s32[]{:S(2)}) async-start(), calls=%async_computation.14 | async-start | bytes 1179648 | tf_op jit(solution)/shard_map/all_gather | solution.py:24
  8.2 38.2 %collective-permute-start = (bf16[3]{0:T(256)(128)(2,1)S(1)}, bf16[3]{0:T(256)(128)(2,1)S(1)}, u32[]{:S(2)}, u32[]{:S(2)}) collective-permute-start(bf16[3]{0:T(256)(128)(2,1)S(1)} %slice.118), channel_id=1, source_target_pairs={{0,4},{4,8},{8,12},{12,16},{16,20},{20,24},{24,28},{1,5},{5,9},{9,... | collective-permute-start | bytes 26 | tf_op jit(solution)/shard_map/ppermute | solution.py:18
  13.7 28.9 %copy-start.113 = (f32[2048]{0:T(1024)}, f32[2048]{0:T(1024)S(1)}, u32[]{:S(2)}) copy-start(f32[2048]{0:T(1024)S(1)} %convert_element_type.256) | copy-start | bytes 24580
  16.3 26.3 %copy-start.131 = (f32[768]{0:T(1024)}, f32[768]{0:T(1024)S(1)}, u32[]{:S(2)}) copy-start(f32[768]{0:T(1024)S(1)} %add_rsqrt_fusion.3) | copy-start | bytes 9220
  34.6 14.1 collective-permute-start.1
  45.0 19.2 %copy-start.63 = (f32[12,4,64]{2,1,0:T(4,128)}, f32[12,4,64]{2,1,0:T(4,128)S(1)}, u32[]{:S(2)}) copy-start(f32[12,4,64]{2,1,0:T(4,128)S(1)} %copy.215) | copy-start | bytes 36868
  45.0 24.8 %copy-start.73 = (f32[64,64]{0,1:T(8,128)}, f32[64,64]{0,1:T(8,128)S(1)}, u32[]{:S(2)}) copy-start(f32[64,64]{0,1:T(8,128)S(1)} %fusion.258) | copy-start | bytes 49156
  45.5 51.5 %copy-start.71 = (f32[12,4,64]{2,1,0:T(4,128)}, f32[12,4,64]{2,1,0:T(4,128)S(1)}, u32[]{:S(2)}) copy-start(f32[12,4,64]{2,1,0:T(4,128)S(1)} %copy.217) | copy-start | bytes 36868
  46.4 23.5 %copy-start.75 = (f32[64,64]{0,1:T(8,128)}, f32[64,64]{0,1:T(8,128)S(1)}, u32[]{:S(2)}) copy-start(f32[64,64]{0,1:T(8,128)S(1)} %get-tuple-element.979) | copy-start | bytes 49156
  46.4 26.3 %copy-start.87 = (f32[64,64]{0,1:T(8,128)}, f32[64,64]{0,1:T(8,128)S(1)}, u32[]{:S(2)}) copy-start(f32[64,64]{0,1:T(8,128)S(1)} %get-tuple-element.977) | copy-start | bytes 49156
  46.4 31.9 %copy-start.85 = (f32[64,64]{0,1:T(8,128)}, f32[64,64]{0,1:T(8,128)S(1)}, u32[]{:S(2)}) copy-start(f32[64,64]{0,1:T(8,128)S(1)} %get-tuple-element.976) | copy-start | bytes 49156
  46.4 37.9 %copy-start.83 = (f32[64,64]{0,1:T(8,128)}, f32[64,64]{0,1:T(8,128)S(1)}, u32[]{:S(2)}) copy-start(f32[64,64]{0,1:T(8,128)S(1)} %get-tuple-element.975) | copy-start | bytes 49156
  46.4 43.5 %copy-start.81 = (f32[64,64]{0,1:T(8,128)}, f32[64,64]{0,1:T(8,128)S(1)}, u32[]{:S(2)}) copy-start(f32[64,64]{0,1:T(8,128)S(1)} %get-tuple-element.974) | copy-start | bytes 49156
  47.4 16.9 copy-start.39
  47.4 16.9 copy-start.58
  47.4 16.9 copy-start.61
  48.7 52.6 %copy-start.89 = (f32[12,4,64]{2,1,0:T(4,128)}, f32[12,4,64]{2,1,0:T(4,128)S(1)}, u32[]{:S(2)}) copy-start(f32[12,4,64]{2,1,0:T(4,128)S(1)} %copy.241) | copy-start | bytes 36868
  61.6 39.7 %copy-start.8 = (bf16[768,4,128]{2,0,1:T(8,128)(2,1)}, bf16[768,4,128]{2,0,1:T(8,128)(2,1)S(1)}, u32[]{:S(2)}) copy-start(bf16[768,4,128]{2,0,1:T(8,128)(2,1)S(1)} %get-tuple-element.944) | copy-start | bytes 2359300
  67.1 22.8 %copy-start.2 = (f32[12,4,64,64]{2,3,1,0:T(8,128)}, f32[12,4,64,64]{2,3,1,0:T(8,128)S(1)}, u32[]{:S(2)}) copy-start(f32[12,4,64,64]{2,3,1,0:T(8,128)S(1)} %get-tuple-element.948) | copy-start | bytes 2359300
  112.5 126.6 %copy-start.151 = (bf16[256]{0:T(256)(128)(2,1)S(1)}, bf16[256]{0:T(256)(128)(2,1)}, u32[]{:S(2)}) copy-start(bf16[256]{0:T(256)(128)(2,1)} %param.30) | copy-start | bytes 1540
  238.3 90.8 %all-gather.11.cloned.1.call-start = ((), (), s32[]{:S(2)}) async-start(), calls=%async_computation.15 | async-start | bytes 2359296 | tf_op jit(solution)/shard_map/all_gather | solution.py:24
  239.1 182.0 %all-reduce.30.cloned.1.call-start = ((), (), s32[]{:S(2)}) async-start(), calls=%async_computation.5 | async-start | bytes 6291456 | tf_op jit(solution)/shard_map/psum | solution.py:299
  344.0 195.9 %all-reduce.32.cloned.1.call-start = ((), (), s32[]{:S(2)}) async-start(), calls=%async_computation.6 | async-start | bytes 6291456 | tf_op jit(solution)/shard_map/psum | solution.py:314
  344.7 285.4 %copy-start.109 = (f32[2048]{0:T(1024)}, f32[2048]{0:T(1024)S(1)}, u32[]{:S(2)}) copy-start(f32[2048]{0:T(1024)S(1)} %convert_element_type.284) | copy-start | bytes 24580
  425.7 204.3 %copy-start.133 = (f32[768]{0:T(1024)}, f32[768]{0:T(1024)S(1)}, u32[]{:S(2)}) copy-start(f32[768]{0:T(1024)S(1)} %add_rsqrt_fusion.2) | copy-start | bytes 9220
  471.2 120.1 %all-gather.13.cloned.1.call-start = ((), (), s32[]{:S(2)}) async-start(), calls=%async_computation.16 | async-start | bytes 2359296 | tf_op jit(solution)/shard_map/all_gather | solution.py:43
  472.2 193.1 %all-gather.15.cloned.1.call-start = ((), (), s32[]{:S(2)}) async-start(), calls=%async_computation.17 | async-start | bytes 4718592 | tf_op jit(solution)/shard_map/all_gather | solution.py:43
  550.2 79.9 %copy-start.138 = (f32[768]{0:T(1024)}, f32[768]{0:T(1024)S(1)}, u32[]{:S(2)}) copy-start(f32[768]{0:T(1024)S(1)} %broadcast_multiply_fusion.2) | copy-start | bytes 9220
  570.7 450.9 %all-reduce.34.cloned.1.call-start = ((), (), s32[]{:S(2)}) async-start(), calls=%async_computation.7 | async-start | bytes 6291456 | tf_op jit(solution)/shard_map/psum | solution.py:347
  681.5 340.1 %reduce-scatter.8.cloned.1.call-start = ((), (), s32[]{:S(2)}) async-start(), calls=%async_computation.8 | async-start | bytes 4718592 | tf_op jit(solution)/shard_map/reduce_scatter | solution.py:349
  682.3 339.3 %reduce-scatter.12.cloned.1.call-start = ((), (), s32[]{:S(2)}) async-start(), calls=%async_computation.10 | async-start | bytes 6488064 | tf_op jit(solution)/shard_map/reduce_scatter | solution.py:349
  683.1 468.0 %reduce-scatter.10.cloned.1.call-start = ((), (), s32[]{:S(2)}) async-start(), calls=%async_computation.9 | async-start | bytes 12976128 | tf_op jit(solution)/shard_map/reduce_scatter | solution.py:349
  690.2 590.2 %all-reduce.36.cloned.1.call-start = ((), (), s32[]{:S(2)}) async-start(), calls=%async_computation.11 | async-start | bytes 6291456 | tf_op jit(solution)/shard_map/psum | solution.py:374
  697.2 232.8 %copy-start.9 = (bf16[768,4,128]{2,0,1:T(8,128)(2,1)S(1)}, bf16[768,4,128]{2,0,1:T(8,128)(2,1)}, u32[]{:S(2)}) copy-start(bf16[768,4,128]{2,0,1:T(8,128)(2,1)} %copy-done.8) | copy-start | bytes 2359300
  697.3 232.8 %copy-start.62 = (pred[12,64,64]{1,2,0:T(8,128)(4,1)S(1)}, pred[12,64,64]{1,2,0:T(8,128)(4,1)}, u32[]{:S(2)}) copy-start(pred[12,64,64]{1,2,0:T(8,128)(4,1)} %copy-done.61) | copy-start | bytes 147460
  697.3 232.9 %copy-start.64 = (f32[12,4,64]{2,1,0:T(4,128)S(1)}, f32[12,4,64]{2,1,0:T(4,128)}, u32[]{:S(2)}) copy-start(f32[12,4,64]{2,1,0:T(4,128)} %copy-done.63) | copy-start | bytes 36868
  1016.3 134.8 %copy-start.104 = (f32[768,4,1]{0,1,2:T(4,128)S(1)}, f32[768,4,1]{0,1,2:T(4,128)}, u32[]{:S(2)}) copy-start(f32[768,4,1]{0,1,2:T(4,128)} %copy-done.103) | copy-start | bytes 36868
  1016.4 134.8 %copy-start.130 = (f32[768,4,2]{0,1,2:T(4,128)S(1)}, f32[768,4,2]{0,1,2:T(4,128)}, u32[]{:S(2)}) copy-start(f32[768,4,2]{0,1,2:T(4,128)} %copy-done.129) | copy-start | bytes 73732
  1016.4 134.8 %copy-start.144 = (f32[4]{0:T(128)S(1)}, f32[4]{0:T(128)}, u32[]{:S(2)}) copy-start(f32[4]{0:T(128)} %param.29) | copy-start | bytes 52
  1016.4 134.8 %copy-start.146 = (f32[4]{0:T(128)S(1)}, f32[4]{0:T(128)}, u32[]{:S(2)}) copy-start(f32[4]{0:T(128)} %copy-done.145) | copy-start | bytes 52
  1176.7 11.8 collective-permute-start.2
  1210.6 136.0 %reduce-scatter.16.cloned.1.call-start = ((), (), s32[]{:S(2)}) async-start(), calls=%async_computation.18 | async-start | bytes 589824
  1218.8 254.0 %all-reduce.38.cloned.1.call-start = ((), (), s32[]{:S(2)}) async-start(), calls=%async_computation.12 | async-start | bytes 303104 | tf_op jit(solution)/shard_map/psum | solution.py:394
  1286.0 399.6 %reduce-scatter.14.cloned.1.call-start = ((), (), s32[]{:S(2)}) async-start(), calls=%async_computation.13 | async-start | bytes 14155776 | tf_op jit(solution)/shard_map/reduce_scatter | solution.py:403
  1307.5 40.8 %copy-start.110 = (f32[2048]{0:T(1024)S(1)}, f32[2048]{0:T(1024)}, u32[]{:S(2)}) copy-start(f32[2048]{0:T(1024)} %copy-done.109) | copy-start | bytes 24580
  1307.5 40.8 %copy-start.134 = (f32[768]{0:T(1024)S(1)}, f32[768]{0:T(1024)}, u32[]{:S(2)}) copy-start(f32[768]{0:T(1024)} %copy-done.133) | copy-start | bytes 9220
  1307.5 40.8 %copy-start.139 = (f32[768]{0:T(1024)S(1)}, f32[768]{0:T(1024)}, u32[]{:S(2)}) copy-start(f32[768]{0:T(1024)} %copy-done.138) | copy-start | bytes 9220
  (123 other events, 478.3 us)
Sparse Core Ops, SparseCore 0:
  238.4 39.8 all-gather.8
  280.9 48.0 all-gather.10
  344.1 76.8 all-reduce.29
  471.4 68.5 all-reduce.31
  541.9 49.3 all-gather.12
  593.3 71.8 all-gather.14
  681.7 66.6 all-reduce.33
  752.0 88.3 reduce-scatter.7
  844.5 110.1 reduce-scatter.11
  958.6 192.4 reduce-scatter.9
  1210.7 69.6 all-reduce.35
  1284.5 62.0 reduce-scatter.15
  1352.7 120.0 all-reduce.37
  1476.3 209.3 reduce-scatter.13

commit v2 on v1

--- a/solution.py
+++ b/solution.py
@@ -1,7 +1,13 @@
+import functools
+
 import jax
 import jax.numpy as jnp
 from jax import lax
+from jax.experimental import pallas as pl
+from jax.experimental.pallas import tpu as pltpu
 from jax.sharding import PartitionSpec as P
+
+MESH_IDS = pl.DeviceIdType.MESH
 
 DK = 128
 GROUP = 64
@@ -18,11 +24,86 @@
     return lax.ppermute(block, axis, route)
 
 
+def peer_gather_kernel(axis, count, mode, x_ref, out_ref, send_sem, recv_sem):
+    me = lax.axis_index(axis)
+    barrier = pltpu.get_barrier_semaphore()
+    for step in range(1, count):
+        pl.semaphore_signal(
+            barrier, inc=1, device_id={axis: lax.rem(me + step, count)}, device_id_type=MESH_IDS
+        )
+    pl.semaphore_wait(barrier, count - 1)
+
+    def link(step, source, target):
+        return pltpu.make_async_remote_copy(
+            src_ref=x_ref,
+            dst_ref=out_ref.at[source],
+            send_sem=send_sem.at[step],
+            recv_sem=recv_sem.at[step],
+            device_id={axis: target},
+            device_id_type=MESH_IDS,
+        )
+
+    def target_of(step):
+        if mode == "up":
+            return me + step, me + step < count
+        if mode == "down":
+            return me - step, me - step >= 0
+        return lax.rem(me + step, count), me >= 0
+
+    def source_of(step):
+        if mode == "up":
+            return me - step, me - step >= 0
+        if mode == "down":
+            return me + step, me + step < count
+        return lax.rem(me + count - step, count), me >= 0
+
+    for step in range(1, count):
+        target, sending = target_of(step)
+
+        @pl.when(sending)
+        def _():
+            link(step, me, target).start()
+
+    for step in range(1, count):
+        target, sending = target_of(step)
+        source, receiving = source_of(step)
+
+        @pl.when(sending)
+        def _():
+            link(step, me, target).wait_send()
+
+        @pl.when(receiving)
+        def _():
+            link(step, source, source).wait_recv()
+
+
+def peer_gather(x, axis, mode, collective_id):
+    count = lax.axis_size(axis)
+    return pl.pallas_call(
+        functools.partial(peer_gather_kernel, axis, count, mode),
+        out_shape=jax.ShapeDtypeStruct((count,) + x.shape, x.dtype),
+        in_specs=[pl.BlockSpec(memory_space=pl.ANY)],
+        out_specs=pl.BlockSpec(memory_space=pl.ANY),
+        scratch_shapes=[pltpu.SemaphoreType.DMA((count,)), pltpu.SemaphoreType.DMA((count,))],
+        compiler_params=pltpu.CompilerParams(collective_id=collective_id, has_side_effects=True),
+    )(x)
+
+
+def joined_gather(value, axis, mode, collective_id, kind):
+    widths = [part.shape[-1] for part in value]
+    packed = jnp.concatenate([part.astype(kind) for part in value], axis=-1)
+    gathered = peer_gather(packed, axis, mode, collective_id)
+    pieces = []
+    start_at = 0
+    for width in widths:
+        pieces.append(gathered[..., start_at : start_at + width])
+        start_at += width
+    return tuple(pieces)
+
+
 def carried_in(value, axis, join, neutral):
     place = lax.axis_index(axis)
-    gathered = jax.tree.map(
-        lambda a, kind: lax.all_gather(a.astype(kind), axis), value, (jnp.bfloat16, jnp.bfloat16)
-    )
+    gathered = joined_gather(value, axis, "up", 1, jnp.bfloat16)
     state = jax.tree.map(lambda a, e: jnp.zeros_like(a) + jnp.asarray(e, a.dtype), value, neutral)
 
     def one(lap, state):
@@ -52,6 +133,16 @@
         return jax.tree.map(lambda new, old: jnp.where(position < mine, new, old), longer, running)
 
     return lax.fori_loop(0, count - 1, lap, running)
+
+
+def own_then_peers(flat, axis, collective_id):
+    size = flat.shape[0]
+    padded = -(-size // 1024) * 1024
+    tiles = jnp.pad(flat, (0, padded - size)).reshape(padded // 128, 128)
+    gathered = peer_gather(tiles, axis, "all", collective_id)
+    slots = lax.broadcasted_iota(jnp.int32, gathered.shape, 0)
+    filled = jnp.where(slots == lax.axis_index(axis), tiles[None], gathered)
+    return filled.reshape(gathered.shape[0], padded)[:, :size]
 
 
 def rounded(values):
@@ -376,36 +467,41 @@
     grad_tokens = (grad_residual + norm_back(mixer_in, gain_one, x_hat_one, scale_one)).astype(
         jnp.bfloat16
     )
-    total_heads = head_count * lax.axis_size("tp")
-    head_start = tp_index * head_count
-    zero_index = tp_index * 0
-    conv_full = lax.dynamic_update_slice(
-        jnp.zeros((taps_all, total_heads, conv_width), jnp.float32),
-        conv_grad,
-        (zero_index, head_start, zero_index),
-    )
-    a_log_full = lax.dynamic_update_slice(
-        jnp.zeros((total_heads,), jnp.float32), a_log_grad, (head_start,)
-    )
-    dt_bias_full = lax.dynamic_update_slice(
-        jnp.zeros((total_heads,), jnp.float32), dt_bias_grad, (head_start,)
-    )
-    small_parts = (gain_one_grad, gain_two_grad, out_gain_grad, conv_full, a_log_full, dt_bias_full)
-    small_flat = lax.psum(
-        jnp.concatenate([part.reshape(-1) for part in small_parts]), ("seq", "tp")
-    )
+    seq_index = lax.axis_index("seq")
+    tp_count = lax.axis_size("tp")
+    seq_parts = (gain_one_grad, gain_two_grad, out_gain_grad, conv_grad, a_log_grad, dt_bias_grad)
+    seq_summed = own_then_peers(
+        jnp.concatenate([part.reshape(-1) for part in seq_parts] + [grad_rate.reshape(-1)]),
+        "seq",
+        3,
+    )
+    seq_summed = jnp.sum(seq_summed, axis=0)
+    tp_size = sum(part.size for part in seq_parts)
+    rate_rows = grad_rate.shape[0] // lax.axis_size("seq")
+    rate_sum = lax.dynamic_slice_in_dim(
+        seq_summed[tp_size:].reshape(grad_rate.shape), seq_index * rate_rows, rate_rows, 0
+    )
+    by_tp = own_then_peers(seq_summed[:tp_size], "tp", 4)
     small_sums = []
     start_at = 0
-    for part in small_parts:
-        small_sums.append(small_flat[start_at : start_at + part.size].reshape(part.shape))
+    for part in seq_parts:
+        piece = by_tp[:, start_at : start_at + part.size]
         start_at += part.size
+        if part.ndim == 1 and part.shape[0] != head_count:
+            small_sums.append(jnp.sum(piece, axis=0))
+        elif part.ndim == 1:
+            small_sums.append(piece.reshape(tp_count * head_count))
+        else:
+            small_sums.append(
+                jnp.moveaxis(piece.reshape((tp_count,) + part.shape), 0, 1).reshape(
+                    (taps_all, tp_count * head_count, conv_width)
+                )
+            )
     weight_sums = (
         lax.psum_scatter(
             grad_mix.astype(jnp.bfloat16), "seq", scatter_dimension=0, tiled=True
         ).astype(jnp.float32),
-        lax.psum_scatter(
-            grad_rate.astype(jnp.bfloat16), "seq", scatter_dimension=0, tiled=True
-        ).astype(jnp.float32),
+        rate_sum,
         early_sums[0].astype(jnp.float32),
         early_sums[1].astype(jnp.float32),
         early_sums[2].astype(jnp.float32),

time: 1710 us -> 1380 us (0.81)
  waiting for transfers between devices: 822 us -> 385 us
  Pallas kernels: 0 us -> 94.7 us
    psum x1 -> x0, waiting for transfers between devices: 114 us -> none  [shards(): lax.psum(jnp.concatenate([part.reshape(-1) for part in small_parts]), ('s...]
    reduce_scatter x1, waiting for transfers between devices: 207 us -> 102 us  [shards(): lax.psum_scatter(grad_mix.astype(jnp.bfloat16), 'seq', scatter_dimension=...]
    pallas_call x0 -> x3, Pallas kernels: none -> 94.7 us  [peer_gather(): pl.pallas_call(functools.partial(peer_gather_kernel, axis, count, mode),...]
    all_gather x2 -> x0, waiting for transfers between devices: 84.8 us -> none  [carried_in(): lax.all_gather(a.astype(kind), axis)]
    reduce_scatter x3, waiting for transfers between devices: 129 us -> 60.5 us  [shards(): lax.psum_scatter(part, 'seq', scatter_dimension=0, tiled=True)]
    unnamed x15 -> x10, waiting for transfers between devices: 37.5 us -> 0.83 us
    psum x1, waiting for transfers between devices: 61.5 us -> 34.1 us  [shards(): lax.psum(mixer_in_part.astype(jnp.bfloat16), 'tp').astype(jnp.float32)]
    all_gather x2, waiting for transfers between devices: 44.1 us -> 23.9 us  [carried_in_2(): pieces = jax.tree.map(lambda part: lax.all_gather(part, axis), value)]
  transfers between devices with their start and end apart: 17 -> 13, of which waited for: 11 -> 6; matrix products, arithmetic and copies ran while one was open for 30% -> 38% of each run, Pallas kernels for 0% -> 3%
where the time goes in v2:
time: 1380 us; the launch traced here: 1370 us
  matrix products  565 us (41%)
  waiting for transfers between devices  385 us (28%)
  local copies, waits for them, and re-layouts  161 us (12%)
  other arithmetic  133 us (10%)
  Pallas kernels  94.7 us (7%)
  between operations  18.1 us (1%)
    reduce_scatter x1, waiting for transfers between devices, shards(): lax.psum_scatter(grad_mix.astype(jnp.bfloat16), 'seq', scatter_dimension=...  102 us
    psum x1, waiting for transfers between devices, shards(): lax.psum(mixer_part.astype(jnp.bfloat16), 'tp').astype(jnp.float32)  95.1 us
    pallas_call x3, Pallas kernels, peer_gather(): pl.pallas_call(functools.partial(peer_gather_kernel, axis, count, mode),...  94.7 us
    dot_general x36, matrix products, advance(): jnp.einsum('htk,hkw->htw', state_rows, carried_state, precision=FAST_ARIT...  72.9 us
    dot_general x36, matrix products, advance(): jnp.einsum('htj,hjw->htw', mixing, new_values, precision=FAST_ARITHMETIC)  68.2 us
    psum x1, waiting for transfers between devices, shards(): lax.psum(ffn_in_part.astype(jnp.bfloat16), 'tp').astype(jnp.float32)  67.7 us
    dot_general x36, matrix products, advance(): jnp.einsum('htk,hkw->htw', query_rows, carried_state, precision=FAST_ARIT...  65.1 us
    dot_general x36, matrix products, advance(): jnp.einsum('hjk,hjw->hkw', end_rows, new_values, precision=FAST_ARITHMETIC)  62.1 us
  transfers between devices with their start and end apart: 13, of which 6 were waited for; matrix products, arithmetic and copies ran while one was open for 38% of the time, Pallas kernels for 3%

profile of v2, /device:TPU:0, one launch (start us, length us, event | category | flops | bytes accessed | tf_op | source)
XLA Modules:
  0.0 1369.5 jit_solution(9288334628656844262)
XLA Ops:
  9.0 4.9 collective-permute-start
  17.2 15.6 %fusion.307 = (bf16[768,4,768]{2,0,1:T(8,128)(2,1)S(1)}, f32[768,4,768]{2,0,1:T(8,128)}) fusion(bf16[2048,4,768]{2,1,0:T(4,128)(2,1)} %param.25, bf16[768,2048]{1,0:T(8,128)(2,1)S(1)} %copy-done.4, f32[2048]{0:T(1024)S(1)} %convert_element_type.254, f32[768]{0:T(1024)S(1)} %add_rsqrt_fusion.3), kind=kOutput, calls=%fused_computation.513 | convolution fusion | flops 9672327168 | bytes 29895680 | tf_op jit(solution)/shard_map/td,dhc->thc/dot_general | solution.py:338
  35.6 4.3 collective-permute-start.1
  39.9 3.8 slice.196
  53.3 6.3 fusion.95
  99.0 4.3 fusion.99
  114.6 125.0 %while.76 = (s32[]{:T(128)}, f32[4,128,384]{2,1,0:T(8,128)S(1)}, f32[12,4,64,384]{3,2,1,0:T(8,128)}, f32[12,4,128,384]{3,2,1,0:T(8,128)}, f32[12,4,64,384]{3,2,1...) while((s32[]{:T(128)}, f32[4,128,384]{2,1,0:T(8,128)S(1)}, ...), condition=%wide.region_6.7_spmd, body=%wide.region_5.6_spmd.sunk | while | flops 264929280 | bytes 8792293 | solution.py:295
  240.6 53.5 %shard_map.237 = bf16[8,4,128,384]{3,2,1,0:T(8,128)(2,1)} custom-call(bf16[4,128,384]{2,1,0:T(8,128)(2,1)} %pad_maximum_fusion.3.x_ref), custom_call_target="tpu_custom_call" | custom-call | tf_op jit(solution)/shard_map/pallas_call | solution.py:82
  308.3 5.0 bitcast_convert_fusion.1
  313.9 95.1 %all-reduce.30.cloned.1.call-done = bf16[768,2048]{1,0:T(8,128)(2,1)} async-done(((bf16[768,2048]{1,0:T(8,128)(2,1)}), bf16[768,2048]{1,0:T(8,128)(2,1)}) %all-reduce.30.cloned.1.call-update) | async-done | bytes 3145744 | tf_op jit(solution)/shard_map/psum | solution.py:390
  409.1 4.1 multiply_reduce_fusion.5
  413.8 15.6 %fusion.76 = f32[768,2,1408]{2,0,1:T(8,128)} fusion(bf16[2048,2,1408]{2,1,0:T(2,128)(2,1)} %param.33, bf16[768,2048]{1,0:T(8,128)(2,1)S(1)} %copy-done.28, bf16[768,2048]{1,0:T(8,128)(2,1)S(1)} %copy-done.5, f32[2048]{0:T(1024)S(1)} %convert_element_type.282, f32[768]{0:T(1024)S(1)} %add_rsqrt_fusion.2), kind=kOutput, calls=%fused_computation.102 | convolution fusion | flops 8867807232 | bytes 26487808 | tf_op jit(solution)/shard_map/td,dcf->tcf/dot_general | solution.py:394
  429.4 12.6 multiply_bitcast_fusion
  442.0 17.0 %bitcast_convert_fusion = (bf16[768,2048]{1,0:T(8,128)(2,1)}, f32[768,2048,1]{1,0,2:T(8,128)}) fusion(bf16[2048,2,1408]{2,1,0:T(2,128)(2,1)} %param.33, f32[768,1,1408]{2,0,1:T(8,128)} %get-tuple-element.935, f32[768,1,1408]{2,0,1:T(8,128)} %get-tuple-element.934), kind=kOutput, calls=%fused_computation.132 | convolution fusion | flops 8864268288 | bytes 29622272 | tf_op jit(solution)/shard_map/tcf,dcf->td/dot_general | solution.py:404
  460.0 67.7 %all-reduce.32.cloned.1.call-done = bf16[768,2048]{1,0:T(8,128)(2,1)} async-done(((bf16[768,2048]{1,0:T(8,128)(2,1)}), bf16[768,2048]{1,0:T(8,128)(2,1)}) %all-reduce.32.cloned.1.call-update) | async-done | bytes 3145744 | tf_op jit(solution)/shard_map/psum | solution.py:405
  527.7 7.7 fusion.94
  537.8 11.4 multiply_reduce_fusion.6
  554.4 3.9 fusion.132
  558.8 9.8 fusion.82
  568.5 8.9 convolution_convert_fusion.4
  577.4 16.7 %convolution_convert_fusion = bf16[2048,2,1408]{2,0,1:T(8,128)(2,1)} fusion(f32[768,1,1408]{2,0,1:T(8,128)} %get-tuple-element.935, f32[768,1,1408]{2,0,1:T(8,128)} %get-tuple-element.934, bf16[768,2048]{1,0:T(8,128)(2,1)} %all-reduce.30.cloned.1.call-done, bf16[768,2048]{1,0:T(8,128)(2,1)S(1)} %copy-done.6, f32[2048]{0:T(1024)S(1)} %convert_element_type.282, ...), kind=kOutput, calls=%fused_computation.99 | convolution fusion | flops 8877899776 | bytes 26487808 | tf_op jit(solution)/shard_map/td,tcf->dcf/dot_general | solution.py:401
  594.2 11.7 convolution_convert_fusion.3
  607.6 23.9 %all-gather.7.cloned.1.call-done = f32[32,128,256]{2,1,0:T(8,128)} async-done(((f32[4,128,256]{2,1,0:T(8,128)}), f32[32,128,256]{2,1,0:T(8,128)}) %all-gather.7.cloned.1.call-update) | async-done | bytes 4194320 | tf_op jit(solution)/shard_map/all_gather | solution.py:124
  631.5 4.7 rev.7
  636.2 10.6 while.79
  662.5 233.4 %while.78 = (s32[]{:T(128)}, f32[4,128,384]{2,1,0:T(8,128)S(1)}, f32[12,4,64,384]{3,2,1,0:T(8,128)}, f32[12,4,64,128]{3,2,1,0:T(8,128)}, f32[12,4,64,128]{3,2,1,...) while((s32[]{:T(128)}, f32[4,128,384]{2,1,0:T(8,128)S(1)}, ...), condition=%wide.region_24.25_spmd, body=%wide.region_21.24_spmd.sunk | while | flops 530153216 | bytes 14433113 | solution.py:295
  896.0 3.9 multiply_bitcast_fusion.1
  941.5 3.8 fusion.313
  953.7 4.0 fusion.173
  957.7 7.5 multiply_select_fusion
  987.4 60.4 %reduce-scatter.7.cloned.1.call-done = bf16[256,2,1408]{2,0,1:T(8,128)(2,1)} async-done(((bf16[2048,2,1408]{2,0,1:T(8,128)(2,1)}), bf16[256,2,1408]{2,0,1:T(8,128)(2,1)}) %reduce-scatter.7.cloned.1.call-update) | async-done | bytes 1441808 | tf_op jit(solution)/shard_map/reduce_scatter | solution.py:440
  1048.1 3.9 multiply_reduce_fusion.10
  1052.2 4.5 add_add_fusion.2
  1056.8 9.7 multiply_reduce_fusion.3
  1066.6 6.0 multiply_multiply_fusion.2
  1078.3 6.8 pad_add_fusion
  1085.1 3.7 fusion.93
  1090.5 16.7 %fusion.308 = (bf16[768,2048]{1,0:T(8,128)(2,1)}, f32[768,2048]{1,0:T(8,128)}) fusion(f32[768,2048,1]{1,0,2:T(8,128)} %fusion.262, bf16[2048,4,768]{2,1,0:T(4,128)(2,1)} %param.25, bf16[768,4,256]{2,0,1:T(8,128)(2,1)} %get-tuple-element.933, bf16[768,4,512]{2,0,1:T(8,128)(2,1)S(1)} %fusion.93), kind=kOutput, calls=%fused_computation.514 | convolution fusion | flops 9676259328 | bytes 33030144 | tf_op jit(solution)/shard_map/thc,dhc->td/dot_general | solution.py:462
  1109.1 16.1 %convolution_convert_fusion.2 = bf16[2048,4,768]{2,0,1:T(8,128)(2,1)} fusion(bf16[768,4,256]{2,0,1:T(8,128)(2,1)} %get-tuple-element.933, bf16[768,4,512]{2,0,1:T(8,128)(2,1)} %copy-done.68, bf16[768,2048]{1,0:T(8,128)(2,1)S(1)} %copy-done.7, f32[2048]{0:T(1024)S(1)} %copy-done.115, f32[768]{0:T(1024)S(1)} %copy-done.133), kind=kOutput, calls=%fused_computation.114 | convolution fusion | flops 9685696512 | bytes 20458496 | tf_op jit(solution)/shard_map/td,thc->dhc/dot_general | solution.py:458
  1129.2 5.5 reshape.1267
  1142.9 34.1 %all-reduce.36.cloned.1.call-done = bf16[768,2048]{1,0:T(8,128)(2,1)} async-done(((bf16[768,2048]{1,0:T(8,128)(2,1)}), bf16[768,2048]{1,0:T(8,128)(2,1)}) %all-reduce.36.cloned.1.call-update) | async-done | bytes 3145744 | tf_op jit(solution)/shard_map/psum | solution.py:465
  1177.0 4.8 fusion.89
  1182.6 36.2 %shard_map.238 = f32[8,232,128]{2,1,0:T(8,128)} custom-call(f32[232,128]{1,0:T(8,128)} %pad_bitcast_fusion.x_ref), custom_call_target="tpu_custom_call" | custom-call | tf_op jit(solution)/shard_map/pallas_call | solution.py:82
  1221.3 5.0 shard_map.239
  1227.5 6.9 reshape.1270
  1244.5 10.9 fusion.88
  1255.4 102.5 %reduce-scatter.11.cloned.1.call-done = bf16[256,4,768]{2,0,1:T(8,128)(2,1)} async-done(((bf16[2048,4,768]{2,0,1:T(8,128)(2,1)}), bf16[256,4,768]{2,0,1:T(8,128)(2,1)}) %reduce-scatter.11.cloned.1.call-update) | async-done | bytes 1572880 | tf_op jit(solution)/shard_map/reduce_scatter | solution.py:501
  1357.9 4.3 copy.309
  (825 shorter events, 584.9 us)
Async XLA Ops:
  8.0 35.7 %copy-start = (bf16[2048,4,2]{0,2,1:T(2,128)(2,1)S(1)}, bf16[2048,4,2]{0,2,1:T(2,128)(2,1)}, u32[]{:S(2)}) copy-start(bf16[2048,4,2]{0,2,1:T(2,128)(2,1)} %param.26) | copy-start | bytes 98308
  8.0 401.0 %all-reduce.30.cloned.1.call-start = ((), (), s32[]{:S(2)}) async-start(), calls=%async_computation.4 | async-start | bytes 6291456 | tf_op jit(solution)/shard_map/psum | solution.py:390
  9.0 39.1 %collective-permute-start = (bf16[3]{0:T(256)(128)(2,1)S(1)}, bf16[3]{0:T(256)(128)(2,1)S(1)}, u32[]{:S(2)}, u32[]{:S(2)}) collective-permute-start(bf16[3]{0:T(256)(128)(2,1)S(1)} %slice.149), channel_id=1, source_target_pairs={{0,4},{4,8},{8,12},{12,16},{16,20},{20,24},{24,28},{1,5},{5,9},{9,... | collective-permute-start | bytes 26 | tf_op jit(solution)/shard_map/ppermute | solution.py:24
  14.6 29.1 %copy-start.114 = (f32[2048]{0:T(1024)}, f32[2048]{0:T(1024)S(1)}, u32[]{:S(2)}) copy-start(f32[2048]{0:T(1024)S(1)} %convert_element_type.254) | copy-start | bytes 24580
  17.2 26.6 %copy-start.132 = (f32[768]{0:T(1024)}, f32[768]{0:T(1024)S(1)}, u32[]{:S(2)}) copy-start(f32[768]{0:T(1024)S(1)} %add_rsqrt_fusion.3) | copy-start | bytes 9220
  35.6 14.8 %collective-permute-start.1 = (bf16[3,4,512]{2,0,1:T(4,128)(2,1)}, bf16[3,4,512]{2,0,1:T(4,128)(2,1)}, u32[]{:S(2)}, u32[]{:S(2)}) collective-permute-start(bf16[3,4,512]{2,0,1:T(4,128)(2,1)} %slice.195), channel_id=1, source_target_pairs={{0,4},{4,8},{8,12},{12,16},{16,20},{20,24},{24,28},{1,5},{5,9},{9,... | collective-permute-start | bytes 36872 | tf_op jit(solution)/shard_map/ppermute | solution.py:24
  46.1 19.8 %copy-start.64 = (f32[12,4,64]{2,1,0:T(4,128)}, f32[12,4,64]{2,1,0:T(4,128)S(1)}, u32[]{:S(2)}) copy-start(f32[12,4,64]{2,1,0:T(4,128)S(1)} %copy.217) | copy-start | bytes 36868
  46.2 25.8 %copy-start.74 = (f32[64,64]{0,1:T(8,128)}, f32[64,64]{0,1:T(8,128)S(1)}, u32[]{:S(2)}) copy-start(f32[64,64]{0,1:T(8,128)S(1)} %fusion.259) | copy-start | bytes 49156
  46.6 52.4 %copy-start.72 = (f32[12,4,64]{2,1,0:T(4,128)}, f32[12,4,64]{2,1,0:T(4,128)S(1)}, u32[]{:S(2)}) copy-start(f32[12,4,64]{2,1,0:T(4,128)S(1)} %copy.219) | copy-start | bytes 36868
  48.1 23.8 %copy-start.76 = (f32[64,64]{0,1:T(8,128)}, f32[64,64]{0,1:T(8,128)S(1)}, u32[]{:S(2)}) copy-start(f32[64,64]{0,1:T(8,128)S(1)} %get-tuple-element.979) | copy-start | bytes 49156
  48.1 26.7 %copy-start.88 = (f32[64,64]{0,1:T(8,128)}, f32[64,64]{0,1:T(8,128)S(1)}, u32[]{:S(2)}) copy-start(f32[64,64]{0,1:T(8,128)S(1)} %get-tuple-element.977) | copy-start | bytes 49156
  48.1 32.2 %copy-start.86 = (f32[64,64]{0,1:T(8,128)}, f32[64,64]{0,1:T(8,128)S(1)}, u32[]{:S(2)}) copy-start(f32[64,64]{0,1:T(8,128)S(1)} %get-tuple-element.976) | copy-start | bytes 49156
  48.1 38.0 %copy-start.84 = (f32[64,64]{0,1:T(8,128)}, f32[64,64]{0,1:T(8,128)S(1)}, u32[]{:S(2)}) copy-start(f32[64,64]{0,1:T(8,128)S(1)} %get-tuple-element.975) | copy-start | bytes 49156
  48.1 43.5 %copy-start.82 = (f32[64,64]{0,1:T(8,128)}, f32[64,64]{0,1:T(8,128)S(1)}, u32[]{:S(2)}) copy-start(f32[64,64]{0,1:T(8,128)S(1)} %get-tuple-element.974) | copy-start | bytes 49156
  49.1 16.9 %copy-start.39 = (f32[12,64,64]{1,2,0:T(8,128)}, f32[12,64,64]{1,2,0:T(8,128)S(1)}, u32[]{:S(2)}) copy-start(f32[12,64,64]{1,2,0:T(8,128)S(1)} %get-tuple-element.964) | copy-start | bytes 589828
  49.1 16.9 %copy-start.59 = (f32[12,64,64]{1,2,0:T(8,128)}, f32[12,64,64]{1,2,0:T(8,128)S(1)}, u32[]{:S(2)}) copy-start(f32[12,64,64]{1,2,0:T(8,128)S(1)} %get-tuple-element.965) | copy-start | bytes 589828
  49.1 16.9 %copy-start.62 = (pred[12,64,64]{1,2,0:T(8,128)(4,1)}, pred[12,64,64]{1,2,0:T(8,128)(4,1)S(1)}, u32[]{:S(2)}) copy-start(pred[12,64,64]{1,2,0:T(8,128)(4,1)S(1)} %get-tuple-element.963) | copy-start | bytes 147460
  50.3 13.5 copy-start.96
  50.4 52.9 %copy-start.90 = (f32[12,4,64]{2,1,0:T(4,128)}, f32[12,4,64]{2,1,0:T(4,128)S(1)}, u32[]{:S(2)}) copy-start(f32[12,4,64]{2,1,0:T(4,128)S(1)} %copy.243) | copy-start | bytes 36868
  63.3 39.9 %copy-start.8 = (bf16[768,4,128]{2,0,1:T(8,128)(2,1)}, bf16[768,4,128]{2,0,1:T(8,128)(2,1)S(1)}, u32[]{:S(2)}) copy-start(bf16[768,4,128]{2,0,1:T(8,128)(2,1)S(1)} %get-tuple-element.946) | copy-start | bytes 2359300
  69.1 22.5 %copy-start.2 = (f32[12,4,64,64]{2,3,1,0:T(8,128)}, f32[12,4,64,64]{2,3,1,0:T(8,128)S(1)}, u32[]{:S(2)}) copy-start(f32[12,4,64,64]{2,3,1,0:T(8,128)S(1)} %get-tuple-element.950) | copy-start | bytes 2359300
  239.6 54.5 %copy-start.61 = (f32[12,4,64,128]{3,2,1,0:T(8,128)}, f32[12,4,64,128]{3,2,1,0:T(8,128)S(1)}, u32[]{:S(2)}) copy-start(f32[12,4,64,128]{3,2,1,0:T(8,128)S(1)} %get-tuple-element.1455) | copy-start | bytes 4718596
  239.6 54.5 %copy-start.92 = (f32[12,4,64]{2,0,1:T(8,128)}, f32[12,4,64]{2,0,1:T(8,128)S(1)}, u32[]{:S(2)}) copy-start(f32[12,4,64]{2,0,1:T(8,128)S(1)} %get-tuple-element.1480) | copy-start | bytes 36868
  313.3 214.4 %all-reduce.32.cloned.1.call-start = ((), (), s32[]{:S(2)}) async-start(), calls=%async_computation.5 | async-start | bytes 6291456 | tf_op jit(solution)/shard_map/psum | solution.py:405
  313.9 280.2 %copy-start.110 = (f32[2048]{0:T(1024)}, f32[2048]{0:T(1024)S(1)}, u32[]{:S(2)}) copy-start(f32[2048]{0:T(1024)S(1)} %convert_element_type.282) | copy-start | bytes 24580
  413.7 180.4 %copy-start.134 = (f32[768]{0:T(1024)}, f32[768]{0:T(1024)S(1)}, u32[]{:S(2)}) copy-start(f32[768]{0:T(1024)S(1)} %add_rsqrt_fusion.2) | copy-start | bytes 9220
  413.7 15.6 %copy-start.66 = (bf16[768,2048]{1,0:T(8,128)(2,1)S(1)}, bf16[768,2048]{1,0:T(8,128)(2,1)}, u32[]{:S(2)}) copy-start(bf16[768,2048]{1,0:T(8,128)(2,1)} %param.35) | copy-start | bytes 9437188
  459.0 146.9 %all-gather.5.cloned.1.call-start = ((), (), s32[]{:S(2)}) async-start(), calls=%async_computation.12 | async-start | bytes 2359296 | tf_op jit(solution)/shard_map/all_gather | solution.py:124
  459.9 171.5 %all-gather.7.cloned.1.call-start = ((), (), s32[]{:S(2)}) async-start(), calls=%async_computation.13 | async-start | bytes 4718592 | tf_op jit(solution)/shard_map/all_gather | solution.py:124
  537.8 56.3 %copy-start.139 = (f32[768]{0:T(1024)}, f32[768]{0:T(1024)S(1)}, u32[]{:S(2)}) copy-start(f32[768]{0:T(1024)S(1)} %broadcast_multiply_fusion.2) | copy-start | bytes 9220
  558.3 429.0 %all-reduce.34.cloned.1.call-start = ((), (), s32[]{:S(2)}) async-start(), calls=%async_computation.6 | async-start | bytes 6291456 | tf_op jit(solution)/shard_map/psum | solution.py:438
  646.8 340.5 %reduce-scatter.5.cloned.1.call-start = ((), (), s32[]{:S(2)}) async-start(), calls=%async_computation.7 | async-start | bytes 4718592 | tf_op jit(solution)/shard_map/reduce_scatter | solution.py:440
  647.6 339.8 %reduce-scatter.9.cloned.1.call-start = ((), (), s32[]{:S(2)}) async-start(), calls=%async_computation.9 | async-start | bytes 6488064 | tf_op jit(solution)/shard_map/reduce_scatter | solution.py:440
  648.3 399.5 %reduce-scatter.7.cloned.1.call-start = ((), (), s32[]{:S(2)}) async-start(), calls=%async_computation.8 | async-start | bytes 12976128 | tf_op jit(solution)/shard_map/reduce_scatter | solution.py:440
  655.4 521.5 %all-reduce.36.cloned.1.call-start = ((), (), s32[]{:S(2)}) async-start(), calls=%async_computation.10 | async-start | bytes 6291456 | tf_op jit(solution)/shard_map/psum | solution.py:465
  662.5 233.4 %copy-start.9 = (bf16[768,4,128]{2,0,1:T(8,128)(2,1)S(1)}, bf16[768,4,128]{2,0,1:T(8,128)(2,1)}, u32[]{:S(2)}) copy-start(bf16[768,4,128]{2,0,1:T(8,128)(2,1)} %copy-done.8) | copy-start | bytes 2359300
  662.5 233.4 %copy-start.63 = (pred[12,64,64]{1,2,0:T(8,128)(4,1)S(1)}, pred[12,64,64]{1,2,0:T(8,128)(4,1)}, u32[]{:S(2)}) copy-start(pred[12,64,64]{1,2,0:T(8,128)(4,1)} %copy-done.62) | copy-start | bytes 147460
  662.5 233.4 %copy-start.65 = (f32[12,4,64]{2,1,0:T(4,128)S(1)}, f32[12,4,64]{2,1,0:T(4,128)}, u32[]{:S(2)}) copy-start(f32[12,4,64]{2,1,0:T(4,128)} %copy-done.64) | copy-start | bytes 36868
  982.4 65.4 %copy-start.105 = (f32[768,4,1]{0,1,2:T(4,128)S(1)}, f32[768,4,1]{0,1,2:T(4,128)}, u32[]{:S(2)}) copy-start(f32[768,4,1]{0,1,2:T(4,128)} %copy-done.104) | copy-start | bytes 36868
  982.4 65.4 %copy-start.131 = (f32[768,4,2]{0,1,2:T(4,128)S(1)}, f32[768,4,2]{0,1,2:T(4,128)}, u32[]{:S(2)}) copy-start(f32[768,4,2]{0,1,2:T(4,128)} %copy-done.130) | copy-start | bytes 73732
  982.4 65.4 %copy-start.147 = (f32[4]{0:T(128)S(1)}, f32[4]{0:T(128)}, u32[]{:S(2)}) copy-start(f32[4]{0:T(128)} %param.29) | copy-start | bytes 52
  982.4 65.4 %copy-start.149 = (f32[4]{0:T(128)S(1)}, f32[4]{0:T(128)}, u32[]{:S(2)}) copy-start(f32[4]{0:T(128)} %copy-done.148) | copy-start | bytes 52
  1073.4 11.7 collective-permute-start.2
  1090.5 16.8 %copy-start.115 = (f32[2048]{0:T(1024)S(1)}, f32[2048]{0:T(1024)}, u32[]{:S(2)}) copy-start(f32[2048]{0:T(1024)} %copy-done.114) | copy-start | bytes 24580
  1107.2 250.7 %reduce-scatter.11.cloned.1.call-start = ((), (), s32[]{:S(2)}) async-start(), calls=%async_computation.11 | async-start | bytes 14155776 | tf_op jit(solution)/shard_map/reduce_scatter | solution.py:501
  1234.3 10.2 copy-start.111
  1234.3 10.2 copy-start.135
  1234.3 10.2 copy-start.140
  (123 other events, 447.9 us)
Sparse Core Ops, SparseCore 0:
  313.4 95.6 all-reduce.29
  459.1 68.5 all-reduce.31
  646.9 66.9 all-reduce.33
  1107.3 69.6 all-reduce.35
Sparse Core Ops, SparseCore 1:
  461.6 49.3 all-gather.4
  558.4 73.0 all-gather.6
  650.9 86.7 reduce-scatter.4
  741.8 110.2 reduce-scatter.8
  856.0 191.7 reduce-scatter.6
  1125.2 232.6 reduce-scatter.10

commit v3 on v2

--- a/solution.py
+++ b/solution.py
@@ -296,6 +296,7 @@
         advance,
         initial,
         (value_part, state_part, query_b, query_keys, end_keys, from_start, from_start[..., -1]),
+        unroll=True,
     )
     emitted_all = jnp.moveaxis(emitted_all, 1, 2).reshape(
         length, head_count, payload_dimension + key_size

time: 1380 us -> 1310 us (0.949)
  matrix products: 565 us -> 444 us
  waiting for transfers between devices: 385 us -> 506 us
  local copies, waits for them, and re-layouts: 161 us -> 113 us
  other arithmetic: 133 us -> 108 us
    reduce_scatter x3, waiting for transfers between devices: 60.5 us -> 172 us  [shards(): lax.psum_scatter(part, 'seq', scatter_dimension=0, tiled=True)]
    dot_general x36, matrix products: 68.2 us -> 18.8 us  [advance(): jnp.einsum('htj,hjw->htw', mixing, new_values, precision=FAST_ARITHMETIC)]
    dot_general x36 -> x35, matrix products: 72.9 us -> 35.6 us  [advance(): jnp.einsum('htk,hkw->htw', state_rows, carried_state, precision=FAST_ARIT...]
    dynamic_update_slice x60 -> x0, local copies, waits for them, and re-layouts: 34.1 us -> none  [delta_local(): lax.scan(advance, initial, (value_part, state_part, query_b, query_keys,...]
    dot_general x36, matrix products: 62.1 us -> 34.3 us  [advance(): jnp.einsum('hjk,hjw->hkw', end_rows, new_values, precision=FAST_ARITHMETIC)]
    mul x36 -> x0, local copies, waits for them, and re-layouts: 24 us -> none  [the longest x24 16 us: advance(): block_decay[:, None, None] * carried_state]
    dot_general x36 -> x35, matrix products: 65.1 us -> 49.2 us  [advance(): jnp.einsum('htk,hkw->htw', query_rows, carried_state, precision=FAST_ARIT...]
    reduce_sum x12 -> x1, other arithmetic: 16.1 us -> 0.19 us  [advance(): block_decay[:, None, None] * carried_state]
  transfers between devices with their start and end apart: 13 -> 13, of which waited for: 6 -> 6; matrix products, arithmetic and copies ran while one was open for 38% -> 31% of each run, Pallas kernels for 3% -> 3%
where the time goes in v3:
time: 1310 us; the launch traced here: 1300 us
  waiting for transfers between devices  506 us (39%)
  matrix products  444 us (34%)
  local copies, waits for them, and re-layouts  113 us (9%)
  other arithmetic  108 us (8%)
  Pallas kernels  94.8 us (7%)
  between operations  20.9 us (2%)
    reduce_scatter x3, waiting for transfers between devices, shards(): lax.psum_scatter(part, 'seq', scatter_dimension=0, tiled=True)  172 us
    psum x1, waiting for transfers between devices, shards(): lax.psum(mixer_part.astype(jnp.bfloat16), 'tp').astype(jnp.float32)  108 us
    reduce_scatter x1, waiting for transfers between devices, shards(): lax.psum_scatter(grad_mix.astype(jnp.bfloat16), 'seq', scatter_dimension=...  102 us
    pallas_call x3, Pallas kernels, peer_gather(): pl.pallas_call(functools.partial(peer_gather_kernel, axis, count, mode),...  94.8 us
    psum x1, waiting for transfers between devices, shards(): lax.psum(ffn_in_part.astype(jnp.bfloat16), 'tp').astype(jnp.float32)  66.8 us
    dot_general x35, matrix products, advance(): jnp.einsum('htk,hkw->htw', query_rows, carried_state, precision=FAST_ARIT...  49.2 us
    unnamed x836, local copies, waits for them, and re-layouts  47.4 us
    dot_general x15, matrix products, unit_lower_inverse(): jnp.einsum('...ij,...jk->...ik', off, inverse, precision=EXACT_ARITHMETIC)  46.8 us
  transfers between devices with their start and end apart: 13, of which 6 were waited for; matrix products, arithmetic and copies ran while one was open for 31% of the time, Pallas kernels for 3%

profile of v3, /device:TPU:0, one launch (start us, length us, event | category | flops | bytes accessed | tf_op | source)
XLA Modules:
  0.0 1299.6 jit_solution(12165660362975010946)
XLA Ops:
  10.9 15.3 %fusion.441 = (bf16[768,4,768]{2,0,1:T(8,128)(2,1)S(1)}, f32[768,4,768]{2,0,1:T(8,128)}) fusion(bf16[2048,4,768]{2,1,0:T(4,128)(2,1)} %param.21, bf16[768,2048]{1,0:T(8,128)(2,1)S(1)} %copy-done.5, f32[2048]{0:T(1024)S(1)} %convert_element_type.253, f32[768]{0:T(1024)S(1)} %add_rsqrt_fusion.3), kind=kOutput, calls=%fused_computation.850 | convolution fusion | flops 9672327168 | bytes 29895680 | tf_op jit(solution)/shard_map/td,dhc->thc/dot_general | solution.py:339
  26.9 5.5 collective-permute-start.1
  58.6 6.3 fusion.36
  151.9 53.5 %shard_map.237 = bf16[8,4,128,384]{3,2,1,0:T(8,128)(2,1)} custom-call(bf16[4,128,384]{2,1,0:T(8,128)(2,1)} %pad_maximum_fusion.3.x_ref), custom_call_target="tpu_custom_call" | custom-call | tf_op jit(solution)/shard_map/pallas_call | solution.py:82
  220.7 4.3 multiply_reduce_fusion.8
  230.5 5.0 bitcast_convert_fusion.1
  236.2 108.2 %all-reduce.30.cloned.1.call-done = bf16[768,2048]{1,0:T(8,128)(2,1)} async-done(((bf16[768,2048]{1,0:T(8,128)(2,1)}), bf16[768,2048]{1,0:T(8,128)(2,1)}) %all-reduce.30.cloned.1.call-update) | async-done | bytes 3145744 | tf_op jit(solution)/shard_map/psum | solution.py:391
  347.6 15.9 %fusion.17 = f32[768,2,1408]{2,0,1:T(8,128)} fusion(bf16[2048,2,1408]{2,1,0:T(2,128)(2,1)} %param.29, bf16[768,2048]{1,0:T(8,128)(2,1)S(1)} %copy-done.66, bf16[768,2048]{1,0:T(8,128)(2,1)S(1)} %copy-done.5, f32[2048]{0:T(1024)S(1)} %convert_element_type.282, f32[768]{0:T(1024)S(1)} %add_rsqrt_fusion.2), kind=kOutput, calls=%fused_computation.20 | convolution fusion | flops 8867807232 | bytes 26487808 | tf_op jit(solution)/shard_map/td,dcf->tcf/dot_general | solution.py:395
  363.4 11.0 multiply_bitcast_fusion
  374.5 17.0 %bitcast_convert_fusion = (bf16[768,2048]{1,0:T(8,128)(2,1)}, f32[768,2048,1]{1,0,2:T(8,128)}) fusion(bf16[2048,2,1408]{2,1,0:T(2,128)(2,1)} %param.29, f32[768,1,1408]{2,0,1:T(8,128)} %get-tuple-element.311, f32[768,1,1408]{2,0,1:T(8,128)} %get-tuple-element.310), kind=kOutput, calls=%fused_computation.50 | convolution fusion | flops 8864268288 | bytes 29622272 | tf_op jit(solution)/shard_map/tcf,dcf->td/dot_general | solution.py:405
  393.4 66.8 %all-reduce.32.cloned.1.call-done = bf16[768,2048]{1,0:T(8,128)(2,1)} async-done(((bf16[768,2048]{1,0:T(8,128)(2,1)}), bf16[768,2048]{1,0:T(8,128)(2,1)}) %all-reduce.32.cloned.1.call-update) | async-done | bytes 3145744 | tf_op jit(solution)/shard_map/psum | solution.py:406
  460.2 6.8 fusion.35
  468.5 11.4 multiply_reduce_fusion.6
  479.9 4.0 add_add_fusion
  483.9 4.7 fusion.81
  488.8 9.7 fusion.23
  498.5 8.9 convolution_convert_fusion.4
  507.4 16.9 %convolution_convert_fusion = bf16[2048,2,1408]{2,0,1:T(8,128)(2,1)} fusion(f32[768,1,1408]{2,0,1:T(8,128)} %get-tuple-element.311, f32[768,1,1408]{2,0,1:T(8,128)} %get-tuple-element.310, bf16[768,2048]{1,0:T(8,128)(2,1)} %all-reduce.30.cloned.1.call-done, bf16[768,2048]{1,0:T(8,128)(2,1)S(1)} %copy-done.5, f32[2048]{0:T(1024)S(1)} %convert_element_type.282, ...), kind=kOutput, calls=%fused_computation.17 | convolution fusion | flops 8877899776 | bytes 26487808 | tf_op jit(solution)/shard_map/td,tcf->dcf/dot_general | solution.py:402
  524.4 11.7 convolution_convert_fusion.3
  539.2 22.5 %all-gather.7.cloned.1.call-done = f32[32,128,256]{2,1,0:T(8,128)} async-done(((f32[4,128,256]{2,1,0:T(8,128)}), f32[32,128,256]{2,1,0:T(8,128)}) %all-gather.7.cloned.1.call-update) | async-done | bytes 4194320 | tf_op jit(solution)/shard_map/all_gather | solution.py:124
  561.7 4.6 rev.7
  566.4 11.2 while.27
  620.8 5.3 fusion.204
  710.8 5.6 fusion.80
  744.3 3.9 fusion.446
  756.9 3.9 fusion.447
  763.6 3.8 fusion.84
  770.2 4.2 fusion.207
  774.5 8.4 multiply_select_fusion
  784.9 4.1 bitcast_multiply_fusion.1
  806.2 172.5 %reduce-scatter.7.cloned.1.call-done = bf16[256,2,1408]{2,0,1:T(8,128)(2,1)} async-done(((bf16[2048,2,1408]{2,0,1:T(8,128)(2,1)}), bf16[256,2,1408]{2,0,1:T(8,128)(2,1)}) %reduce-scatter.7.cloned.1.call-update) | async-done | bytes 1441808 | tf_op jit(solution)/shard_map/reduce_scatter | solution.py:441
  978.7 3.9 multiply_reduce_fusion.10
  983.8 4.9 add_add_fusion.2
  988.8 7.9 multiply_reduce_fusion.3
  996.7 5.9 multiply_multiply_fusion.2
  1009.1 6.9 pad_add_fusion
  1019.7 17.8 %fusion.442 = (bf16[768,2048]{1,0:T(8,128)(2,1)}, f32[768,2048]{1,0:T(8,128)}) fusion(f32[768,2048,1]{1,0,2:T(8,128)} %fusion.389, bf16[2048,4,768]{2,1,0:T(4,128)(2,1)} %param.21, bf16[768,4,256]{2,0,1:T(8,128)(2,1)} %get-tuple-element.309, bf16[768,4,512]{2,0,1:T(8,128)(2,1)S(1)} %fusion.34), kind=kOutput, calls=%fused_computation.851 | convolution fusion | flops 9676259328 | bytes 33030144 | tf_op jit(solution)/shard_map/thc,dhc->td/dot_general | solution.py:463
  1039.5 15.6 %convolution_convert_fusion.2 = bf16[2048,4,768]{2,0,1:T(8,128)(2,1)} fusion(bf16[768,4,256]{2,0,1:T(8,128)(2,1)} %get-tuple-element.309, bf16[768,4,512]{2,0,1:T(8,128)(2,1)} %copy-done.239, bf16[768,2048]{1,0:T(8,128)(2,1)S(1)} %copy-done.6, f32[2048]{0:T(1024)S(1)} %copy-done.293, f32[768]{0:T(1024)S(1)} %copy-done.313), kind=kOutput, calls=%fused_computation.32 | convolution fusion | flops 9685696512 | bytes 20458496 | tf_op jit(solution)/shard_map/td,thc->dhc/dot_general | solution.py:459
  1059.2 5.5 reshape.1395
  1064.8 4.4 copy.284
  1074.2 33.3 %all-reduce.36.cloned.1.call-done = bf16[768,2048]{1,0:T(8,128)(2,1)} async-done(((bf16[768,2048]{1,0:T(8,128)(2,1)}), bf16[768,2048]{1,0:T(8,128)(2,1)}) %all-reduce.36.cloned.1.call-update) | async-done | bytes 3145744 | tf_op jit(solution)/shard_map/psum | solution.py:466
  1107.4 4.9 fusion.30
  1113.1 36.2 %shard_map.238 = f32[8,232,128]{2,1,0:T(8,128)} custom-call(f32[232,128]{1,0:T(8,128)} %pad_bitcast_fusion.x_ref), custom_call_target="tpu_custom_call" | custom-call | tf_op jit(solution)/shard_map/pallas_call | solution.py:82
  1151.1 6.8 reshape.1398
  1162.3 5.0 shard_map.239
  1174.9 10.8 fusion.29
  1185.7 102.2 %reduce-scatter.11.cloned.1.call-done = bf16[256,4,768]{2,0,1:T(8,128)(2,1)} async-done(((bf16[2048,4,768]{2,0,1:T(8,128)(2,1)}), bf16[256,4,768]{2,0,1:T(8,128)(2,1)}) %reduce-scatter.11.cloned.1.call-update) | async-done | bytes 1572880 | tf_op jit(solution)/shard_map/reduce_scatter | solution.py:502
  1288.0 4.3 copy.281
  (1200 shorter events, 380.3 us)
Async XLA Ops:
  8.0 36.0 %copy-start = (bf16[2048,4,2]{0,2,1:T(2,128)(2,1)S(1)}, bf16[2048,4,2]{0,2,1:T(2,128)(2,1)}, u32[]{:S(2)}) copy-start(bf16[2048,4,2]{0,2,1:T(2,128)(2,1)} %param.22) | copy-start | bytes 98308
  8.0 336.3 %all-reduce.30.cloned.1.call-start = ((), (), s32[]{:S(2)}) async-start(), calls=%async_computation.4 | async-start | bytes 6291456 | tf_op jit(solution)/shard_map/psum | solution.py:391
  10.8 33.1 %copy-start.312 = (f32[768]{0:T(1024)}, f32[768]{0:T(1024)S(1)}, u32[]{:S(2)}) copy-start(f32[768]{0:T(1024)S(1)} %add_rsqrt_fusion.3) | copy-start | bytes 9220
  10.9 33.1 %copy-start.292 = (f32[2048]{0:T(1024)}, f32[2048]{0:T(1024)S(1)}, u32[]{:S(2)}) copy-start(f32[2048]{0:T(1024)S(1)} %convert_element_type.253) | copy-start | bytes 24580
  10.9 21.4 %copy-start.353 = (s32[768]{0:T(1024)S(1)}, s32[768]{0:T(1024)}, u32[]{:S(2)}) copy-start(s32[768]{0:T(1024)} %param.19) | copy-start | bytes 9220
  26.9 28.8 %collective-permute-start.1 = (bf16[3,4,512]{2,0,1:T(4,128)(2,1)}, bf16[3,4,512]{2,0,1:T(4,128)(2,1)}, u32[]{:S(2)}, u32[]{:S(2)}) collective-permute-start(bf16[3,4,512]{2,0,1:T(4,128)(2,1)} %slice.644), channel_id=1, source_target_pairs={{0,4},{4,8},{8,12},{12,16},{16,20},{20,24},{24,28},{1,5},{5,9},{9,... | collective-permute-start | bytes 36872 | tf_op jit(solution)/shard_map/ppermute | solution.py:24
  32.9 17.2 %collective-permute-start = (bf16[3]{0:T(256)(128)(2,1)}, bf16[3]{0:T(256)(128)(2,1)}, u32[]{:S(2)}, u32[]{:S(2)}) collective-permute-start(bf16[3]{0:T(256)(128)(2,1)} %slice.505), channel_id=1, source_target_pairs={{0,4},{4,8},{8,12},{12,16},{16,20},{20,24},{24,28},{1,5},{5,9},{9,... | collective-permute-start | bytes 26 | tf_op jit(solution)/shard_map/ppermute | solution.py:24
  39.0 36.7 %copy-start.244 = (f32[64,64]{1,0:T(8,128)}, f32[64,64]{1,0:T(8,128)S(1)}, u32[]{:S(2)}) copy-start(f32[64,64]{1,0:T(8,128)S(1)} %fusion.386) | copy-start | bytes 49156
  46.8 22.5 %copy-start.210 = (f32[12,4,64]{2,1,0:T(4,128)}, f32[12,4,64]{2,1,0:T(4,128)S(1)}, u32[]{:S(2)}) copy-start(f32[12,4,64]{2,1,0:T(4,128)S(1)} %copy.191) | copy-start | bytes 36868
  48.3 46.0 %copy-start.242 = (f32[12,4,64]{2,1,0:T(4,128)}, f32[12,4,64]{2,1,0:T(4,128)S(1)}, u32[]{:S(2)}) copy-start(f32[12,4,64]{2,1,0:T(4,128)S(1)} %copy.194) | copy-start | bytes 36868
  50.0 23.9 %copy-start.266 = (f32[64,64]{1,0:T(8,128)}, f32[64,64]{1,0:T(8,128)S(1)}, u32[]{:S(2)}) copy-start(f32[64,64]{1,0:T(8,128)S(1)} %get-tuple-element.366) | copy-start | bytes 49156
  50.0 25.7 %copy-start.246 = (f32[64,64]{1,0:T(8,128)}, f32[64,64]{1,0:T(8,128)S(1)}, u32[]{:S(2)}) copy-start(f32[64,64]{1,0:T(8,128)S(1)} %get-tuple-element.367) | copy-start | bytes 49156
  50.0 27.7 %copy-start.259 = (f32[64,64]{1,0:T(8,128)}, f32[64,64]{1,0:T(8,128)S(1)}, u32[]{:S(2)}) copy-start(f32[64,64]{1,0:T(8,128)S(1)} %get-tuple-element.365) | copy-start | bytes 49156
  50.1 31.4 %copy-start.257 = (f32[64,64]{1,0:T(8,128)}, f32[64,64]{1,0:T(8,128)S(1)}, u32[]{:S(2)}) copy-start(f32[64,64]{1,0:T(8,128)S(1)} %get-tuple-element.364) | copy-start | bytes 49156
  50.1 35.1 %copy-start.255 = (f32[64,64]{1,0:T(8,128)}, f32[64,64]{1,0:T(8,128)S(1)}, u32[]{:S(2)}) copy-start(f32[64,64]{1,0:T(8,128)S(1)} %get-tuple-element.363) | copy-start | bytes 49156
  50.1 39.2 %copy-start.253 = (f32[64,64]{1,0:T(8,128)}, f32[64,64]{1,0:T(8,128)S(1)}, u32[]{:S(2)}) copy-start(f32[64,64]{1,0:T(8,128)S(1)} %get-tuple-element.362) | copy-start | bytes 49156
  54.7 14.6 %copy-start.208 = (pred[12,64,64]{2,1,0:T(8,128)(4,1)}, pred[12,64,64]{2,1,0:T(8,128)(4,1)S(1)}, u32[]{:S(2)}) copy-start(pred[12,64,64]{2,1,0:T(8,128)(4,1)S(1)} %get-tuple-element.351) | copy-start | bytes 147460
  55.5 37.4 %copy-start.263 = (f32[12,4,64]{2,1,0:T(4,128)}, f32[12,4,64]{2,1,0:T(4,128)S(1)}, u32[]{:S(2)}) copy-start(f32[12,4,64]{2,1,0:T(4,128)S(1)} %copy.197) | copy-start | bytes 36868
  55.6 41.1 %copy-start.269 = (f32[12,4,64]{2,1,0:T(4,128)}, f32[12,4,64]{2,1,0:T(4,128)S(1)}, u32[]{:S(2)}) copy-start(f32[12,4,64]{2,1,0:T(4,128)S(1)} %copy.198) | copy-start | bytes 36868
  68.6 28.1 %copy-start.7 = (bf16[768,4,128]{2,0,1:T(8,128)(2,1)}, bf16[768,4,128]{2,0,1:T(8,128)(2,1)S(1)}, u32[]{:S(2)}) copy-start(bf16[768,4,128]{2,0,1:T(8,128)(2,1)S(1)} %get-tuple-element.322) | copy-start | bytes 2359300
  69.3 36.3 %copy-start.96 = (f32[12,64,4,128]{3,1,2,0:T(8,128)}, f32[12,64,4,128]{3,1,2,0:T(8,128)S(1)}, u32[]{:S(2)}) copy-start(f32[12,64,4,128]{3,1,2,0:T(8,128)S(1)} %copy.451) | copy-start | bytes 4718596
  73.9 15.4 %copy-start.2 = (f32[12,4,64,64]{3,2,1,0:T(8,128)}, f32[12,4,64,64]{3,2,1,0:T(8,128)S(1)}, u32[]{:S(2)}) copy-start(f32[12,4,64,64]{3,2,1,0:T(8,128)S(1)} %get-tuple-element.326) | copy-start | bytes 2359300
  235.5 224.6 %all-reduce.32.cloned.1.call-start = ((), (), s32[]{:S(2)}) async-start(), calls=%async_computation.5 | async-start | bytes 6291456 | tf_op jit(solution)/shard_map/psum | solution.py:406
  236.2 288.2 %copy-start.288 = (f32[2048]{0:T(1024)}, f32[2048]{0:T(1024)S(1)}, u32[]{:S(2)}) copy-start(f32[2048]{0:T(1024)S(1)} %convert_element_type.282) | copy-start | bytes 24580
  344.4 19.0 %slice-start.10 = ((s8[5767168]{0:T(1024)(128)(4,1)}), s8[4194304]{0:T(1024)(128)(4,1)S(1)}, s32[]{:S(2)}) async-start(s8[5767168]{0:T(1024)(128)(4,1)} %bitcast.1271), calls=%async_computation.24 | async-start | bytes 8388608
  347.5 176.9 %copy-start.314 = (f32[768]{0:T(1024)}, f32[768]{0:T(1024)S(1)}, u32[]{:S(2)}) copy-start(f32[768]{0:T(1024)S(1)} %add_rsqrt_fusion.2) | copy-start | bytes 9220
  347.5 15.9 %copy-start.237 = (bf16[768,2048]{1,0:T(8,128)(2,1)S(1)}, bf16[768,2048]{1,0:T(8,128)(2,1)}, u32[]{:S(2)}) copy-start(bf16[768,2048]{1,0:T(8,128)(2,1)} %param.31) | copy-start | bytes 9437188
  347.5 15.9 %slice-start.11 = ((s8[5767168]{0:T(1024)(128)(4,1)}), s8[1572864]{0:T(1024)(128)(4,1)S(1)}, s32[]{:S(2)}) async-start(s8[5767168]{0:T(1024)(128)(4,1)} %bitcast.1271), calls=%async_computation.25 | async-start | bytes 3145728
  391.5 144.6 %all-gather.5.cloned.1.call-start = ((), (), s32[]{:S(2)}) async-start(), calls=%async_computation.12 | async-start | bytes 2359296 | tf_op jit(solution)/shard_map/all_gather | solution.py:124
  393.3 168.4 %all-gather.7.cloned.1.call-start = ((), (), s32[]{:S(2)}) async-start(), calls=%async_computation.13 | async-start | bytes 4718592 | tf_op jit(solution)/shard_map/all_gather | solution.py:124
  468.5 55.9 %copy-start.350 = (f32[768]{0:T(1024)}, f32[768]{0:T(1024)S(1)}, u32[]{:S(2)}) copy-start(f32[768]{0:T(1024)S(1)} %broadcast_multiply_fusion.2) | copy-start | bytes 9220
  488.6 317.6 %all-reduce.34.cloned.1.call-start = ((), (), s32[]{:S(2)}) async-start(), calls=%async_computation.6 | async-start | bytes 6291456 | tf_op jit(solution)/shard_map/psum | solution.py:439
  577.6 228.6 %reduce-scatter.5.cloned.1.call-start = ((), (), s32[]{:S(2)}) async-start(), calls=%async_computation.7 | async-start | bytes 4718592 | tf_op jit(solution)/shard_map/reduce_scatter | solution.py:441
  578.2 228.0 %reduce-scatter.9.cloned.1.call-start = ((), (), s32[]{:S(2)}) async-start(), calls=%async_computation.9 | async-start | bytes 6488064 | tf_op jit(solution)/shard_map/reduce_scatter | solution.py:441
  585.1 18.7 %copy-start.4 = (f32[12,64,4,384]{3,1,2,0:T(8,128)}, f32[12,64,4,384]{3,1,2,0:T(8,128)S(1)}, u32[]{:S(2)}) copy-start(f32[12,64,4,384]{3,1,2,0:T(8,128)S(1)} %copy.450) | copy-start | bytes 14155780
  605.3 373.4 %reduce-scatter.7.cloned.1.call-start = ((), (), s32[]{:S(2)}) async-start(), calls=%async_computation.8 | async-start | bytes 12976128 | tf_op jit(solution)/shard_map/reduce_scatter | solution.py:441
  652.7 454.8 %all-reduce.36.cloned.1.call-start = ((), (), s32[]{:S(2)}) async-start(), calls=%async_computation.10 | async-start | bytes 6291456 | tf_op jit(solution)/shard_map/psum | solution.py:466
  681.7 12.0 copy-start.170
  801.5 182.3 %copy-start.280 = (f32[768,4]{0,1:T(4,128)S(1)}, f32[768,4]{0,1:T(4,128)}, u32[]{:S(2)}) copy-start(f32[768,4]{0,1:T(4,128)} %copy-done.279) | copy-start | bytes 36868
  801.5 187.2 %slice-start.6 = ((s8[6291456]{0:T(1024)(128)(4,1)}), s8[2097152]{0:T(1024)(128)(4,1)S(1)}, s32[]{:S(2)}) async-start(s8[6291456]{0:T(1024)(128)(4,1)} %bitcast.1154), calls=%async_computation.20 | async-start | bytes 4194304
  1003.6 12.4 collective-permute-start.2
  1019.7 17.9 %copy-start.239 = (bf16[768,4,512]{2,0,1:T(8,128)(2,1)}, bf16[768,4,512]{2,0,1:T(8,128)(2,1)S(1)}, u32[]{:S(2)}) copy-start(bf16[768,4,512]{2,0,1:T(8,128)(2,1)S(1)} %fusion.34) | copy-start | bytes 9437188
  1019.7 18.3 %copy-start.293 = (f32[2048]{0:T(1024)S(1)}, f32[2048]{0:T(1024)}, u32[]{:S(2)}) copy-start(f32[2048]{0:T(1024)} %copy-done.292) | copy-start | bytes 24580
  1019.7 18.3 %copy-start.313 = (f32[768]{0:T(1024)S(1)}, f32[768]{0:T(1024)}, u32[]{:S(2)}) copy-start(f32[768]{0:T(1024)} %copy-done.312) | copy-start | bytes 9220
  1037.6 250.4 %reduce-scatter.11.cloned.1.call-start = ((), (), s32[]{:S(2)}) async-start(), calls=%async_computation.11 | async-start | bytes 14155776 | tf_op jit(solution)/shard_map/reduce_scatter | solution.py:502
  1159.8 15.0 %copy-start.289 = (f32[2048]{0:T(1024)S(1)}, f32[2048]{0:T(1024)}, u32[]{:S(2)}) copy-start(f32[2048]{0:T(1024)} %copy-done.288) | copy-start | bytes 24580
  1159.8 15.0 %copy-start.315 = (f32[768]{0:T(1024)S(1)}, f32[768]{0:T(1024)}, u32[]{:S(2)}) copy-start(f32[768]{0:T(1024)} %copy-done.314) | copy-start | bytes 9220
  1159.8 15.0 %copy-start.351 = (f32[768]{0:T(1024)S(1)}, f32[768]{0:T(1024)}, u32[]{:S(2)}) copy-start(f32[768]{0:T(1024)} %copy-done.350) | copy-start | bytes 9220
  (374 other events, 1009.3 us)
Sparse Core Ops, SparseCore 0:
  235.6 108.6 all-reduce.29
  391.6 68.5 all-reduce.31
  577.7 66.8 all-reduce.33
  1037.7 69.6 all-reduce.35
Sparse Core Ops, SparseCore 1:
  394.1 49.3 all-gather.4
  488.7 73.0 all-gather.6
  581.7 86.7 reduce-scatter.4
  672.6 110.2 reduce-scatter.8
  786.9 191.7 reduce-scatter.6
  1055.2 232.7 reduce-scatter.10

commit v4 on v3

--- a/solution.py
+++ b/solution.py
@@ -121,7 +121,9 @@
 
 def carried_in_2(value, axis, join, neutral):
     count, mine = (lax.axis_size(axis), lax.axis_index(axis))
-    pieces = jax.tree.map(lambda part: lax.all_gather(part, axis), value)
+    pieces = jax.tree.map(
+        lambda part: lax.all_gather(part.astype(jnp.bfloat16), axis).astype(part.dtype), value
+    )
     pieces = jax.tree.map(lambda part: part[::-1], pieces)
     mine = count - 1 - mine
     running = jax.tree.map(
@@ -443,11 +445,7 @@
     delta_grads = delta_pull(
         (core_output_grad, branch_derivatives, state_gradient, transfer_gradient)
     )
-    ffn_sum, early_sums, delta_grads = lax.optimization_barrier(
-        (ffn_sum, early_sums, delta_grads)
-    )
     grad_query, grad_keys, grad_values, grad_strength, grad_decay = delta_grads
-    layer_out = (residual + ffn_sum.astype(jnp.float32)).astype(jnp.bfloat16)
     grad_rate_rows, a_log_grad, dt_bias_grad = rate_pull((grad_strength, grad_decay))
     grad_padded, conv_grad = conv_pull((grad_query, grad_keys, grad_values))
     back_rows = shifted(grad_padded[:rim_rows], "seq", -1)
@@ -455,6 +453,8 @@
         [jnp.zeros((length - rim_rows,) + back_rows.shape[1:], jnp.float32), back_rows]
     )
     grad_mixed = jnp.concatenate([grad_conv_rows, grad_gate_rows], axis=-1).astype(jnp.bfloat16)
+    ffn_sum, early_sums, grad_mixed = lax.optimization_barrier((ffn_sum, early_sums, grad_mixed))
+    layer_out = (residual + ffn_sum.astype(jnp.float32)).astype(jnp.bfloat16)
     grad_rates = grad_rate_rows.astype(jnp.bfloat16)
     grad_mix = jnp.einsum("td,thc->dhc", normed_one, grad_mixed, preferred_element_type=jnp.float32)
     grad_rate = jnp.einsum(

time: 1310 us -> 1260 us (0.962)
  waiting for transfers between devices: 506 us -> 395 us
  matrix products: 444 us -> 494 us
    reduce_scatter x3, waiting for transfers between devices: 172 us -> 97.3 us  [shards(): lax.psum_scatter(part, 'seq', scatter_dimension=0, tiled=True)]
    psum x1, waiting for transfers between devices: 66.8 us -> 30.3 us  [shards(): lax.psum(ffn_in_part.astype(jnp.bfloat16), 'tp').astype(jnp.float32)]
    dot_general x36, matrix products: 34.3 us -> 49.8 us  [advance(): jnp.einsum('hjk,hjw->hkw', end_rows, new_values, precision=FAST_ARITHMETIC)]
    dot_general x36, matrix products: 18.8 us -> 32.9 us  [advance(): jnp.einsum('htj,hjw->htw', mixing, new_values, precision=FAST_ARITHMETIC)]
    unnamed x836 -> x826, local copies, waits for them, and re-layouts: 47.4 us -> 52.9 us
  transfers between devices with their start and end apart: 13 -> 13, of which waited for: 6 -> 6; matrix products, arithmetic and copies ran while one was open for 31% -> 40% of each run, Pallas kernels for 3% -> 3%
where the time goes in v4:
time: 1260 us; the launch traced here: 1250 us
  matrix products  494 us (39%)
  waiting for transfers between devices  395 us (31%)
  local copies, waits for them, and re-layouts  124 us (10%)
  other arithmetic  107 us (8%)
  Pallas kernels  94.5 us (8%)
  between operations  20.3 us (2%)
  starting transfers between devices  12.8 us (1%)
    psum x1, waiting for transfers between devices, shards(): lax.psum(mixer_part.astype(jnp.bfloat16), 'tp').astype(jnp.float32)  105 us
    reduce_scatter x1, waiting for transfers between devices, shards(): lax.psum_scatter(grad_mix.astype(jnp.bfloat16), 'seq', scatter_dimension=...  101 us
    reduce_scatter x3, waiting for transfers between devices, shards(): lax.psum_scatter(part, 'seq', scatter_dimension=0, tiled=True)  97.3 us
    pallas_call x3, Pallas kernels, peer_gather(): pl.pallas_call(functools.partial(peer_gather_kernel, axis, count, mode),...  94.5 us
    dot_general x35, matrix products, advance(): jnp.einsum('htk,hkw->htw', query_rows, carried_state, precision=FAST_ARIT...  60.6 us
    unnamed x826, local copies, waits for them, and re-layouts  52.9 us
    dot_general x36, matrix products, advance(): jnp.einsum('hjk,hjw->hkw', end_rows, new_values, precision=FAST_ARITHMETIC)  49.8 us
    dot_general x35, matrix products, advance(): jnp.einsum('htk,hkw->htw', state_rows, carried_state, precision=FAST_ARIT...  47.2 us
  transfers between devices with their start and end apart: 13, of which 6 were waited for; matrix products, arithmetic and copies ran while one was open for 40% of the time, Pallas kernels for 3%

profile of v4, /device:TPU:0, one launch (start us, length us, event | category | flops | bytes accessed | tf_op | source)
XLA Modules:
  0.0 1248.2 jit_solution(12923488317229181204)
XLA Ops:
  10.9 15.5 %fusion.444 = (bf16[768,4,768]{2,0,1:T(8,128)(2,1)S(1)}, f32[768,4,768]{2,0,1:T(8,128)}) fusion(bf16[2048,4,768]{2,1,0:T(4,128)(2,1)} %param.21, bf16[768,2048]{1,0:T(8,128)(2,1)S(1)} %copy-done.5, f32[2048]{0:T(1024)S(1)} %convert_element_type.266, f32[768]{0:T(1024)S(1)} %add_rsqrt_fusion.3), kind=kOutput, calls=%fused_computation.856 | convolution fusion | flops 9672327168 | bytes 29895680 | tf_op jit(solution)/shard_map/td,dhc->thc/dot_general | solution.py:341
  27.0 5.5 collective-permute-start.1
  33.1 3.9 collective-permute-start
  61.8 6.4 fusion.36
  156.9 53.5 %shard_map.237 = bf16[8,4,128,384]{3,2,1,0:T(8,128)(2,1)} custom-call(bf16[4,128,384]{2,1,0:T(8,128)(2,1)} %pad_maximum_fusion.1.x_ref), custom_call_target="tpu_custom_call" | custom-call | tf_op jit(solution)/shard_map/pallas_call | solution.py:82
  225.7 4.3 multiply_reduce_fusion.8
  235.5 5.0 bitcast_convert_fusion.1
  243.7 105.4 %all-reduce.30.cloned.1.call-done = bf16[768,2048]{1,0:T(8,128)(2,1)} async-done(((bf16[768,2048]{1,0:T(8,128)(2,1)}), bf16[768,2048]{1,0:T(8,128)(2,1)}) %all-reduce.30.cloned.1.call-update) | async-done | bytes 3145744 | tf_op jit(solution)/shard_map/psum | solution.py:393
  352.4 15.6 %fusion.17 = f32[768,2,1408]{2,0,1:T(8,128)} fusion(bf16[2048,2,1408]{2,1,0:T(2,128)(2,1)} %param.29, bf16[768,2048]{1,0:T(8,128)(2,1)S(1)} %copy-done.64, bf16[768,2048]{1,0:T(8,128)(2,1)S(1)} %copy-done.5, f32[2048]{0:T(1024)S(1)} %convert_element_type.295, f32[768]{0:T(1024)S(1)} %add_rsqrt_fusion.2), kind=kOutput, calls=%fused_computation.20 | convolution fusion | flops 8867807232 | bytes 26487808 | tf_op jit(solution)/shard_map/td,dcf->tcf/dot_general | solution.py:397
  367.9 11.0 multiply_bitcast_fusion
  378.9 17.1 %bitcast_convert_fusion = (bf16[768,2048]{1,0:T(8,128)(2,1)}, f32[768,2048,1]{1,0,2:T(8,128)}) fusion(bf16[2048,2,1408]{2,1,0:T(2,128)(2,1)} %param.29, f32[768,1,1408]{2,0,1:T(8,128)} %get-tuple-element.303, f32[768,1,1408]{2,0,1:T(8,128)} %get-tuple-element.302), kind=kOutput, calls=%fused_computation.50 | convolution fusion | flops 8864268288 | bytes 29622272 | tf_op jit(solution)/shard_map/tcf,dcf->td/dot_general | solution.py:407
  396.1 16.9 %convolution_convert_fusion = bf16[2048,2,1408]{2,0,1:T(8,128)(2,1)} fusion(f32[768,1,1408]{2,0,1:T(8,128)} %get-tuple-element.303, f32[768,1,1408]{2,0,1:T(8,128)} %get-tuple-element.302, bf16[768,2048]{1,0:T(8,128)(2,1)} %all-reduce.30.cloned.1.call-done, bf16[768,2048]{1,0:T(8,128)(2,1)S(1)} %copy-done.5, f32[2048]{0:T(1024)S(1)} %convert_element_type.295, ...), kind=kOutput, calls=%fused_computation.17 | convolution fusion | flops 8877899776 | bytes 26487808 | tf_op jit(solution)/shard_map/td,tcf->dcf/dot_general | solution.py:404
  413.1 9.7 fusion.23
  422.8 9.0 convolution_convert_fusion.4
  434.5 30.3 %all-reduce.32.cloned.1.call-done = bf16[768,2048]{1,0:T(8,128)(2,1)} async-done(((bf16[768,2048]{1,0:T(8,128)(2,1)}), bf16[768,2048]{1,0:T(8,128)(2,1)}) %all-reduce.32.cloned.1.call-update) | async-done | bytes 3145744 | tf_op jit(solution)/shard_map/psum | solution.py:408
  464.8 6.8 fusion.35
  473.1 11.4 multiply_reduce_fusion.6
  484.5 4.0 add_add_fusion
  488.5 4.6 fusion.125
  507.2 6.8 convolution_convert_fusion.3
  513.9 28.6 %all-gather.7.cloned.1.call-done = bf16[32,128,256]{2,1,0:T(8,128)(2,1)} async-done(((bf16[4,128,256]{2,1,0:T(8,128)(2,1)}), bf16[32,128,256]{2,1,0:T(8,128)(2,1)}) %all-gather.7.cloned.1.call-update) | async-done | bytes 2097168 | tf_op jit(solution)/shard_map/all_gather | solution.py:125
  542.6 4.1 rev.7
  546.7 11.2 while.27
  607.0 5.2 fusion.211
  724.3 5.3 fusion.72
  743.0 5.3 fusion.83
  787.7 4.0 fusion.450
  801.0 4.2 fusion.213
  805.3 8.5 multiply_select_fusion
  815.9 4.4 fusion.38
  827.0 4.6 add_bitcast_fusion.1
  840.2 7.9 multiply_reduce_fusion.3
  848.1 6.0 multiply_multiply_fusion.2
  860.6 6.9 pad_add_fusion
  867.5 3.9 fusion.34
  873.8 97.3 %reduce-scatter.7.cloned.1.call-done = bf16[256,2,1408]{2,0,1:T(8,128)(2,1)} async-done(((bf16[2048,2,1408]{2,0,1:T(8,128)(2,1)}), bf16[256,2,1408]{2,0,1:T(8,128)(2,1)}) %reduce-scatter.7.cloned.1.call-update) | async-done | bytes 1441808 | tf_op jit(solution)/shard_map/reduce_scatter | solution.py:443
  971.2 17.7 %fusion.445 = (bf16[768,2048]{1,0:T(8,128)(2,1)}, f32[768,2048]{1,0:T(8,128)}) fusion(f32[768,2048,1]{1,0,2:T(8,128)} %fusion.397, bf16[768,4,768]{2,0,1:T(8,128)(2,1)} %pad_maximum_fusion, bf16[2048,4,768]{2,1,0:T(4,128)(2,1)} %param.21), kind=kOutput, calls=%fused_computation.857 | convolution fusion | flops 9666822144 | bytes 33030144 | tf_op jit(solution)/shard_map/thc,dhc->td/dot_general | solution.py:463
  990.8 15.2 %convolution_convert_fusion.2 = bf16[2048,4,768]{2,0,1:T(8,128)(2,1)} fusion(bf16[768,4,768]{2,0,1:T(8,128)(2,1)} %pad_maximum_fusion, bf16[768,2048]{1,0:T(8,128)(2,1)S(1)} %copy-done.6, f32[2048]{0:T(1024)S(1)} %copy-done.289, f32[768]{0:T(1024)S(1)} %copy-done.307), kind=kOutput, calls=%fused_computation.32 | convolution fusion | flops 9676259328 | bytes 20458496 | tf_op jit(solution)/shard_map/td,thc->dhc/dot_general | solution.py:459
  1010.0 5.5 reshape.1435
  1015.8 4.4 copy.284
  1025.1 31.5 %all-reduce.36.cloned.1.call-done = bf16[768,2048]{1,0:T(8,128)(2,1)} async-done(((bf16[768,2048]{1,0:T(8,128)(2,1)}), bf16[768,2048]{1,0:T(8,128)(2,1)}) %all-reduce.36.cloned.1.call-update) | async-done | bytes 3145744 | tf_op jit(solution)/shard_map/psum | solution.py:466
  1056.7 5.0 fusion.30
  1062.5 36.0 %shard_map.238 = f32[8,232,128]{2,1,0:T(8,128)} custom-call(f32[232,128]{1,0:T(8,128)} %pad_bitcast_fusion.x_ref), custom_call_target="tpu_custom_call" | custom-call | tf_op jit(solution)/shard_map/pallas_call | solution.py:82
  1100.4 6.7 reshape.1438
  1111.4 5.0 shard_map.239
  1124.0 11.1 fusion.29
  1135.1 101.5 %reduce-scatter.11.cloned.1.call-done = bf16[256,4,768]{2,0,1:T(8,128)(2,1)} async-done(((bf16[2048,4,768]{2,0,1:T(8,128)(2,1)}), bf16[256,4,768]{2,0,1:T(8,128)(2,1)}) %reduce-scatter.11.cloned.1.call-update) | async-done | bytes 1572880 | tf_op jit(solution)/shard_map/reduce_scatter | solution.py:502
  1236.5 4.3 copy.281
  (1195 shorter events, 444.7 us)
Async XLA Ops:
  8.0 36.5 %copy-start = (bf16[2048,4,2]{0,2,1:T(2,128)(2,1)S(1)}, bf16[2048,4,2]{0,2,1:T(2,128)(2,1)}, u32[]{:S(2)}) copy-start(bf16[2048,4,2]{0,2,1:T(2,128)(2,1)} %param.22) | copy-start | bytes 98308
  8.0 341.1 %all-reduce.30.cloned.1.call-start = ((), (), s32[]{:S(2)}) async-start(), calls=%async_computation.4 | async-start | bytes 6291456 | tf_op jit(solution)/shard_map/psum | solution.py:393
  10.8 33.7 %copy-start.306 = (f32[768]{0:T(1024)}, f32[768]{0:T(1024)S(1)}, u32[]{:S(2)}) copy-start(f32[768]{0:T(1024)S(1)} %add_rsqrt_fusion.3) | copy-start | bytes 9220
  10.9 33.6 %copy-start.288 = (f32[2048]{0:T(1024)}, f32[2048]{0:T(1024)S(1)}, u32[]{:S(2)}) copy-start(f32[2048]{0:T(1024)S(1)} %convert_element_type.266) | copy-start | bytes 24580
  10.9 21.6 %copy-start.347 = (s32[768]{0:T(1024)S(1)}, s32[768]{0:T(1024)}, u32[]{:S(2)}) copy-start(s32[768]{0:T(1024)} %param.19) | copy-start | bytes 9220
  27.0 31.9 %collective-permute-start.1 = (bf16[3,4,512]{2,0,1:T(4,128)(2,1)}, bf16[3,4,512]{2,0,1:T(4,128)(2,1)}, u32[]{:S(2)}, u32[]{:S(2)}) collective-permute-start(bf16[3,4,512]{2,0,1:T(4,128)(2,1)} %slice.644), channel_id=1, source_target_pairs={{0,4},{4,8},{8,12},{12,16},{16,20},{20,24},{24,28},{1,5},{5,9},{9,... | collective-permute-start | bytes 36872 | tf_op jit(solution)/shard_map/ppermute | solution.py:24
  33.1 19.4 %collective-permute-start = (bf16[3]{0:T(256)(128)(2,1)}, bf16[3]{0:T(256)(128)(2,1)}, u32[]{:S(2)}, u32[]{:S(2)}) collective-permute-start(bf16[3]{0:T(256)(128)(2,1)} %slice.505), channel_id=1, source_target_pairs={{0,4},{4,8},{8,12},{12,16},{16,20},{20,24},{24,28},{1,5},{5,9},{9,... | collective-permute-start | bytes 26 | tf_op jit(solution)/shard_map/ppermute | solution.py:24
  39.6 39.5 %copy-start.239 = (f32[64,64]{1,0:T(8,128)}, f32[64,64]{1,0:T(8,128)S(1)}, u32[]{:S(2)}) copy-start(f32[64,64]{1,0:T(8,128)S(1)} %fusion.394) | copy-start | bytes 49156
  47.9 24.8 %copy-start.203 = (f32[12,4,64]{2,1,0:T(4,128)}, f32[12,4,64]{2,1,0:T(4,128)S(1)}, u32[]{:S(2)}) copy-start(f32[12,4,64]{2,1,0:T(4,128)S(1)} %copy.191) | copy-start | bytes 36868
  50.8 46.7 %copy-start.237 = (f32[12,4,64]{2,1,0:T(4,128)}, f32[12,4,64]{2,1,0:T(4,128)S(1)}, u32[]{:S(2)}) copy-start(f32[12,4,64]{2,1,0:T(4,128)S(1)} %copy.194) | copy-start | bytes 36868
  52.4 24.8 %copy-start.259 = (f32[64,64]{1,0:T(8,128)}, f32[64,64]{1,0:T(8,128)S(1)}, u32[]{:S(2)}) copy-start(f32[64,64]{1,0:T(8,128)S(1)} %get-tuple-element.359) | copy-start | bytes 49156
  52.5 26.6 %copy-start.241 = (f32[64,64]{1,0:T(8,128)}, f32[64,64]{1,0:T(8,128)S(1)}, u32[]{:S(2)}) copy-start(f32[64,64]{1,0:T(8,128)S(1)} %get-tuple-element.360) | copy-start | bytes 49156
  52.5 28.6 %copy-start.251 = (f32[64,64]{1,0:T(8,128)}, f32[64,64]{1,0:T(8,128)S(1)}, u32[]{:S(2)}) copy-start(f32[64,64]{1,0:T(8,128)S(1)} %get-tuple-element.358) | copy-start | bytes 49156
  52.5 32.3 %copy-start.249 = (f32[64,64]{1,0:T(8,128)}, f32[64,64]{1,0:T(8,128)S(1)}, u32[]{:S(2)}) copy-start(f32[64,64]{1,0:T(8,128)S(1)} %get-tuple-element.357) | copy-start | bytes 49156
  52.5 36.0 %copy-start.247 = (f32[64,64]{1,0:T(8,128)}, f32[64,64]{1,0:T(8,128)S(1)}, u32[]{:S(2)}) copy-start(f32[64,64]{1,0:T(8,128)S(1)} %get-tuple-element.356) | copy-start | bytes 49156
  52.5 39.9 %copy-start.245 = (f32[64,64]{1,0:T(8,128)}, f32[64,64]{1,0:T(8,128)S(1)}, u32[]{:S(2)}) copy-start(f32[64,64]{1,0:T(8,128)S(1)} %get-tuple-element.355) | copy-start | bytes 49156
  58.0 14.7 %copy-start.201 = (pred[12,64,64]{2,1,0:T(8,128)(4,1)}, pred[12,64,64]{2,1,0:T(8,128)(4,1)S(1)}, u32[]{:S(2)}) copy-start(pred[12,64,64]{2,1,0:T(8,128)(4,1)S(1)} %get-tuple-element.342) | copy-start | bytes 147460
  58.8 37.3 %copy-start.256 = (f32[12,4,64]{2,1,0:T(4,128)}, f32[12,4,64]{2,1,0:T(4,128)S(1)}, u32[]{:S(2)}) copy-start(f32[12,4,64]{2,1,0:T(4,128)S(1)} %copy.197) | copy-start | bytes 36868
  58.8 41.0 %copy-start.264 = (f32[12,4,64]{2,1,0:T(4,128)}, f32[12,4,64]{2,1,0:T(4,128)S(1)}, u32[]{:S(2)}) copy-start(f32[12,4,64]{2,1,0:T(4,128)S(1)} %copy.198) | copy-start | bytes 36868
  72.0 27.9 %copy-start.7 = (bf16[768,4,128]{2,0,1:T(8,128)(2,1)}, bf16[768,4,128]{2,0,1:T(8,128)(2,1)S(1)}, u32[]{:S(2)}) copy-start(bf16[768,4,128]{2,0,1:T(8,128)(2,1)S(1)} %get-tuple-element.314) | copy-start | bytes 2359300
  72.6 38.1 %copy-start.93 = (f32[12,64,4,128]{3,1,2,0:T(8,128)}, f32[12,64,4,128]{3,1,2,0:T(8,128)S(1)}, u32[]{:S(2)}) copy-start(f32[12,64,4,128]{3,1,2,0:T(8,128)S(1)} %copy.451) | copy-start | bytes 4718596
  77.2 15.2 %copy-start.2 = (f32[12,4,64,64]{3,2,1,0:T(8,128)}, f32[12,4,64,64]{3,2,1,0:T(8,128)S(1)}, u32[]{:S(2)}) copy-start(f32[12,4,64,64]{3,2,1,0:T(8,128)S(1)} %get-tuple-element.318) | copy-start | bytes 2359300
  100.8 11.1 copy-start.74
  240.5 191.2 %all-gather.5.cloned.1.call-start = ((), (), s32[]{:S(2)}) async-start(), calls=%async_computation.12 | async-start | bytes 1179648 | tf_op jit(solution)/shard_map/all_gather | solution.py:125
  242.0 265.2 %copy-start.284 = (f32[2048]{0:T(1024)}, f32[2048]{0:T(1024)S(1)}, u32[]{:S(2)}) copy-start(f32[2048]{0:T(1024)S(1)} %convert_element_type.295) | copy-start | bytes 24580
  243.7 221.1 %all-reduce.32.cloned.1.call-start = ((), (), s32[]{:S(2)}) async-start(), calls=%async_computation.5 | async-start | bytes 6291456 | tf_op jit(solution)/shard_map/psum | solution.py:408
  349.2 18.8 %slice-start.16 = ((s8[5767168]{0:T(1024)(128)(4,1)}), s8[4194304]{0:T(1024)(128)(4,1)S(1)}, s32[]{:S(2)}) async-start(s8[5767168]{0:T(1024)(128)(4,1)} %bitcast.1274), calls=%async_computation.30 | async-start | bytes 8388608
  352.3 154.8 %copy-start.308 = (f32[768]{0:T(1024)}, f32[768]{0:T(1024)S(1)}, u32[]{:S(2)}) copy-start(f32[768]{0:T(1024)S(1)} %add_rsqrt_fusion.2) | copy-start | bytes 9220
  352.3 15.6 %copy-start.230 = (bf16[768,2048]{1,0:T(8,128)(2,1)S(1)}, bf16[768,2048]{1,0:T(8,128)(2,1)}, u32[]{:S(2)}) copy-start(bf16[768,2048]{1,0:T(8,128)(2,1)} %param.31) | copy-start | bytes 9437188
  352.3 15.6 %slice-start.17 = ((s8[5767168]{0:T(1024)(128)(4,1)}), s8[1572864]{0:T(1024)(128)(4,1)S(1)}, s32[]{:S(2)}) async-start(s8[5767168]{0:T(1024)(128)(4,1)} %bitcast.1274), calls=%async_computation.31 | async-start | bytes 3145728
  396.1 146.5 %all-gather.7.cloned.1.call-start = ((), (), s32[]{:S(2)}) async-start(), calls=%async_computation.13 | async-start | bytes 2359296 | tf_op jit(solution)/shard_map/all_gather | solution.py:125
  473.1 34.0 %copy-start.344 = (f32[768]{0:T(1024)}, f32[768]{0:T(1024)S(1)}, u32[]{:S(2)}) copy-start(f32[768]{0:T(1024)S(1)} %broadcast_multiply_fusion.3) | copy-start | bytes 9220
  493.1 380.7 %all-reduce.34.cloned.1.call-start = ((), (), s32[]{:S(2)}) async-start(), calls=%async_computation.6 | async-start | bytes 6291456 | tf_op jit(solution)/shard_map/psum | solution.py:441
  558.0 315.9 %reduce-scatter.5.cloned.1.call-start = ((), (), s32[]{:S(2)}) async-start(), calls=%async_computation.7 | async-start | bytes 4718592 | tf_op jit(solution)/shard_map/reduce_scatter | solution.py:443
  571.7 20.5 %slice-start.2 = ((s8[4718592]{0:T(1024)(128)(4,1)}), s8[524288]{0:T(1024)(128)(4,1)S(1)}, s32[]{:S(2)}) async-start(s8[4718592]{0:T(1024)(128)(4,1)} %bitcast.1117), calls=%async_computation.16 | async-start | bytes 1048576
  574.2 299.6 %reduce-scatter.9.cloned.1.call-start = ((), (), s32[]{:S(2)}) async-start(), calls=%async_computation.9 | async-start | bytes 6488064 | tf_op jit(solution)/shard_map/reduce_scatter | solution.py:443
  577.2 15.1 %slice-start.3 = ((s8[4718592]{0:T(1024)(128)(4,1)}), s8[4194304]{0:T(1024)(128)(4,1)S(1)}, s32[]{:S(2)}) async-start(s8[4718592]{0:T(1024)(128)(4,1)} %bitcast.1117), calls=%async_computation.17 | async-start | bytes 8388608
  642.2 329.0 %reduce-scatter.7.cloned.1.call-start = ((), (), s32[]{:S(2)}) async-start(), calls=%async_computation.8 | async-start | bytes 12976128 | tf_op jit(solution)/shard_map/reduce_scatter | solution.py:443
  671.9 12.2 copy-start.380
  671.9 12.9 %copy-start.349 = (f32[1,4]{0,1:T(4,128)S(1)}, f32[1,4]{0,1:T(4,128)}, u32[]{:S(2)}) copy-start(f32[1,4]{0,1:T(4,128)} %copy.268) | copy-start | bytes 52
  708.4 348.3 %all-reduce.36.cloned.1.call-start = ((), (), s32[]{:S(2)}) async-start(), calls=%async_computation.10 | async-start | bytes 6291456 | tf_op jit(solution)/shard_map/psum | solution.py:466
  855.0 12.5 collective-permute-start.2
  971.2 18.0 %copy-start.289 = (f32[2048]{0:T(1024)S(1)}, f32[2048]{0:T(1024)}, u32[]{:S(2)}) copy-start(f32[2048]{0:T(1024)} %copy-done.288) | copy-start | bytes 24580
  971.2 18.0 %copy-start.307 = (f32[768]{0:T(1024)S(1)}, f32[768]{0:T(1024)}, u32[]{:S(2)}) copy-start(f32[768]{0:T(1024)} %copy-done.306) | copy-start | bytes 9220
  988.9 247.6 %reduce-scatter.11.cloned.1.call-start = ((), (), s32[]{:S(2)}) async-start(), calls=%async_computation.11 | async-start | bytes 14155776 | tf_op jit(solution)/shard_map/reduce_scatter | solution.py:502
  1108.9 15.0 %copy-start.285 = (f32[2048]{0:T(1024)S(1)}, f32[2048]{0:T(1024)}, u32[]{:S(2)}) copy-start(f32[2048]{0:T(1024)} %copy-done.284) | copy-start | bytes 24580
  1108.9 15.0 %copy-start.309 = (f32[768]{0:T(1024)S(1)}, f32[768]{0:T(1024)}, u32[]{:S(2)}) copy-start(f32[768]{0:T(1024)} %copy-done.308) | copy-start | bytes 9220
  1108.9 15.0 %copy-start.345 = (f32[768]{0:T(1024)S(1)}, f32[768]{0:T(1024)}, u32[]{:S(2)}) copy-start(f32[768]{0:T(1024)} %copy-done.344) | copy-start | bytes 9220
  (369 other events, 1229.7 us)
Sparse Core Ops, SparseCore 0:
  240.6 108.4 all-reduce.29
  396.2 68.5 all-reduce.31
  558.1 66.9 all-reduce.33
  989.0 67.5 all-reduce.35
Sparse Core Ops, SparseCore 1:
  243.8 80.4 all-gather.4
  493.2 49.3 all-gather.6
  574.3 86.7 reduce-scatter.4
  665.2 110.2 reduce-scatter.8
  779.4 191.7 reduce-scatter.6
  1006.1 230.4 reduce-scatter.10

commit v5 on v4

--- a/solution.py
+++ b/solution.py
@@ -221,8 +221,8 @@
             inverse = inverse - jnp.einsum(
                 "...ij,...jk->...ik",
                 inverse,
-                jnp.einsum("...ij,...jk->...ik", off, inverse, precision=EXACT_ARITHMETIC),
-                precision=EXACT_ARITHMETIC,
+                jnp.einsum("...ij,...jk->...ik", off, inverse, precision=FAST_ARITHMETIC),
+                precision=FAST_ARITHMETIC,
             )
         width *= 2
     return inverse
@@ -257,7 +257,9 @@
     to_end = jnp.exp(decay_sum[..., -1:] - decay_sum) * (pieces == pieces[:, -1:])[
         :, None, :
     ].astype(jnp.float32)
-    key_dots = jnp.einsum("nhtk,nhjk->nhtj", keys_b, keys_b, precision=FAST_ARITHMETIC)
+    key_dots = jnp.einsum(
+        "nhtk,nhjk->nhtj", keys_b, keys_b, preferred_element_type=jnp.float32
+    )
     lower_mat = (
         jnp.eye(GROUP, dtype=jnp.float32) + key_dots * decays * before * strength_b[..., :, None]
     )

time: 1260 us -> 1250 us (level)
  matrix products: 494 us -> 459 us
  waiting for transfers between devices: 395 us -> 422 us
    reduce_scatter x3, waiting for transfers between devices: 97.3 us -> 124 us  [shards(): lax.psum_scatter(part, 'seq', scatter_dimension=0, tiled=True)]
    dot_general x18, matrix products: 54.5 us -> 36.4 us  [the longest x15 27.9 us: unit_lower_inverse(): jnp.einsum('...ij,...jk->...ik', off, inverse, precision=FAST_ARITHMETIC)]
    dot_general x15, matrix products: 38.1 us -> 20.6 us  [unit_lower_inverse(): jnp.einsum('...ij,...jk->...ik', inverse, jnp.einsum('...ij,...jk->...ik'...]
  transfers between devices with their start and end apart: 13 -> 13, of which waited for: 6 -> 6; matrix products, arithmetic and copies ran while one was open for 40% -> 38% of each run, Pallas kernels for 3% -> 3%
where the time goes in v5:
time: 1250 us; the launch traced here: 1240 us
  matrix products  459 us (37%)
  waiting for transfers between devices  422 us (34%)
  local copies, waits for them, and re-layouts  126 us (10%)
  other arithmetic  107 us (9%)
  Pallas kernels  94.6 us (8%)
  between operations  20.2 us (2%)
    reduce_scatter x3, waiting for transfers between devices, shards(): lax.psum_scatter(part, 'seq', scatter_dimension=0, tiled=True)  124 us
    psum x1, waiting for transfers between devices, shards(): lax.psum(mixer_part.astype(jnp.bfloat16), 'tp').astype(jnp.float32)  105 us
    reduce_scatter x1, waiting for transfers between devices, shards(): lax.psum_scatter(grad_mix.astype(jnp.bfloat16), 'seq', scatter_dimension=...  102 us
    pallas_call x3, Pallas kernels, peer_gather(): pl.pallas_call(functools.partial(peer_gather_kernel, axis, count, mode),...  94.6 us
    dot_general x35, matrix products, advance(): jnp.einsum('htk,hkw->htw', query_rows, carried_state, precision=FAST_ARIT...  60.8 us
    unnamed x826, local copies, waits for them, and re-layouts  54.4 us
    dot_general x36, matrix products, advance(): jnp.einsum('hjk,hjw->hkw', end_rows, new_values, precision=FAST_ARITHMETIC)  49.4 us
    dot_general x35, matrix products, advance(): jnp.einsum('htk,hkw->htw', state_rows, carried_state, precision=FAST_ARIT...  47.2 us
  transfers between devices with their start and end apart: 13, of which 6 were waited for; matrix products, arithmetic and copies ran while one was open for 38% of the time, Pallas kernels for 3%

profile of v5, /device:TPU:0, one launch (start us, length us, event | category | flops | bytes accessed | tf_op | source)
XLA Modules:
  0.0 1241.3 jit_solution(4939614325115379157)
XLA Ops:
  10.9 15.5 %fusion.444 = (bf16[768,4,768]{2,0,1:T(8,128)(2,1)S(1)}, f32[768,4,768]{2,0,1:T(8,128)}) fusion(bf16[2048,4,768]{2,1,0:T(4,128)(2,1)} %param.21, bf16[768,2048]{1,0:T(8,128)(2,1)S(1)} %copy-done.5, f32[2048]{0:T(1024)S(1)} %convert_element_type.266, f32[768]{0:T(1024)S(1)} %add_rsqrt_fusion.3), kind=kOutput, calls=%fused_computation.856 | convolution fusion | flops 9672327168 | bytes 29895680 | tf_op jit(solution)/shard_map/td,dhc->thc/dot_general | solution.py:343
  27.0 5.5 collective-permute-start.1
  33.1 3.9 collective-permute-start
  61.8 6.4 fusion.36
  149.6 53.5 %shard_map.237 = bf16[8,4,128,384]{3,2,1,0:T(8,128)(2,1)} custom-call(bf16[4,128,384]{2,1,0:T(8,128)(2,1)} %pad_maximum_fusion.1.x_ref), custom_call_target="tpu_custom_call" | custom-call | tf_op jit(solution)/shard_map/pallas_call | solution.py:82
  218.3 4.3 multiply_reduce_fusion.8
  228.1 5.0 bitcast_convert_fusion.1
  236.4 105.4 %all-reduce.30.cloned.1.call-done = bf16[768,2048]{1,0:T(8,128)(2,1)} async-done(((bf16[768,2048]{1,0:T(8,128)(2,1)}), bf16[768,2048]{1,0:T(8,128)(2,1)}) %all-reduce.30.cloned.1.call-update) | async-done | bytes 3145744 | tf_op jit(solution)/shard_map/psum | solution.py:395
  345.0 15.8 %fusion.17 = f32[768,2,1408]{2,0,1:T(8,128)} fusion(bf16[2048,2,1408]{2,1,0:T(2,128)(2,1)} %param.29, bf16[768,2048]{1,0:T(8,128)(2,1)S(1)} %copy-done.64, bf16[768,2048]{1,0:T(8,128)(2,1)S(1)} %copy-done.5, f32[2048]{0:T(1024)S(1)} %convert_element_type.295, f32[768]{0:T(1024)S(1)} %add_rsqrt_fusion.2), kind=kOutput, calls=%fused_computation.20 | convolution fusion | flops 8867807232 | bytes 26487808 | tf_op jit(solution)/shard_map/td,dcf->tcf/dot_general | solution.py:399
  360.8 11.0 multiply_bitcast_fusion
  371.8 17.0 %bitcast_convert_fusion = (bf16[768,2048]{1,0:T(8,128)(2,1)}, f32[768,2048,1]{1,0,2:T(8,128)}) fusion(bf16[2048,2,1408]{2,1,0:T(2,128)(2,1)} %param.29, f32[768,1,1408]{2,0,1:T(8,128)} %get-tuple-element.303, f32[768,1,1408]{2,0,1:T(8,128)} %get-tuple-element.302), kind=kOutput, calls=%fused_computation.50 | convolution fusion | flops 8864268288 | bytes 29622272 | tf_op jit(solution)/shard_map/tcf,dcf->td/dot_general | solution.py:409
  388.8 16.7 %convolution_convert_fusion = bf16[2048,2,1408]{2,0,1:T(8,128)(2,1)} fusion(f32[768,1,1408]{2,0,1:T(8,128)} %get-tuple-element.303, f32[768,1,1408]{2,0,1:T(8,128)} %get-tuple-element.302, bf16[768,2048]{1,0:T(8,128)(2,1)} %all-reduce.30.cloned.1.call-done, bf16[768,2048]{1,0:T(8,128)(2,1)S(1)} %copy-done.5, f32[2048]{0:T(1024)S(1)} %convert_element_type.295, ...), kind=kOutput, calls=%fused_computation.17 | convolution fusion | flops 8877899776 | bytes 26487808 | tf_op jit(solution)/shard_map/td,tcf->dcf/dot_general | solution.py:406
  405.5 9.7 fusion.23
  415.3 9.0 convolution_convert_fusion.4
  427.0 30.5 %all-reduce.32.cloned.1.call-done = bf16[768,2048]{1,0:T(8,128)(2,1)} async-done(((bf16[768,2048]{1,0:T(8,128)(2,1)}), bf16[768,2048]{1,0:T(8,128)(2,1)}) %all-reduce.32.cloned.1.call-update) | async-done | bytes 3145744 | tf_op jit(solution)/shard_map/psum | solution.py:410
  457.5 6.9 fusion.35
  465.8 11.4 multiply_reduce_fusion.6
  477.2 4.0 add_add_fusion
  481.1 4.6 fusion.125
  500.0 6.8 convolution_convert_fusion.3
  506.8 28.5 %all-gather.7.cloned.1.call-done = bf16[32,128,256]{2,1,0:T(8,128)(2,1)} async-done(((bf16[4,128,256]{2,1,0:T(8,128)(2,1)}), bf16[32,128,256]{2,1,0:T(8,128)(2,1)}) %all-gather.7.cloned.1.call-update) | async-done | bytes 2097168 | tf_op jit(solution)/shard_map/all_gather | solution.py:125
  535.3 4.1 rev.7
  539.4 11.2 while.27
  599.8 5.2 fusion.211
  717.0 5.3 fusion.72
  735.7 5.6 fusion.83
  772.9 7.4 multiply_select_fusion
  782.3 4.4 fusion.38
  789.6 3.5 fusion.215
  793.2 4.5 add_bitcast_fusion.1
  805.8 7.9 multiply_reduce_fusion.3
  813.8 6.4 multiply_multiply_fusion.2
  822.5 3.7 fusion.397
  826.2 7.0 pad_add_fusion
  833.2 3.9 fusion.34
  839.6 124.5 %reduce-scatter.7.cloned.1.call-done = bf16[256,2,1408]{2,0,1:T(8,128)(2,1)} async-done(((bf16[2048,2,1408]{2,0,1:T(8,128)(2,1)}), bf16[256,2,1408]{2,0,1:T(8,128)(2,1)}) %reduce-scatter.7.cloned.1.call-update) | async-done | bytes 1441808 | tf_op jit(solution)/shard_map/reduce_scatter | solution.py:445
  964.0 17.6 %fusion.445 = (bf16[768,2048]{1,0:T(8,128)(2,1)}, f32[768,2048]{1,0:T(8,128)}) fusion(f32[768,2048,1]{1,0,2:T(8,128)} %fusion.397, bf16[768,4,768]{2,0,1:T(8,128)(2,1)} %pad_maximum_fusion, bf16[2048,4,768]{2,1,0:T(4,128)(2,1)} %param.21), kind=kOutput, calls=%fused_computation.857 | convolution fusion | flops 9666822144 | bytes 33030144 | tf_op jit(solution)/shard_map/thc,dhc->td/dot_general | solution.py:465
  983.6 15.3 %convolution_convert_fusion.2 = bf16[2048,4,768]{2,0,1:T(8,128)(2,1)} fusion(bf16[768,4,768]{2,0,1:T(8,128)(2,1)} %pad_maximum_fusion, bf16[768,2048]{1,0:T(8,128)(2,1)S(1)} %copy-done.6, f32[2048]{0:T(1024)S(1)} %copy-done.289, f32[768]{0:T(1024)S(1)} %copy-done.307), kind=kOutput, calls=%fused_computation.32 | convolution fusion | flops 9676259328 | bytes 20458496 | tf_op jit(solution)/shard_map/td,thc->dhc/dot_general | solution.py:461
  1003.0 5.5 reshape.1435
  1008.7 4.4 copy.284
  1018.1 31.3 %all-reduce.36.cloned.1.call-done = bf16[768,2048]{1,0:T(8,128)(2,1)} async-done(((bf16[768,2048]{1,0:T(8,128)(2,1)}), bf16[768,2048]{1,0:T(8,128)(2,1)}) %all-reduce.36.cloned.1.call-update) | async-done | bytes 3145744 | tf_op jit(solution)/shard_map/psum | solution.py:468
  1049.4 5.0 fusion.30
  1055.2 36.1 %shard_map.238 = f32[8,232,128]{2,1,0:T(8,128)} custom-call(f32[232,128]{1,0:T(8,128)} %pad_bitcast_fusion.x_ref), custom_call_target="tpu_custom_call" | custom-call | tf_op jit(solution)/shard_map/pallas_call | solution.py:82
  1093.1 6.7 reshape.1438
  1104.2 5.0 shard_map.239
  1116.7 11.1 fusion.29
  1127.8 101.8 %reduce-scatter.11.cloned.1.call-done = bf16[256,4,768]{2,0,1:T(8,128)(2,1)} async-done(((bf16[2048,4,768]{2,0,1:T(8,128)(2,1)}), bf16[256,4,768]{2,0,1:T(8,128)(2,1)}) %reduce-scatter.11.cloned.1.call-update) | async-done | bytes 1572880 | tf_op jit(solution)/shard_map/reduce_scatter | solution.py:504
  1229.6 4.3 copy.281
  (1195 shorter events, 412.0 us)
Async XLA Ops:
  8.0 36.5 %copy-start = (bf16[2048,4,2]{0,2,1:T(2,128)(2,1)S(1)}, bf16[2048,4,2]{0,2,1:T(2,128)(2,1)}, u32[]{:S(2)}) copy-start(bf16[2048,4,2]{0,2,1:T(2,128)(2,1)} %param.22) | copy-start | bytes 98308
  8.0 333.7 %all-reduce.30.cloned.1.call-start = ((), (), s32[]{:S(2)}) async-start(), calls=%async_computation.4 | async-start | bytes 6291456 | tf_op jit(solution)/shard_map/psum | solution.py:395
  10.8 33.7 %copy-start.306 = (f32[768]{0:T(1024)}, f32[768]{0:T(1024)S(1)}, u32[]{:S(2)}) copy-start(f32[768]{0:T(1024)S(1)} %add_rsqrt_fusion.3) | copy-start | bytes 9220
  10.9 33.6 %copy-start.288 = (f32[2048]{0:T(1024)}, f32[2048]{0:T(1024)S(1)}, u32[]{:S(2)}) copy-start(f32[2048]{0:T(1024)S(1)} %convert_element_type.266) | copy-start | bytes 24580
  10.9 21.6 %copy-start.347 = (s32[768]{0:T(1024)S(1)}, s32[768]{0:T(1024)}, u32[]{:S(2)}) copy-start(s32[768]{0:T(1024)} %param.19) | copy-start | bytes 9220
  27.0 31.9 %collective-permute-start.1 = (bf16[3,4,512]{2,0,1:T(4,128)(2,1)}, bf16[3,4,512]{2,0,1:T(4,128)(2,1)}, u32[]{:S(2)}, u32[]{:S(2)}) collective-permute-start(bf16[3,4,512]{2,0,1:T(4,128)(2,1)} %slice.644), channel_id=1, source_target_pairs={{0,4},{4,8},{8,12},{12,16},{16,20},{20,24},{24,28},{1,5},{5,9},{9,... | collective-permute-start | bytes 36872 | tf_op jit(solution)/shard_map/ppermute | solution.py:24
  33.1 19.4 %collective-permute-start = (bf16[3]{0:T(256)(128)(2,1)}, bf16[3]{0:T(256)(128)(2,1)}, u32[]{:S(2)}, u32[]{:S(2)}) collective-permute-start(bf16[3]{0:T(256)(128)(2,1)} %slice.505), channel_id=1, source_target_pairs={{0,4},{4,8},{8,12},{12,16},{16,20},{20,24},{24,28},{1,5},{5,9},{9,... | collective-permute-start | bytes 26 | tf_op jit(solution)/shard_map/ppermute | solution.py:24
  39.6 38.7 %copy-start.239 = (f32[64,64]{1,0:T(8,128)}, f32[64,64]{1,0:T(8,128)S(1)}, u32[]{:S(2)}) copy-start(f32[64,64]{1,0:T(8,128)S(1)} %fusion.394) | copy-start | bytes 49156
  47.9 24.8 %copy-start.203 = (f32[12,4,64]{2,1,0:T(4,128)}, f32[12,4,64]{2,1,0:T(4,128)S(1)}, u32[]{:S(2)}) copy-start(f32[12,4,64]{2,1,0:T(4,128)S(1)} %copy.191) | copy-start | bytes 36868
  50.8 39.3 %copy-start.237 = (f32[12,4,64]{2,1,0:T(4,128)}, f32[12,4,64]{2,1,0:T(4,128)S(1)}, u32[]{:S(2)}) copy-start(f32[12,4,64]{2,1,0:T(4,128)S(1)} %copy.194) | copy-start | bytes 36868
  52.4 24.8 %copy-start.259 = (f32[64,64]{1,0:T(8,128)}, f32[64,64]{1,0:T(8,128)S(1)}, u32[]{:S(2)}) copy-start(f32[64,64]{1,0:T(8,128)S(1)} %get-tuple-element.359) | copy-start | bytes 49156
  52.5 25.8 %copy-start.241 = (f32[64,64]{1,0:T(8,128)}, f32[64,64]{1,0:T(8,128)S(1)}, u32[]{:S(2)}) copy-start(f32[64,64]{1,0:T(8,128)S(1)} %get-tuple-element.360) | copy-start | bytes 49156
  52.5 26.9 %copy-start.251 = (f32[64,64]{1,0:T(8,128)}, f32[64,64]{1,0:T(8,128)S(1)}, u32[]{:S(2)}) copy-start(f32[64,64]{1,0:T(8,128)S(1)} %get-tuple-element.358) | copy-start | bytes 49156
  52.5 29.3 %copy-start.249 = (f32[64,64]{1,0:T(8,128)}, f32[64,64]{1,0:T(8,128)S(1)}, u32[]{:S(2)}) copy-start(f32[64,64]{1,0:T(8,128)S(1)} %get-tuple-element.357) | copy-start | bytes 49156
  52.5 31.6 %copy-start.247 = (f32[64,64]{1,0:T(8,128)}, f32[64,64]{1,0:T(8,128)S(1)}, u32[]{:S(2)}) copy-start(f32[64,64]{1,0:T(8,128)S(1)} %get-tuple-element.356) | copy-start | bytes 49156
  52.5 33.9 %copy-start.245 = (f32[64,64]{1,0:T(8,128)}, f32[64,64]{1,0:T(8,128)S(1)}, u32[]{:S(2)}) copy-start(f32[64,64]{1,0:T(8,128)S(1)} %get-tuple-element.355) | copy-start | bytes 49156
  58.0 14.7 %copy-start.201 = (pred[12,64,64]{2,1,0:T(8,128)(4,1)}, pred[12,64,64]{2,1,0:T(8,128)(4,1)S(1)}, u32[]{:S(2)}) copy-start(pred[12,64,64]{2,1,0:T(8,128)(4,1)S(1)} %get-tuple-element.342) | copy-start | bytes 147460
  58.8 29.8 %copy-start.256 = (f32[12,4,64]{2,1,0:T(4,128)}, f32[12,4,64]{2,1,0:T(4,128)S(1)}, u32[]{:S(2)}) copy-start(f32[12,4,64]{2,1,0:T(4,128)S(1)} %copy.197) | copy-start | bytes 36868
  58.8 34.0 %copy-start.264 = (f32[12,4,64]{2,1,0:T(4,128)}, f32[12,4,64]{2,1,0:T(4,128)S(1)}, u32[]{:S(2)}) copy-start(f32[12,4,64]{2,1,0:T(4,128)S(1)} %copy.198) | copy-start | bytes 36868
  72.0 20.9 %copy-start.7 = (bf16[768,4,128]{2,0,1:T(8,128)(2,1)}, bf16[768,4,128]{2,0,1:T(8,128)(2,1)S(1)}, u32[]{:S(2)}) copy-start(bf16[768,4,128]{2,0,1:T(8,128)(2,1)S(1)} %get-tuple-element.314) | copy-start | bytes 2359300
  72.6 30.7 %copy-start.93 = (f32[12,64,4,128]{3,1,2,0:T(8,128)}, f32[12,64,4,128]{3,1,2,0:T(8,128)S(1)}, u32[]{:S(2)}) copy-start(f32[12,64,4,128]{3,1,2,0:T(8,128)S(1)} %copy.451) | copy-start | bytes 4718596
  93.8 10.7 copy-start.74
  233.2 191.1 %all-gather.5.cloned.1.call-start = ((), (), s32[]{:S(2)}) async-start(), calls=%async_computation.12 | async-start | bytes 1179648 | tf_op jit(solution)/shard_map/all_gather | solution.py:125
  234.6 265.4 %copy-start.284 = (f32[2048]{0:T(1024)}, f32[2048]{0:T(1024)S(1)}, u32[]{:S(2)}) copy-start(f32[2048]{0:T(1024)S(1)} %convert_element_type.295) | copy-start | bytes 24580
  236.3 221.2 %all-reduce.32.cloned.1.call-start = ((), (), s32[]{:S(2)}) async-start(), calls=%async_computation.5 | async-start | bytes 6291456 | tf_op jit(solution)/shard_map/psum | solution.py:410
  341.8 19.0 %slice-start.16 = ((s8[5767168]{0:T(1024)(128)(4,1)}), s8[4194304]{0:T(1024)(128)(4,1)S(1)}, s32[]{:S(2)}) async-start(s8[5767168]{0:T(1024)(128)(4,1)} %bitcast.1274), calls=%async_computation.30 | async-start | bytes 8388608
  344.9 155.0 %copy-start.308 = (f32[768]{0:T(1024)}, f32[768]{0:T(1024)S(1)}, u32[]{:S(2)}) copy-start(f32[768]{0:T(1024)S(1)} %add_rsqrt_fusion.2) | copy-start | bytes 9220
  345.0 15.8 %copy-start.230 = (bf16[768,2048]{1,0:T(8,128)(2,1)S(1)}, bf16[768,2048]{1,0:T(8,128)(2,1)}, u32[]{:S(2)}) copy-start(bf16[768,2048]{1,0:T(8,128)(2,1)} %param.31) | copy-start | bytes 9437188
  345.0 15.8 %slice-start.17 = ((s8[5767168]{0:T(1024)(128)(4,1)}), s8[1572864]{0:T(1024)(128)(4,1)S(1)}, s32[]{:S(2)}) async-start(s8[5767168]{0:T(1024)(128)(4,1)} %bitcast.1274), calls=%async_computation.31 | async-start | bytes 3145728
  388.8 146.5 %all-gather.7.cloned.1.call-start = ((), (), s32[]{:S(2)}) async-start(), calls=%async_computation.13 | async-start | bytes 2359296 | tf_op jit(solution)/shard_map/all_gather | solution.py:125
  465.8 34.2 %copy-start.344 = (f32[768]{0:T(1024)}, f32[768]{0:T(1024)S(1)}, u32[]{:S(2)}) copy-start(f32[768]{0:T(1024)S(1)} %broadcast_multiply_fusion.3) | copy-start | bytes 9220
  485.8 353.8 %all-reduce.34.cloned.1.call-start = ((), (), s32[]{:S(2)}) async-start(), calls=%async_computation.6 | async-start | bytes 6291456 | tf_op jit(solution)/shard_map/psum | solution.py:443
  550.7 288.9 %reduce-scatter.5.cloned.1.call-start = ((), (), s32[]{:S(2)}) async-start(), calls=%async_computation.7 | async-start | bytes 4718592 | tf_op jit(solution)/shard_map/reduce_scatter | solution.py:445
  564.5 20.6 %slice-start.2 = ((s8[4718592]{0:T(1024)(128)(4,1)}), s8[524288]{0:T(1024)(128)(4,1)S(1)}, s32[]{:S(2)}) async-start(s8[4718592]{0:T(1024)(128)(4,1)} %bitcast.1117), calls=%async_computation.16 | async-start | bytes 1048576
  566.9 272.6 %reduce-scatter.9.cloned.1.call-start = ((), (), s32[]{:S(2)}) async-start(), calls=%async_computation.9 | async-start | bytes 6488064 | tf_op jit(solution)/shard_map/reduce_scatter | solution.py:445
  570.0 15.1 %slice-start.3 = ((s8[4718592]{0:T(1024)(128)(4,1)}), s8[4194304]{0:T(1024)(128)(4,1)S(1)}, s32[]{:S(2)}) async-start(s8[4718592]{0:T(1024)(128)(4,1)} %bitcast.1117), calls=%async_computation.17 | async-start | bytes 8388608
  595.9 11.0 slice-start.4
  635.2 328.8 %reduce-scatter.7.cloned.1.call-start = ((), (), s32[]{:S(2)}) async-start(), calls=%async_computation.8 | async-start | bytes 12976128 | tf_op jit(solution)/shard_map/reduce_scatter | solution.py:445
  664.9 12.2 copy-start.380
  664.9 12.9 %copy-start.349 = (f32[1,4]{0,1:T(4,128)S(1)}, f32[1,4]{0,1:T(4,128)}, u32[]{:S(2)}) copy-start(f32[1,4]{0,1:T(4,128)} %copy.268) | copy-start | bytes 52
  701.4 348.1 %all-reduce.36.cloned.1.call-start = ((), (), s32[]{:S(2)}) async-start(), calls=%async_computation.10 | async-start | bytes 6291456 | tf_op jit(solution)/shard_map/psum | solution.py:468
  821.0 12.2 collective-permute-start.2
  964.0 17.7 %copy-start.289 = (f32[2048]{0:T(1024)S(1)}, f32[2048]{0:T(1024)}, u32[]{:S(2)}) copy-start(f32[2048]{0:T(1024)} %copy-done.288) | copy-start | bytes 24580
  964.0 17.7 %copy-start.307 = (f32[768]{0:T(1024)S(1)}, f32[768]{0:T(1024)}, u32[]{:S(2)}) copy-start(f32[768]{0:T(1024)} %copy-done.306) | copy-start | bytes 9220
  981.7 247.9 %reduce-scatter.11.cloned.1.call-start = ((), (), s32[]{:S(2)}) async-start(), calls=%async_computation.11 | async-start | bytes 14155776 | tf_op jit(solution)/shard_map/reduce_scatter | solution.py:504
  1101.7 15.0 %copy-start.285 = (f32[2048]{0:T(1024)S(1)}, f32[2048]{0:T(1024)}, u32[]{:S(2)}) copy-start(f32[2048]{0:T(1024)} %copy-done.284) | copy-start | bytes 24580
  1101.7 15.0 %copy-start.309 = (f32[768]{0:T(1024)S(1)}, f32[768]{0:T(1024)}, u32[]{:S(2)}) copy-start(f32[768]{0:T(1024)} %copy-done.308) | copy-start | bytes 9220
  1101.7 15.0 %copy-start.345 = (f32[768]{0:T(1024)S(1)}, f32[768]{0:T(1024)}, u32[]{:S(2)}) copy-start(f32[768]{0:T(1024)} %copy-done.344) | copy-start | bytes 9220
  (369 other events, 1184.3 us)
Sparse Core Ops, SparseCore 0:
  233.3 108.4 all-reduce.29
  388.9 68.5 all-reduce.31
  550.8 66.9 all-reduce.33
  981.8 67.5 all-reduce.35
Sparse Core Ops, SparseCore 1:
  236.4 80.4 all-gather.4
  485.9 49.4 all-gather.6
  567.0 86.8 reduce-scatter.4
  657.9 110.2 reduce-scatter.8
  772.3 191.7 reduce-scatter.6
  999.0 230.5 reduce-scatter.10

commit v6 on v5

--- a/solution.py
+++ b/solution.py
@@ -271,7 +271,11 @@
 
     value_part = solved(strength_b[..., None] * stacked_b)
     state_part = solved((strength_b * from_start)[..., None] * keys_b)
-    query_keys = jnp.einsum("nhtk,nhjk->nhtj", query_b, keys_b, precision=FAST_ARITHMETIC) * decays
+    query_keys = (
+        jnp.einsum("nhtk,nhjk->nhtj", blocked(query), keys_b, preferred_element_type=jnp.float32)
+        * key_size ** (-0.5)
+        * decays
+    )
     end_keys = to_end[..., None] * keys_b
     initial = jnp.concatenate(
         [

time: 1250 us -> 1250 us (level)
  waiting for transfers between devices: 422 us -> 438 us
  local copies, waits for them, and re-layouts: 126 us -> 111 us
    reduce_scatter x3, waiting for transfers between devices: 124 us -> 140 us  [shards(): lax.psum_scatter(part, 'seq', scatter_dimension=0, tiled=True)]
    unnamed x826 -> x836, local copies, waits for them, and re-layouts: 54.4 us -> 53.3 us
  transfers between devices with their start and end apart: 13 -> 13, of which waited for: 6 -> 6; matrix products, arithmetic and copies ran while one was open for 38% -> 37% of each run, Pallas kernels for 3% -> 3%
where the time goes in v6:
time: 1250 us; the launch traced here: 1240 us
  matrix products  458 us (37%)
  waiting for transfers between devices  438 us (35%)
  local copies, waits for them, and re-layouts  111 us (9%)
  other arithmetic  105 us (8%)
  Pallas kernels  94.6 us (8%)
  between operations  20.4 us (2%)
    reduce_scatter x3, waiting for transfers between devices, shards(): lax.psum_scatter(part, 'seq', scatter_dimension=0, tiled=True)  140 us
    psum x1, waiting for transfers between devices, shards(): lax.psum(mixer_part.astype(jnp.bfloat16), 'tp').astype(jnp.float32)  106 us
    reduce_scatter x1, waiting for transfers between devices, shards(): lax.psum_scatter(grad_mix.astype(jnp.bfloat16), 'seq', scatter_dimension=...  102 us
    pallas_call x3, Pallas kernels, peer_gather(): pl.pallas_call(functools.partial(peer_gather_kernel, axis, count, mode),...  94.6 us
    dot_general x35, matrix products, advance(): jnp.einsum('htk,hkw->htw', query_rows, carried_state, precision=FAST_ARIT...  60.8 us
    unnamed x836, local copies, waits for them, and re-layouts  53.3 us
    dot_general x36, matrix products, advance(): jnp.einsum('hjk,hjw->hkw', end_rows, new_values, precision=FAST_ARITHMETIC)  49.4 us
    dot_general x35, matrix products, advance(): jnp.einsum('htk,hkw->htw', state_rows, carried_state, precision=FAST_ARIT...  44.5 us
  transfers between devices with their start and end apart: 13, of which 6 were waited for; matrix products, arithmetic and copies ran while one was open for 37% of the time, Pallas kernels for 3%

profile of v6, /device:TPU:0, one launch (start us, length us, event | category | flops | bytes accessed | tf_op | source)
XLA Modules:
  0.0 1238.9 jit_solution(9121273696155101816)
XLA Ops:
  10.9 15.5 %fusion.447 = (bf16[768,4,768]{2,0,1:T(8,128)(2,1)S(1)}, f32[768,4,768]{2,0,1:T(8,128)}) fusion(bf16[2048,4,768]{2,1,0:T(4,128)(2,1)} %param.21, bf16[768,2048]{1,0:T(8,128)(2,1)S(1)} %copy-done.5, f32[2048]{0:T(1024)S(1)} %convert_element_type.266, f32[768]{0:T(1024)S(1)} %add_rsqrt_fusion.3), kind=kOutput, calls=%fused_computation.862 | convolution fusion | flops 9672327168 | bytes 29895680 | tf_op jit(solution)/shard_map/td,dhc->thc/dot_general | solution.py:347
  27.0 5.5 collective-permute-start.1
  33.0 3.7 collective-permute-start
  60.8 6.3 fusion.36
  147.2 53.5 %shard_map.237 = bf16[8,4,128,384]{3,2,1,0:T(8,128)(2,1)} custom-call(bf16[4,128,384]{2,1,0:T(8,128)(2,1)} %pad_maximum_fusion.1.x_ref), custom_call_target="tpu_custom_call" | custom-call | tf_op jit(solution)/shard_map/pallas_call | solution.py:82
  216.0 4.3 multiply_reduce_fusion.8
  225.8 5.0 bitcast_convert_fusion.1
  234.0 105.5 %all-reduce.30.cloned.1.call-done = bf16[768,2048]{1,0:T(8,128)(2,1)} async-done(((bf16[768,2048]{1,0:T(8,128)(2,1)}), bf16[768,2048]{1,0:T(8,128)(2,1)}) %all-reduce.30.cloned.1.call-update) | async-done | bytes 3145744 | tf_op jit(solution)/shard_map/psum | solution.py:399
  342.8 15.6 %fusion.17 = f32[768,2,1408]{2,0,1:T(8,128)} fusion(bf16[2048,2,1408]{2,1,0:T(2,128)(2,1)} %param.29, bf16[768,2048]{1,0:T(8,128)(2,1)S(1)} %copy-done.65, bf16[768,2048]{1,0:T(8,128)(2,1)S(1)} %copy-done.5, f32[2048]{0:T(1024)S(1)} %convert_element_type.295, f32[768]{0:T(1024)S(1)} %add_rsqrt_fusion.2), kind=kOutput, calls=%fused_computation.20 | convolution fusion | flops 8867807232 | bytes 26487808 | tf_op jit(solution)/shard_map/td,dcf->tcf/dot_general | solution.py:403
  358.3 11.0 multiply_bitcast_fusion
  369.4 17.0 %bitcast_convert_fusion = (bf16[768,2048]{1,0:T(8,128)(2,1)}, f32[768,2048,1]{1,0,2:T(8,128)}) fusion(bf16[2048,2,1408]{2,1,0:T(2,128)(2,1)} %param.29, f32[768,1,1408]{2,0,1:T(8,128)} %get-tuple-element.305, f32[768,1,1408]{2,0,1:T(8,128)} %get-tuple-element.304), kind=kOutput, calls=%fused_computation.50 | convolution fusion | flops 8864268288 | bytes 29622272 | tf_op jit(solution)/shard_map/tcf,dcf->td/dot_general | solution.py:413
  386.4 16.7 %convolution_convert_fusion = bf16[2048,2,1408]{2,0,1:T(8,128)(2,1)} fusion(f32[768,1,1408]{2,0,1:T(8,128)} %get-tuple-element.305, f32[768,1,1408]{2,0,1:T(8,128)} %get-tuple-element.304, bf16[768,2048]{1,0:T(8,128)(2,1)} %all-reduce.30.cloned.1.call-done, bf16[768,2048]{1,0:T(8,128)(2,1)S(1)} %copy-done.5, f32[2048]{0:T(1024)S(1)} %convert_element_type.295, ...), kind=kOutput, calls=%fused_computation.17 | convolution fusion | flops 8877899776 | bytes 26487808 | tf_op jit(solution)/shard_map/td,tcf->dcf/dot_general | solution.py:410
  403.1 9.7 fusion.23
  412.9 9.0 convolution_convert_fusion.4
  424.6 30.4 %all-reduce.32.cloned.1.call-done = bf16[768,2048]{1,0:T(8,128)(2,1)} async-done(((bf16[768,2048]{1,0:T(8,128)(2,1)}), bf16[768,2048]{1,0:T(8,128)(2,1)}) %all-reduce.32.cloned.1.call-update) | async-done | bytes 3145744 | tf_op jit(solution)/shard_map/psum | solution.py:414
  455.1 7.1 fusion.35
  463.4 11.4 multiply_reduce_fusion.6
  474.8 4.0 add_add_fusion
  478.7 4.6 fusion.123
  497.4 6.7 convolution_convert_fusion.3
  504.1 28.7 %all-gather.7.cloned.1.call-done = bf16[32,128,256]{2,1,0:T(8,128)(2,1)} async-done(((bf16[4,128,256]{2,1,0:T(8,128)(2,1)}), bf16[32,128,256]{2,1,0:T(8,128)(2,1)}) %all-gather.7.cloned.1.call-update) | async-done | bytes 2097168 | tf_op jit(solution)/shard_map/all_gather | solution.py:125
  532.8 4.1 rev.7
  536.9 11.2 while.27
  595.1 4.0 fusion.209
  696.9 5.4 fusion.72
  715.6 5.3 fusion.81
  754.2 7.6 multiply_select_fusion
  763.8 4.4 fusion.38
  771.0 3.5 fusion.211
  774.6 5.4 add_bitcast_fusion.1
  788.0 7.9 multiply_reduce_fusion.3
  795.9 6.2 multiply_multiply_fusion.2
  804.6 3.7 fusion.398
  808.3 6.8 pad_add_fusion
  815.1 4.1 fusion.34
  821.7 139.8 %reduce-scatter.7.cloned.1.call-done = bf16[256,2,1408]{2,0,1:T(8,128)(2,1)} async-done(((bf16[2048,2,1408]{2,0,1:T(8,128)(2,1)}), bf16[256,2,1408]{2,0,1:T(8,128)(2,1)}) %reduce-scatter.7.cloned.1.call-update) | async-done | bytes 1441808 | tf_op jit(solution)/shard_map/reduce_scatter | solution.py:449
  961.5 17.6 %fusion.448 = (bf16[768,2048]{1,0:T(8,128)(2,1)}, f32[768,2048]{1,0:T(8,128)}) fusion(f32[768,2048,1]{1,0,2:T(8,128)} %fusion.398, bf16[768,4,768]{2,0,1:T(8,128)(2,1)} %pad_maximum_fusion, bf16[2048,4,768]{2,1,0:T(4,128)(2,1)} %param.21), kind=kOutput, calls=%fused_computation.863 | convolution fusion | flops 9666822144 | bytes 33030144 | tf_op jit(solution)/shard_map/thc,dhc->td/dot_general | solution.py:469
  981.0 15.4 %convolution_convert_fusion.2 = bf16[2048,4,768]{2,0,1:T(8,128)(2,1)} fusion(bf16[768,4,768]{2,0,1:T(8,128)(2,1)} %pad_maximum_fusion, bf16[768,2048]{1,0:T(8,128)(2,1)S(1)} %copy-done.6, f32[2048]{0:T(1024)S(1)} %copy-done.293, f32[768]{0:T(1024)S(1)} %copy-done.311), kind=kOutput, calls=%fused_computation.32 | convolution fusion | flops 9676259328 | bytes 20458496 | tf_op jit(solution)/shard_map/td,thc->dhc/dot_general | solution.py:465
  1000.5 5.5 reshape.1440
  1006.2 4.4 copy.287
  1015.6 31.3 %all-reduce.36.cloned.1.call-done = bf16[768,2048]{1,0:T(8,128)(2,1)} async-done(((bf16[768,2048]{1,0:T(8,128)(2,1)}), bf16[768,2048]{1,0:T(8,128)(2,1)}) %all-reduce.36.cloned.1.call-update) | async-done | bytes 3145744 | tf_op jit(solution)/shard_map/psum | solution.py:472
  1046.9 5.0 fusion.30
  1052.6 36.1 %shard_map.238 = f32[8,232,128]{2,1,0:T(8,128)} custom-call(f32[232,128]{1,0:T(8,128)} %pad_bitcast_fusion.x_ref), custom_call_target="tpu_custom_call" | custom-call | tf_op jit(solution)/shard_map/pallas_call | solution.py:82
  1090.6 6.7 reshape.1443
  1101.6 5.0 shard_map.239
  1114.2 11.1 fusion.29
  1125.3 101.8 %reduce-scatter.11.cloned.1.call-done = bf16[256,4,768]{2,0,1:T(8,128)(2,1)} async-done(((bf16[2048,4,768]{2,0,1:T(8,128)(2,1)}), bf16[256,4,768]{2,0,1:T(8,128)(2,1)}) %reduce-scatter.11.cloned.1.call-update) | async-done | bytes 1572880 | tf_op jit(solution)/shard_map/reduce_scatter | solution.py:508
  1227.2 4.3 copy.284
  (1205 shorter events, 394.5 us)
Async XLA Ops:
  8.0 36.3 %copy-start = (bf16[2048,4,2]{0,2,1:T(2,128)(2,1)S(1)}, bf16[2048,4,2]{0,2,1:T(2,128)(2,1)}, u32[]{:S(2)}) copy-start(bf16[2048,4,2]{0,2,1:T(2,128)(2,1)} %param.22) | copy-start | bytes 98308
  8.0 331.5 %all-reduce.30.cloned.1.call-start = ((), (), s32[]{:S(2)}) async-start(), calls=%async_computation.4 | async-start | bytes 6291456 | tf_op jit(solution)/shard_map/psum | solution.py:399
  10.8 33.5 %copy-start.310 = (f32[768]{0:T(1024)}, f32[768]{0:T(1024)S(1)}, u32[]{:S(2)}) copy-start(f32[768]{0:T(1024)S(1)} %add_rsqrt_fusion.3) | copy-start | bytes 9220
  10.9 33.4 %copy-start.292 = (f32[2048]{0:T(1024)}, f32[2048]{0:T(1024)S(1)}, u32[]{:S(2)}) copy-start(f32[2048]{0:T(1024)S(1)} %convert_element_type.266) | copy-start | bytes 24580
  10.9 21.6 %copy-start.351 = (s32[768]{0:T(1024)S(1)}, s32[768]{0:T(1024)}, u32[]{:S(2)}) copy-start(s32[768]{0:T(1024)} %param.19) | copy-start | bytes 9220
  27.0 30.9 %collective-permute-start.1 = (bf16[3,4,512]{2,0,1:T(4,128)(2,1)}, bf16[3,4,512]{2,0,1:T(4,128)(2,1)}, u32[]{:S(2)}, u32[]{:S(2)}) collective-permute-start(bf16[3,4,512]{2,0,1:T(4,128)(2,1)} %slice.644), channel_id=1, source_target_pairs={{0,4},{4,8},{8,12},{12,16},{16,20},{20,24},{24,28},{1,5},{5,9},{9,... | collective-permute-start | bytes 36872 | tf_op jit(solution)/shard_map/ppermute | solution.py:24
  33.0 19.3 %collective-permute-start = (bf16[3]{0:T(256)(128)(2,1)}, bf16[3]{0:T(256)(128)(2,1)}, u32[]{:S(2)}, u32[]{:S(2)}) collective-permute-start(bf16[3]{0:T(256)(128)(2,1)} %slice.505), channel_id=1, source_target_pairs={{0,4},{4,8},{8,12},{12,16},{16,20},{20,24},{24,28},{1,5},{5,9},{9,... | collective-permute-start | bytes 26 | tf_op jit(solution)/shard_map/ppermute | solution.py:24
  39.3 36.5 %copy-start.241 = (f32[64,64]{1,0:T(8,128)}, f32[64,64]{1,0:T(8,128)S(1)}, u32[]{:S(2)}) copy-start(f32[64,64]{1,0:T(8,128)S(1)} %fusion.395) | copy-start | bytes 49156
  47.7 23.8 %copy-start.205 = (f32[12,4,64]{2,1,0:T(4,128)}, f32[12,4,64]{2,1,0:T(4,128)S(1)}, u32[]{:S(2)}) copy-start(f32[12,4,64]{2,1,0:T(4,128)S(1)} %copy.194) | copy-start | bytes 36868
  50.6 37.1 %copy-start.239 = (f32[12,4,64]{2,1,0:T(4,128)}, f32[12,4,64]{2,1,0:T(4,128)S(1)}, u32[]{:S(2)}) copy-start(f32[12,4,64]{2,1,0:T(4,128)S(1)} %copy.197) | copy-start | bytes 36868
  52.3 22.5 %copy-start.261 = (f32[64,64]{1,0:T(8,128)}, f32[64,64]{1,0:T(8,128)S(1)}, u32[]{:S(2)}) copy-start(f32[64,64]{1,0:T(8,128)S(1)} %get-tuple-element.358) | copy-start | bytes 49156
  52.3 23.5 %copy-start.243 = (f32[64,64]{1,0:T(8,128)}, f32[64,64]{1,0:T(8,128)S(1)}, u32[]{:S(2)}) copy-start(f32[64,64]{1,0:T(8,128)S(1)} %get-tuple-element.359) | copy-start | bytes 49156
  52.3 24.7 %copy-start.253 = (f32[64,64]{1,0:T(8,128)}, f32[64,64]{1,0:T(8,128)S(1)}, u32[]{:S(2)}) copy-start(f32[64,64]{1,0:T(8,128)S(1)} %get-tuple-element.357) | copy-start | bytes 49156
  52.3 27.1 %copy-start.251 = (f32[64,64]{1,0:T(8,128)}, f32[64,64]{1,0:T(8,128)S(1)}, u32[]{:S(2)}) copy-start(f32[64,64]{1,0:T(8,128)S(1)} %get-tuple-element.356) | copy-start | bytes 49156
  52.3 29.4 %copy-start.249 = (f32[64,64]{1,0:T(8,128)}, f32[64,64]{1,0:T(8,128)S(1)}, u32[]{:S(2)}) copy-start(f32[64,64]{1,0:T(8,128)S(1)} %get-tuple-element.355) | copy-start | bytes 49156
  52.3 31.7 %copy-start.247 = (f32[64,64]{1,0:T(8,128)}, f32[64,64]{1,0:T(8,128)S(1)}, u32[]{:S(2)}) copy-start(f32[64,64]{1,0:T(8,128)S(1)} %get-tuple-element.354) | copy-start | bytes 49156
  56.9 14.6 %copy-start.70 = (f32[12,64,64]{2,1,0:T(8,128)}, f32[12,64,64]{2,1,0:T(8,128)S(1)}, u32[]{:S(2)}) copy-start(f32[12,64,64]{2,1,0:T(8,128)S(1)} %get-tuple-element.344) | copy-start | bytes 589828
  56.9 14.6 %copy-start.120 = (f32[12,64,64]{2,1,0:T(8,128)}, f32[12,64,64]{2,1,0:T(8,128)S(1)}, u32[]{:S(2)}) copy-start(f32[12,64,64]{2,1,0:T(8,128)S(1)} %get-tuple-element.347) | copy-start | bytes 589828
  56.9 14.6 %copy-start.203 = (pred[12,64,64]{2,1,0:T(8,128)(4,1)}, pred[12,64,64]{2,1,0:T(8,128)(4,1)S(1)}, u32[]{:S(2)}) copy-start(pred[12,64,64]{2,1,0:T(8,128)(4,1)S(1)} %get-tuple-element.343) | copy-start | bytes 147460
  57.8 28.4 %copy-start.258 = (f32[12,4,64]{2,1,0:T(4,128)}, f32[12,4,64]{2,1,0:T(4,128)S(1)}, u32[]{:S(2)}) copy-start(f32[12,4,64]{2,1,0:T(4,128)S(1)} %copy.200) | copy-start | bytes 36868
  57.8 32.4 %copy-start.266 = (f32[12,4,64]{2,1,0:T(4,128)}, f32[12,4,64]{2,1,0:T(4,128)S(1)}, u32[]{:S(2)}) copy-start(f32[12,4,64]{2,1,0:T(4,128)S(1)} %copy.201) | copy-start | bytes 36868
  70.9 19.3 %copy-start.7 = (bf16[768,4,128]{2,0,1:T(8,128)(2,1)}, bf16[768,4,128]{2,0,1:T(8,128)(2,1)S(1)}, u32[]{:S(2)}) copy-start(bf16[768,4,128]{2,0,1:T(8,128)(2,1)S(1)} %get-tuple-element.315) | copy-start | bytes 2359300
  91.2 10.7 copy-start.78
  91.2 9.6 copy-start.95
  230.8 191.0 %all-gather.5.cloned.1.call-start = ((), (), s32[]{:S(2)}) async-start(), calls=%async_computation.12 | async-start | bytes 1179648 | tf_op jit(solution)/shard_map/all_gather | solution.py:125
  232.3 265.1 %copy-start.288 = (f32[2048]{0:T(1024)}, f32[2048]{0:T(1024)S(1)}, u32[]{:S(2)}) copy-start(f32[2048]{0:T(1024)S(1)} %convert_element_type.295) | copy-start | bytes 24580
  234.0 221.1 %all-reduce.32.cloned.1.call-start = ((), (), s32[]{:S(2)}) async-start(), calls=%async_computation.5 | async-start | bytes 6291456 | tf_op jit(solution)/shard_map/psum | solution.py:414
  339.6 18.7 %slice-start.16 = ((s8[5767168]{0:T(1024)(128)(4,1)}), s8[4194304]{0:T(1024)(128)(4,1)S(1)}, s32[]{:S(2)}) async-start(s8[5767168]{0:T(1024)(128)(4,1)} %bitcast.1276), calls=%async_computation.30 | async-start | bytes 8388608
  342.7 154.6 %copy-start.312 = (f32[768]{0:T(1024)}, f32[768]{0:T(1024)S(1)}, u32[]{:S(2)}) copy-start(f32[768]{0:T(1024)S(1)} %add_rsqrt_fusion.2) | copy-start | bytes 9220
  342.7 15.6 %copy-start.232 = (bf16[768,2048]{1,0:T(8,128)(2,1)S(1)}, bf16[768,2048]{1,0:T(8,128)(2,1)}, u32[]{:S(2)}) copy-start(bf16[768,2048]{1,0:T(8,128)(2,1)} %param.31) | copy-start | bytes 9437188
  342.7 15.6 %slice-start.17 = ((s8[5767168]{0:T(1024)(128)(4,1)}), s8[1572864]{0:T(1024)(128)(4,1)S(1)}, s32[]{:S(2)}) async-start(s8[5767168]{0:T(1024)(128)(4,1)} %bitcast.1276), calls=%async_computation.31 | async-start | bytes 3145728
  386.4 146.5 %all-gather.7.cloned.1.call-start = ((), (), s32[]{:S(2)}) async-start(), calls=%async_computation.13 | async-start | bytes 2359296 | tf_op jit(solution)/shard_map/all_gather | solution.py:125
  463.4 34.0 %copy-start.348 = (f32[768]{0:T(1024)}, f32[768]{0:T(1024)S(1)}, u32[]{:S(2)}) copy-start(f32[768]{0:T(1024)S(1)} %broadcast_multiply_fusion.2) | copy-start | bytes 9220
  483.4 338.3 %all-reduce.34.cloned.1.call-start = ((), (), s32[]{:S(2)}) async-start(), calls=%async_computation.6 | async-start | bytes 6291456 | tf_op jit(solution)/shard_map/psum | solution.py:447
  548.2 273.5 %reduce-scatter.5.cloned.1.call-start = ((), (), s32[]{:S(2)}) async-start(), calls=%async_computation.7 | async-start | bytes 4718592 | tf_op jit(solution)/shard_map/reduce_scatter | solution.py:449
  562.0 20.5 %slice-start.2 = ((s8[4718592]{0:T(1024)(128)(4,1)}), s8[524288]{0:T(1024)(128)(4,1)S(1)}, s32[]{:S(2)}) async-start(s8[4718592]{0:T(1024)(128)(4,1)} %bitcast.1120), calls=%async_computation.16 | async-start | bytes 1048576
  564.4 10.3 copy-start.329
  564.4 257.3 %reduce-scatter.9.cloned.1.call-start = ((), (), s32[]{:S(2)}) async-start(), calls=%async_computation.9 | async-start | bytes 6488064 | tf_op jit(solution)/shard_map/reduce_scatter | solution.py:449
  567.5 15.1 %slice-start.3 = ((s8[4718592]{0:T(1024)(128)(4,1)}), s8[4194304]{0:T(1024)(128)(4,1)S(1)}, s32[]{:S(2)}) async-start(s8[4718592]{0:T(1024)(128)(4,1)} %bitcast.1120), calls=%async_computation.17 | async-start | bytes 8388608
  628.5 333.0 %reduce-scatter.7.cloned.1.call-start = ((), (), s32[]{:S(2)}) async-start(), calls=%async_computation.8 | async-start | bytes 12976128 | tf_op jit(solution)/shard_map/reduce_scatter | solution.py:449
  680.9 365.9 %all-reduce.36.cloned.1.call-start = ((), (), s32[]{:S(2)}) async-start(), calls=%async_computation.10 | async-start | bytes 6291456 | tf_op jit(solution)/shard_map/psum | solution.py:472
  803.1 12.0 collective-permute-start.2
  961.5 17.7 %copy-start.293 = (f32[2048]{0:T(1024)S(1)}, f32[2048]{0:T(1024)}, u32[]{:S(2)}) copy-start(f32[2048]{0:T(1024)} %copy-done.292) | copy-start | bytes 24580
  961.5 17.7 %copy-start.311 = (f32[768]{0:T(1024)S(1)}, f32[768]{0:T(1024)}, u32[]{:S(2)}) copy-start(f32[768]{0:T(1024)} %copy-done.310) | copy-start | bytes 9220
  979.2 248.0 %reduce-scatter.11.cloned.1.call-start = ((), (), s32[]{:S(2)}) async-start(), calls=%async_computation.11 | async-start | bytes 14155776 | tf_op jit(solution)/shard_map/reduce_scatter | solution.py:508
  1099.2 15.0 %copy-start.289 = (f32[2048]{0:T(1024)S(1)}, f32[2048]{0:T(1024)}, u32[]{:S(2)}) copy-start(f32[2048]{0:T(1024)} %copy-done.288) | copy-start | bytes 24580
  1099.2 15.0 %copy-start.313 = (f32[768]{0:T(1024)S(1)}, f32[768]{0:T(1024)}, u32[]{:S(2)}) copy-start(f32[768]{0:T(1024)} %copy-done.312) | copy-start | bytes 9220
  1099.2 15.0 %copy-start.349 = (f32[768]{0:T(1024)S(1)}, f32[768]{0:T(1024)}, u32[]{:S(2)}) copy-start(f32[768]{0:T(1024)} %copy-done.348) | copy-start | bytes 9220
  (374 other events, 1202.0 us)
Sparse Core Ops, SparseCore 0:
  231.0 108.5 all-reduce.29
  386.5 68.5 all-reduce.31
  548.3 66.9 all-reduce.33
  979.3 67.5 all-reduce.35
Sparse Core Ops, SparseCore 1:
  234.1 80.5 all-gather.4
  483.5 49.3 all-gather.6
  564.5 86.7 reduce-scatter.4
  655.4 110.2 reduce-scatter.8
  769.7 191.7 reduce-scatter.6
  996.5 230.6 reduce-scatter.10
